TPU v7x, 32 devices: a whole 2x2x4 slice. The times are simulated.
32 devices in a mesh: curve: 8 (over z, y), band: 4 (over x, core).
Axes of the slice: x: 2, y: 2, z: 4, core: 2. Of those that a mesh axis runs over, the one named last changes fastest.
Arguments:
- state: float32 [16, 2048, 128], P('band', 'curve'), may hold values from -3 to 3
- blocks: bfloat16 [2048, 4, 128, 128], P('curve', 'band'), may hold values from -0.25 to 0.25
- diag_blocks: bfloat16 [2048, 128, 128], P(('curve', 'band')), may hold values from -1 to 1, as said below
- block_cols: int32 [2048, 4], P('curve', 'band'), may hold values from 0 to 2047, as said below
Outputs:
- updated: float32 [16, 2048, 128], P('band', 'curve')
Inputs may be any that keep to these rules, and one draw needn't show every extreme that they name: `diag_blocks`: every diagonal block is symmetric. `block_cols`: A column is never the row's own patch, and no pair of patches is stored twice, in either order. The owner of patch p is index p // 256 of curve. Of the 256 rows of one index of curve, in each slot exactly 8 have their column on another index: 2 on each of 4 other indices; the columns of the others lie on the own index.
All inputs are finite; a program needn't handle non-finite values.
Results may differ from a plain program's by a relative error of at most 0.0003.
The roundings to bfloat16 on the way count: a program that leaves them out, or rounds other values in their place, can miss the bound.
Values may be sent and summed in bfloat16 or wider, within the bound.
No kernel may reach another device: no remote copies, remote signals or barrier semaphores. Data moves between devices by JAX's collectives and lax.ppermute only.
A program may use at most 64 MiB of HBM per device.

v0:
```python
import jax
import jax.numpy as jnp
from jax import lax
from jax.sharding import PartitionSpec as P

CAP = 2
TAYLOR = 16


epsilon = 1e-06
time_step = 0.5
quadratic = 1.0


def nonlinear(field):
    return quadratic * field * field - field * field * field


def phi_weights(alpha_first, beta_first, alpha_second):

    def advance(turn, carry):
        term_one, term_two, total_one, total_two = carry
        factor = time_step / (turn + 1.0)
        next_one = factor * (alpha_first * term_one + beta_first * term_two)
        next_two = factor * (beta_first * term_one + alpha_second * term_two)
        return (next_one, next_two, total_one + next_one, total_two + next_two)

    ones = jnp.ones_like(alpha_first)
    zeros = jnp.zeros_like(alpha_first)
    result = lax.fori_loop(1, TAYLOR, advance, (ones, zeros, ones, zeros))
    return (result[2], result[3])


def routing(block_cols):
    groups = lax.axis_size("curve")
    here = lax.axis_index("curve")
    patch_rows = block_cols.shape[0]
    columns = block_cols[:, 0]
    owner = columns // patch_rows
    target = columns % patch_rows
    remote = owner != here
    peers = jnp.arange(groups, dtype=jnp.int32)
    member = ((owner[:, None] == peers[None, :]) & remote[:, None]).astype(jnp.int32)
    rank = jnp.sum(jnp.cumsum(member, axis=0) * member, axis=1) - 1
    bucket = jnp.where(remote, owner * CAP + rank, groups * CAP)
    pick = jnp.where(remote, patch_rows + owner * CAP + rank, target)
    wanted = jnp.full((groups * CAP + 1,), -1, jnp.int32).at[bucket].set(target)
    asked = lax.all_to_all(
        wanted[:-1].reshape(groups, CAP), "curve", split_axis=0, concat_axis=0, tiled=True
    )
    asked_flat = asked.reshape(-1)
    return (remote, target, bucket, pick, jnp.maximum(asked_flat, 0), asked_flat >= 0)


def local_product(whole, blocks, diag_blocks, plan):
    remote, target, bucket, pick, asked_index, asked_valid = plan
    groups = lax.axis_size("curve")
    vectors, patch_rows, node_count = whole.shape
    reply = whole[:, asked_index, :].reshape(vectors, groups, CAP, node_count)
    arrived = lax.all_to_all(reply, "curve", split_axis=1, concat_axis=1, tiled=True)
    pool = jnp.concatenate([whole, arrived.reshape(vectors, groups * CAP, node_count)], axis=1)
    gathered = pool[:, pick, :]
    stored = blocks[:, 0]
    result = jnp.einsum("rac,vrc->vra", stored, gathered, preferred_element_type=jnp.float32)
    mirrored = jnp.einsum("rac,vra->vrc", stored, whole, preferred_element_type=jnp.float32)
    kept = jnp.where(remote[None, :, None], 0.0, mirrored)
    result = result.at[:, target, :].add(kept)
    outgoing = (
        jnp.zeros((vectors, groups * CAP + 1, node_count), jnp.float32)
        .at[:, bucket, :]
        .add(mirrored)
    )
    outgoing = outgoing[:, :-1, :].reshape(vectors, groups, CAP, node_count)
    returned = lax.all_to_all(outgoing, "curve", split_axis=1, concat_axis=1, tiled=True)
    returned = jnp.where(
        asked_valid[None, :, None], returned.reshape(vectors, groups * CAP, node_count), 0.0
    )
    result = result.at[:, asked_index, :].add(returned)
    quarter = diag_blocks.shape[0]
    start = lax.axis_index("band") * quarter
    own_rows = lax.dynamic_slice_in_dim(whole, start, quarter, 1)
    diagonal = jnp.einsum("rac,vrc->vra", diag_blocks, own_rows, preferred_element_type=jnp.float32)
    current = lax.dynamic_slice_in_dim(result, start, quarter, 1)
    return lax.dynamic_update_slice_in_dim(result, current + diagonal, start, 1)


def operate(vector, blocks, diag_blocks, plan):
    whole = lax.all_gather(vector, "band", axis=0, tiled=True)
    product = lax.psum_scatter(
        local_product(whole, blocks, diag_blocks, plan), "band", scatter_dimension=0, tiled=True
    )
    return product


def body(state, blocks, diag_blocks, block_cols):
    plan = routing(block_cols)
    drive = operate(state.astype(jnp.bfloat16), blocks, diag_blocks, plan) + nonlinear(state)
    drive_norm = lax.psum(jnp.sum(drive * drive, axis=(1, 2)), "curve")
    beta_zero = jnp.sqrt(drive_norm + epsilon)
    first = drive / beta_zero[:, None, None]
    image = operate(first.astype(jnp.bfloat16), blocks, diag_blocks, plan)
    alpha_first, energy = lax.psum(
        (jnp.sum(first * image, axis=(1, 2)), jnp.sum(image * image, axis=(1, 2))), "curve"
    )
    rest = image - alpha_first[:, None, None] * first
    beta_first = jnp.sqrt(jnp.maximum(energy - alpha_first * alpha_first, 0.0) + epsilon)
    second = rest / beta_first[:, None, None]
    image_second = operate(second.astype(jnp.bfloat16), blocks, diag_blocks, plan)
    image_second = image_second - beta_first[:, None, None] * first
    alpha_second = lax.psum(jnp.sum(second * image_second, axis=(1, 2)), "curve")
    weight_one, weight_two = phi_weights(alpha_first, beta_first, alpha_second)
    combined = weight_one[:, None, None] * first + weight_two[:, None, None] * second
    updated = state + time_step * beta_zero[:, None, None] * combined
    return updated


def solution(mesh):
    return jax.shard_map(
        body,
        mesh=mesh,
        in_specs=(
            P("band", "curve", None),
            P("curve", "band", None, None),
            P(("curve", "band"), None, None),
            P("curve", "band"),
        ),
        out_specs=P("band", "curve", None),
        check_vma=False,
    )
```

profile of v0, /device:TPU:0, one launch (start us, length us, event | category | flops | bytes accessed | tf_op | source)
XLA Modules:
  0.0 534.2 jit_solution(13686195170682434651)
XLA Ops:
  13.6 7.3 %all-to-all-start = ((s32[8,1,2]{2,1,0:T(1,128)}), s32[8,1,2]{2,1,0:T(1,128)S(1)}, u32[]{:S(2)}, u32[]{:S(2)}) async-start(s32[8,1,2]{2,1,0:T(1,128)} %bitcast.7), calls=%async_computation | async-start | bytes 8192 | tf_op jit(solution)/shard_map/all_to_all | solution.py:48
  37.0 8.0 %broadcast_select_fusion.6 = (f32[256,16,128]{2,1,0:T(8,128)}, f32[256,16,128]{2,1,0:T(8,128)}) fusion(pred[256]{0:T(512)(128)(4,1)S(1)} %fusion.43, bf16[256,1,128,128]{3,2,1,0:T(8,128)(2,1)} %param.7, bf16[16,256,128]{2,1,0:T(8,128)(2,1)} %all-gather.4.cloned.1.call-done), kind=kOutput, calls=%fused_computation.56 | convolution fusion | flops 134742016 | bytes 13631744 | tf_op jit(solution)/shard_map/rac,vra->vrc/dot_general | solution.py:65
  45.0 20.9 %scatter_fusion.1 = f32[16,17,128]{2,0,1:T(8,128)S(1)} fusion(f32[16,17,128]{2,0,1:T(8,128)S(1)} %broadcast.192.clone, s32[256]{0:T(256)S(1)} %bitcast.116, f32[256,16,128]{2,1,0:T(8,128)} %get-tuple-element.211), kind=kCustom, calls=%fused_computation.8 | custom fusion | flops 524288 | bytes 6292480 | tf_op jit(solution)/shard_map/scatter-add | solution.py:71
  66.6 6.0 %all-to-all-start.2 = ((f32[16,8,2,128]{3,0,2,1:T(8,128)}), f32[16,8,2,128]{3,0,2,1:T(8,128)S(1)}, u32[]{:S(2)}, u32[]{:S(2)}) async-start(f32[16,8,2,128]{3,0,2,1:T(8,128)} %bitcast.16), calls=%async_computation.2 | async-start | bytes 262144 | tf_op jit(solution)/shard_map/all_to_all | solution.py:74
  76.7 9.5 %fusion.14 = f32[16,256,128]{2,0,1:T(8,128)} fusion(bf16[256,1,128,128]{3,2,1,0:T(8,128)(2,1)} %param.7, bf16[256,16,128]{2,1,0:T(8,128)(2,1)} %gather_fusion.1), kind=kOutput, calls=%fused_computation.36 | convolution fusion | flops 134217728 | bytes 11534336 | tf_op jit(solution)/shard_map/rac,vrc->vra/dot_general | solution.py:64
  86.2 31.4 %scatter_fusion = f32[16,256,128]{2,0,1:T(8,128)} fusion(f32[16,256,128]{2,0,1:T(8,128)} %fusion.14, s32[256]{0:T(256)S(1)} %bitcast.112, f32[256,16,128]{2,1,0:T(8,128)} %get-tuple-element.210), kind=kCustom, calls=%fused_computation.7 | custom fusion | flops 524288 | bytes 6292480 | tf_op jit(solution)/shard_map/scatter-add | solution.py:67
  127.0 31.5 %reduce-scatter.4.cloned.1.call-done = f32[4,256,128]{2,1,0:T(8,128)} async-done(((f32[16,256,128]{2,1,0:T(8,128)}), f32[4,256,128]{2,1,0:T(8,128)}) %reduce-scatter.4.cloned.1.call-update) | async-done | bytes 524304 | tf_op jit(solution)/shard_map/reduce_scatter | solution.py:89
  159.8 21.3 %psum.28 = f32[4]{0:T(128)S(1)} all-reduce(f32[4]{0:T(128)S(1)} %multiply_reduce_fusion.3), channel_id=1, replica_groups=mesh['curve'=8,'band'=4] {'curve'}, use_global_device_ids=true, to_apply=%region_9.10 | all-reduce | flops 4 | bytes 32 | tf_op jit(solution)/shard_map/psum | solution.py:98
  183.1 13.2 %all-gather.6.cloned.1.call-done = bf16[16,256,128]{2,1,0:T(8,128)(2,1)} async-done(((bf16[4,256,128]{2,1,0:T(8,128)(2,1)}), bf16[16,256,128]{2,1,0:T(8,128)(2,1)}) %all-gather.6.cloned.1.call-update) | async-done | bytes 1048592 | tf_op jit(solution)/shard_map/all_gather | solution.py:88
  207.1 8.0 %broadcast_select_fusion.5 = (f32[256,16,128]{2,1,0:T(8,128)}, f32[256,16,128]{2,1,0:T(8,128)}) fusion(pred[256]{0:T(512)(128)(4,1)S(1)} %fusion.43, bf16[256,1,128,128]{3,2,1,0:T(8,128)(2,1)} %param.7, bf16[16,256,128]{2,1,0:T(8,128)(2,1)} %all-gather.6.cloned.1.call-done), kind=kOutput, calls=%fused_computation.55 | convolution fusion | flops 134742016 | bytes 13631744 | tf_op jit(solution)/shard_map/rac,vra->vrc/dot_general | solution.py:65
  215.1 20.9 %scatter_fusion.4 = f32[16,17,128]{2,0,1:T(8,128)S(1)} fusion(f32[16,17,128]{2,0,1:T(8,128)S(1)} %broadcast.192.clone.1, s32[256]{0:T(256)S(1)} %bitcast.117, f32[256,16,128]{2,1,0:T(8,128)} %get-tuple-element.213), kind=kCustom, calls=%fused_computation.11 | custom fusion | flops 524288 | bytes 6292480 | tf_op jit(solution)/shard_map/scatter-add | solution.py:71
  236.7 6.0 %all-to-all-start.4 = ((f32[16,8,2,128]{3,0,2,1:T(8,128)}), f32[16,8,2,128]{3,0,2,1:T(8,128)S(1)}, u32[]{:S(2)}, u32[]{:S(2)}) async-start(f32[16,8,2,128]{3,0,2,1:T(8,128)} %bitcast.25), calls=%async_computation.5 | async-start | bytes 262144 | tf_op jit(solution)/shard_map/all_to_all | solution.py:74
  248.1 9.5 %fusion.17 = f32[16,256,128]{2,0,1:T(8,128)} fusion(bf16[256,1,128,128]{3,2,1,0:T(8,128)(2,1)} %param.7, bf16[256,16,128]{2,1,0:T(8,128)(2,1)} %gather_fusion.3), kind=kOutput, calls=%fused_computation.37 | convolution fusion | flops 134217728 | bytes 11534336 | tf_op jit(solution)/shard_map/rac,vrc->vra/dot_general | solution.py:64
  257.6 31.4 %scatter_fusion.3 = f32[16,256,128]{2,0,1:T(8,128)} fusion(f32[16,256,128]{2,0,1:T(8,128)} %fusion.17, s32[256]{0:T(256)S(1)} %bitcast.113, f32[256,16,128]{2,1,0:T(8,128)} %get-tuple-element.212), kind=kCustom, calls=%fused_computation.10 | custom fusion | flops 524288 | bytes 6292480 | tf_op jit(solution)/shard_map/scatter-add | solution.py:67
  298.4 31.5 %reduce-scatter.6.cloned.1.call-done = f32[4,256,128]{2,1,0:T(8,128)} async-done(((f32[16,256,128]{2,1,0:T(8,128)}), f32[4,256,128]{2,1,0:T(8,128)}) %reduce-scatter.6.cloned.1.call-update) | async-done | bytes 524304 | tf_op jit(solution)/shard_map/reduce_scatter | solution.py:89
  331.2 21.3 %all-reduce = (f32[4]{0:T(128)S(1)}, f32[4]{0:T(128)S(1)}) all-reduce(f32[4]{0:T(128)S(1)} %get-tuple-element.175, f32[4]{0:T(128)S(1)} %get-tuple-element.174), channel_id=1, replica_groups=mesh['curve'=8,'band'=4] {'curve'}, use_global_device_ids=true, to_apply=%region_15.16 | all-reduce | flops 8 | bytes 64 | tf_op jit(solution)/shard_map/psum | solution.py:102
  354.5 13.2 %all-gather.8.cloned.1.call-done = bf16[16,256,128]{2,1,0:T(8,128)(2,1)} async-done(((bf16[4,256,128]{2,1,0:T(8,128)(2,1)}), bf16[16,256,128]{2,1,0:T(8,128)(2,1)}) %all-gather.8.cloned.1.call-update) | async-done | bytes 1048592 | tf_op jit(solution)/shard_map/all_gather | solution.py:88
  378.5 8.0 %broadcast_select_fusion.4 = (f32[256,16,128]{2,1,0:T(8,128)}, f32[256,16,128]{2,1,0:T(8,128)}) fusion(pred[256]{0:T(512)(128)(4,1)S(1)} %fusion.43, bf16[256,1,128,128]{3,2,1,0:T(8,128)(2,1)} %param.7, bf16[16,256,128]{2,1,0:T(8,128)(2,1)} %all-gather.8.cloned.1.call-done), kind=kOutput, calls=%fused_computation.54 | convolution fusion | flops 134742016 | bytes 13631744 | tf_op jit(solution)/shard_map/rac,vra->vrc/dot_general | solution.py:65
  386.5 20.9 %scatter_fusion.7 = f32[16,17,128]{2,0,1:T(8,128)S(1)} fusion(f32[16,17,128]{2,0,1:T(8,128)S(1)} %broadcast.192, s32[256]{0:T(256)S(1)} %bitcast.118, f32[256,16,128]{2,1,0:T(8,128)} %get-tuple-element.215), kind=kCustom, calls=%fused_computation.14 | custom fusion | flops 524288 | bytes 6292480 | tf_op jit(solution)/shard_map/scatter-add | solution.py:71
  408.1 6.0 %all-to-all-start.6 = ((f32[16,8,2,128]{3,0,2,1:T(8,128)}), f32[16,8,2,128]{3,0,2,1:T(8,128)S(1)}, u32[]{:S(2)}, u32[]{:S(2)}) async-start(f32[16,8,2,128]{3,0,2,1:T(8,128)} %bitcast.34), calls=%async_computation.8 | async-start | bytes 262144 | tf_op jit(solution)/shard_map/all_to_all | solution.py:74
  419.7 9.5 %fusion.20 = f32[16,256,128]{2,0,1:T(8,128)} fusion(bf16[256,1,128,128]{3,2,1,0:T(8,128)(2,1)} %param.7, bf16[256,16,128]{2,1,0:T(8,128)(2,1)} %gather_fusion.5), kind=kOutput, calls=%fused_computation.38 | convolution fusion | flops 134217728 | bytes 11534336 | tf_op jit(solution)/shard_map/rac,vrc->vra/dot_general | solution.py:64
  429.2 31.4 %scatter_fusion.6 = f32[16,256,128]{2,0,1:T(8,128)} fusion(f32[16,256,128]{2,0,1:T(8,128)} %fusion.20, s32[256]{0:T(256)S(1)} %bitcast.114, f32[256,16,128]{2,1,0:T(8,128)} %get-tuple-element.214), kind=kCustom, calls=%fused_computation.13 | custom fusion | flops 524288 | bytes 6292480 | tf_op jit(solution)/shard_map/scatter-add | solution.py:67
  470.1 31.3 %reduce-scatter.8.cloned.1.call-done = f32[4,256,128]{2,1,0:T(8,128)} async-done(((f32[16,256,128]{2,1,0:T(8,128)}), f32[4,256,128]{2,1,0:T(8,128)}) %reduce-scatter.8.cloned.1.call-update) | async-done | bytes 524304 | tf_op jit(solution)/shard_map/reduce_scatter | solution.py:89
  502.7 21.4 %psum.31 = f32[4]{0:T(128)S(1)} all-reduce(f32[4]{0:T(128)S(1)} %multiply_reduce_fusion), channel_id=1, replica_groups=mesh['curve'=8,'band'=4] {'curve'}, use_global_device_ids=true, to_apply=%region_23.24 | all-reduce | flops 4 | bytes 32 | tf_op jit(solution)/shard_map/psum | solution.py:110
  (108 shorter events, 101.3 us)
Async XLA Ops:
  6.5 113.7 %copy-start = (bf16[64,128,128]{2,1,0:T(8,128)(2,1)S(1)}, bf16[64,128,128]{2,1,0:T(8,128)(2,1)}, u32[]{:S(2)}) copy-start(bf16[64,128,128]{2,1,0:T(8,128)(2,1)} %param.8) | copy-start | bytes 6291460
  6.5 21.8 %all-gather.4.cloned.1.call-start = ((), (), s32[]{:S(2)}) async-start(), calls=%async_computation.10 | async-start | bytes 1310720 | tf_op jit(solution)/shard_map/all_gather | solution.py:88
  13.6 13.8 %all-to-all-start = ((s32[8,1,2]{2,1,0:T(1,128)}), s32[8,1,2]{2,1,0:T(1,128)S(1)}, u32[]{:S(2)}, u32[]{:S(2)}) async-start(s32[8,1,2]{2,1,0:T(1,128)} %bitcast.7), calls=%async_computation | async-start | bytes 8192 | tf_op jit(solution)/shard_map/all_to_all | solution.py:48
  31.4 35.1 %all-to-all-start.1 = ((bf16[16,8,2,128]{3,0,2,1:T(8,128)(2,1)}), bf16[16,8,2,128]{3,0,2,1:T(8,128)(2,1)S(1)}, u32[]{:S(2)}, u32[]{:S(2)}) async-start(bf16[16,8,2,128]{3,0,2,1:T(8,128)(2,1)} %bitcast.9), calls=%async_computation.1 | async-start | bytes 131072 | tf_op jit(solution)/shard_map/all_to_all | solution.py:60
  66.6 51.1 %all-to-all-start.2 = ((f32[16,8,2,128]{3,0,2,1:T(8,128)}), f32[16,8,2,128]{3,0,2,1:T(8,128)S(1)}, u32[]{:S(2)}, u32[]{:S(2)}) async-start(f32[16,8,2,128]{3,0,2,1:T(8,128)} %bitcast.16), calls=%async_computation.2 | async-start | bytes 262144 | tf_op jit(solution)/shard_map/all_to_all | solution.py:74
  72.5 86.0 %reduce-scatter.4.cloned.1.call-start = ((), (), s32[]{:S(2)}) async-start(), calls=%async_computation.11 | async-start | bytes 2621440 | tf_op jit(solution)/shard_map/reduce_scatter | solution.py:89
  126.9 31.6 %copy-start.2 = (f32[4,256,128]{2,1,0:T(8,128)S(1)}, f32[4,256,128]{2,1,0:T(8,128)}, u32[]{:S(2)}) copy-start(f32[4,256,128]{2,1,0:T(8,128)} %param.6) | copy-start | bytes 1572868
  127.0 69.3 %all-gather.6.cloned.1.call-start = ((), (), s32[]{:S(2)}) async-start(), calls=%async_computation.12 | async-start | bytes 1310720 | tf_op jit(solution)/shard_map/all_gather | solution.py:88
  201.5 35.1 %all-to-all-start.3 = ((bf16[16,8,2,128]{3,0,2,1:T(8,128)(2,1)}), bf16[16,8,2,128]{3,0,2,1:T(8,128)(2,1)S(1)}, u32[]{:S(2)}, u32[]{:S(2)}) async-start(bf16[16,8,2,128]{3,0,2,1:T(8,128)(2,1)} %bitcast.21), calls=%async_computation.4 | async-start | bytes 131072 | tf_op jit(solution)/shard_map/all_to_all | solution.py:60
  236.7 52.4 %all-to-all-start.4 = ((f32[16,8,2,128]{3,0,2,1:T(8,128)}), f32[16,8,2,128]{3,0,2,1:T(8,128)S(1)}, u32[]{:S(2)}, u32[]{:S(2)}) async-start(f32[16,8,2,128]{3,0,2,1:T(8,128)} %bitcast.25), calls=%async_computation.5 | async-start | bytes 262144 | tf_op jit(solution)/shard_map/all_to_all | solution.py:74
  242.6 87.3 %reduce-scatter.6.cloned.1.call-start = ((), (), s32[]{:S(2)}) async-start(), calls=%async_computation.13 | async-start | bytes 2621440 | tf_op jit(solution)/shard_map/reduce_scatter | solution.py:89
  298.4 69.3 %all-gather.8.cloned.1.call-start = ((), (), s32[]{:S(2)}) async-start(), calls=%async_computation.14 | async-start | bytes 1310720 | tf_op jit(solution)/shard_map/all_gather | solution.py:88
  372.9 35.1 %all-to-all-start.5 = ((bf16[16,8,2,128]{3,0,2,1:T(8,128)(2,1)}), bf16[16,8,2,128]{3,0,2,1:T(8,128)(2,1)S(1)}, u32[]{:S(2)}, u32[]{:S(2)}) async-start(bf16[16,8,2,128]{3,0,2,1:T(8,128)(2,1)} %bitcast.30), calls=%async_computation.7 | async-start | bytes 131072 | tf_op jit(solution)/shard_map/all_to_all | solution.py:60
  408.1 52.6 %all-to-all-start.6 = ((f32[16,8,2,128]{3,0,2,1:T(8,128)}), f32[16,8,2,128]{3,0,2,1:T(8,128)S(1)}, u32[]{:S(2)}, u32[]{:S(2)}) async-start(f32[16,8,2,128]{3,0,2,1:T(8,128)} %bitcast.34), calls=%async_computation.8 | async-start | bytes 262144 | tf_op jit(solution)/shard_map/all_to_all | solution.py:74
  414.1 87.3 %reduce-scatter.8.cloned.1.call-start = ((), (), s32[]{:S(2)}) async-start(), calls=%async_computation.15 | async-start | bytes 2621440 | tf_op jit(solution)/shard_map/reduce_scatter | solution.py:89
  470.0 31.4 %copy-start.1 = (f32[4,256,128]{2,1,0:T(8,128)S(1)}, f32[4,256,128]{2,1,0:T(8,128)}, u32[]{:S(2)}) copy-start(f32[4,256,128]{2,1,0:T(8,128)} %reduce-scatter.6.cloned.1.call-done) | copy-start | bytes 1572868
Sparse Core Ops, SparseCore 0:
  8.9 19.4 all-gather.3
  127.1 31.4 reduce-scatter.3
  183.2 12.9 all-gather.5
  298.5 31.4 reduce-scatter.5
  354.6 12.9 all-gather.7
  470.1 31.1 reduce-scatter.7
where the time goes:
time: 538 us; the launch traced here: 534 us
  other arithmetic  186 us (35%)
  waiting for transfers between devices  127 us (24%)
  blocking collectives  64 us (12%)
  matrix products  61.8 us (11%)
  starting transfers between devices  42.2 us (8%)
  local copies, waits for them, and re-layouts  38.1 us (7%)
  between operations  13.6 us (3%)
    reduce_scatter x3, waiting for transfers between devices, operate(): lax.psum_scatter(local_product(whole, blocks, diag_blocks, plan), 'band',...  94.4 us
    scatter-add x3, other arithmetic, local_product(): result = result.at[:, target, :].add(kept)  94.3 us
    scatter-add x3, other arithmetic, local_product(): outgoing = jnp.zeros((vectors, groups * CAP + 1, node_count), jnp.float32...  62.8 us
    dot_general x3, matrix products, local_product(): jnp.einsum('rac,vrc->vra', stored, gathered, preferred_element_type=jnp.f...  28.5 us
    all_gather x3, waiting for transfers between devices, operate(): whole = lax.all_gather(vector, 'band', axis=0, tiled=True)  27 us
    dot_general x3, matrix products, local_product(): jnp.einsum('rac,vra->vrc', stored, whole, preferred_element_type=jnp.floa...  24 us
    psum x1, blocking collectives, body(): lax.psum(jnp.sum(second * image_second, axis=(1, 2)), 'curve')  21.4 us
    psum x1, blocking collectives, body(): drive_norm = lax.psum(jnp.sum(drive * drive, axis=(1, 2)), 'curve')  21.3 us
  transfers between devices with their start and end apart: 13, of which 7 were waited for; matrix products, arithmetic and copies ran while one was open for 43% of the time, Pallas kernels for 0%

commit v1 on v0

v1 whole, which is shorter than its diff:
```python
import functools

import jax
import jax.numpy as jnp
from jax import lax
from jax.experimental import pallas as pl
from jax.experimental.pallas import tpu as pltpu
from jax.sharding import PartitionSpec as P

CAP = 2
TAYLOR = 16
UNROLL = 8
STEPS = 8

epsilon = 1e-06
time_step = 0.5
quadratic = 1.0
STEP = 256.0
FULL = 32767.0

f32 = jnp.float32
bf16 = jnp.bfloat16
i32 = jnp.int32


def nonlinear(field):
    return quadratic * field * field - field * field * field


def tile(index, rows):
    return pl.ds(pl.multiple_of(index * rows, rows), rows)


def smem():
    return pl.BlockSpec(memory_space=pltpu.SMEM)


def vmem():
    return pl.BlockSpec(memory_space=pltpu.VMEM)


def times(field, block):
    return lax.dot_general(field, block, (((1,), (0,)), ((), ())), preferred_element_type=f32)


def times_transposed(field, block):
    return lax.dot_general(field, block, (((1,), (1,)), ((), ())), preferred_element_type=f32)


def row_sum(part):
    return jnp.sum(part, axis=1, keepdims=True)


def plan_kernel(rows, groups, cols, where, pick, target, wanted, origin, count):
    here = where[0]

    def clear(peer, carry):
        count[peer] = 0
        return carry

    lax.fori_loop(0, groups, clear, 0)

    def empty(slot, carry):
        wanted[slot] = -1
        origin[slot] = 0
        return carry

    lax.fori_loop(0, groups * CAP, empty, 0)

    def visit(row, carry):
        column = cols[row]
        owner = column // rows
        inner = column - owner * rows
        pick[row] = inner
        target[row] = inner

        @pl.when(owner != here)
        def _():
            rank = count[owner]
            count[owner] = rank + 1
            slot = owner * CAP + rank
            wanted[slot] = inner
            origin[slot] = row
            pick[row] = rows + owner * (2 * CAP) + rank
            target[row] = rows

        return carry

    lax.fori_loop(0, rows, visit, 0)


def plan(cols, here):
    rows = cols.shape[0]
    groups = lax.axis_size("curve")
    slots = groups * CAP
    return pl.pallas_call(
        functools.partial(plan_kernel, rows, groups),
        out_shape=[jax.ShapeDtypeStruct((n,), i32) for n in (rows, rows, slots, slots)],
        in_specs=[smem(), smem()],
        out_specs=[smem()] * 4,
        scratch_shapes=[pltpu.SMEM((groups,), i32)],
        name="plan",
    )(cols, here)


def pick_blocks_kernel(slots, origin, blocks, out, sems):
    copies = [pltpu.make_async_copy(blocks.at[origin[k], 0], out.at[k], sems.at[k]) for k in range(slots)]
    for copy in copies:
        copy.start()
    for copy in copies:
        copy.wait()


def pick_blocks(origin, blocks):
    slots = origin.shape[0]
    node = blocks.shape[-1]
    return pl.pallas_call(
        functools.partial(pick_blocks_kernel, slots),
        out_shape=jax.ShapeDtypeStruct((slots, node, node), blocks.dtype),
        in_specs=[smem(), pl.BlockSpec(memory_space=pl.ANY)],
        out_specs=pl.BlockSpec(memory_space=pl.ANY),
        scratch_shapes=[pltpu.SemaphoreType.DMA((slots,))],
        name="pick_blocks",
    )(origin, blocks)


def spread_kernel(rows, vectors, groups, width, asked, origin, where, *refs):
    parts, (field, message, wide) = refs[: vectors // width], refs[vectors // width :]
    band = where[1]
    for k, part in enumerate(parts):
        start = jnp.bitwise_xor(band, k) * width
        for v in range(width):
            wide[pl.ds(start + v, rows, stride=vectors), :] = part[v].astype(f32)
    field[...] = wide[...].astype(bf16)

    def send(slot, carry):
        peer = slot // CAP
        rank = slot - peer * CAP
        place = peer * (2 * CAP) + rank
        message[tile(place, vectors), :] = field[tile(jnp.maximum(asked[slot], 0), vectors), :]
        message[tile(place + CAP, vectors), :] = field[tile(origin[slot], vectors), :]
        return carry

    lax.fori_loop(0, groups * CAP, send, 0)


def spread(parts, asked, origin, where):
    width, rows, node = parts[0].shape
    groups = lax.axis_size("curve")
    vectors = width * len(parts)
    return pl.pallas_call(
        functools.partial(spread_kernel, rows, vectors, groups, width),
        out_shape=[
            jax.ShapeDtypeStruct((rows * vectors, node), bf16),
            jax.ShapeDtypeStruct((groups * 2 * CAP * vectors, node), bf16),
        ],
        in_specs=[smem()] * 3 + [vmem()] * len(parts),
        out_specs=[vmem()] * 2,
        scratch_shapes=[pltpu.VMEM((rows * vectors, node), f32)],
        name="spread",
    )(asked, origin, where, *parts)


def block_products(rows, vectors, step, pick, target, band, field, blocks, diag, total):
    count = blocks.shape[0]
    base = step * count

    def some(chunk, carry):
        forward, mirrored, places = [], [], []
        for u in range(UNROLL):
            inner = chunk * UNROLL + u
            row = base + inner
            block = blocks[inner, 0]
            forward.append(times_transposed(field[tile(pick[row], vectors), :], block))
            mirrored.append(times(field[tile(row, vectors), :], block))
            places.append((row, target[row]))
        for (row, aim), one, two in zip(places, forward, mirrored):
            total[tile(row, vectors), :] += one
            total[tile(aim, vectors), :] += two
        return carry

    lax.fori_loop(0, count // UNROLL, some, 0)

    own = diag.shape[0]
    first = band * (own * pl.num_programs(0)) + step * own
    values = [times(field[tile(first + d, vectors), :], diag[d]) for d in range(own)]
    for d, value in enumerate(values):
        total[tile(first + d, vectors), :] += value


def received_products(rows, vectors, groups, asked, field, arrived, total):
    def some(peer, carry):
        values = []
        for k in range(CAP):
            slot = peer * CAP + k
            place = rows + peer * (2 * CAP) + CAP + k
            values.append((asked[slot], times(field[tile(place, vectors), :], arrived[slot])))
        for aim, value in values:
            total[tile(jnp.where(aim < 0, rows, aim), vectors), :] += value
        return carry

    lax.fori_loop(0, groups, some, 0)


def split_out(rows, vectors, band, total, keep, give):
    half = rows // 2
    core = jnp.bitwise_and(band, 1)
    size = half * vectors
    keep[...] = total[pl.ds(pl.multiple_of(core * size, size), size), :]
    give[...] = total[pl.ds(pl.multiple_of((1 - core) * size, size), size), :]


def first_kernel(rows, vectors, groups, pick, target, asked, where, gathered, halo, state, blocks, diag, arrived,
                 keep, give, field, total):
    step = pl.program_id(0)
    band = where[1]

    @pl.when(step == 0)
    def _():
        field[0 : rows * vectors, :] = gathered[...]
        field[rows * vectors :, :] = halo[...]
        total[...] = jnp.zeros_like(total)
        width = state.shape[0]
        for v in range(width):
            total[pl.ds(band * width + v, rows, stride=vectors), :] = nonlinear(state[v])

    block_products(rows, vectors, step, pick, target, band, field, blocks, diag, total)

    @pl.when(step == pl.num_programs(0) - 1)
    def _():
        received_products(rows, vectors, groups, asked, field, arrived, total)
        split_out(rows, vectors, band, total, keep, give)


def unpack(rows, vectors, groups, extra, band, mine, other, halo, convert):
    half = rows // 2
    core = jnp.bitwise_and(band, 1)
    size = half * vectors
    convert(pl.multiple_of(core * size, size), size, lambda ref: ref[0])
    convert(pl.multiple_of((1 - core) * size, size), size, lambda ref: ref[1])


def second_kernel(rows, vectors, groups, pick, target, asked, where, mine, other, halo, blocks, diag, arrived,
                  keep, give, scale, field, total):
    step = pl.program_id(0)
    band = where[1]
    half = rows // 2
    size = half * vectors
    stride = (2 * CAP + 1) * vectors

    @pl.when(step == 0)
    def _():
        energy = jnp.zeros((vectors, halo.shape[1]), f32)
        for g in range(groups):
            energy = energy + halo[g * stride + 2 * CAP * vectors : (g + 1) * stride, :]
        beta = jnp.sqrt(row_sum(energy) + epsilon)
        beta = jnp.broadcast_to(beta, energy.shape)
        scale[...] = beta
        inverse = 1.0 / beta
        core = jnp.bitwise_and(band, 1)

        def one(p, carry):
            field[tile(core * half + p, vectors), :] = (mine[tile(p, vectors), :] * inverse).astype(bf16)
            field[tile((1 - core) * half + p, vectors), :] = (other[tile(p, vectors), :] * inverse).astype(bf16)
            return carry

        lax.fori_loop(0, half, one, 0, unroll=8)

        def row(g, carry):
            for k in range(2 * CAP):
                value = halo[tile(g * (2 * CAP + 1) + k, vectors), :] * inverse
                field[tile(rows + g * (2 * CAP) + k, vectors), :] = value.astype(bf16)
            return carry

        lax.fori_loop(0, groups, row, 0)
        total[...] = jnp.zeros_like(total)

    block_products(rows, vectors, step, pick, target, band, field, blocks, diag, total)

    @pl.when(step == pl.num_programs(0) - 1)
    def _():
        received_products(rows, vectors, groups, asked, field, arrived, total)
        split_out(rows, vectors, band, total, keep, give)


def third_kernel(rows, vectors, groups, width, pick, where, scale, mine_d, other_d, halo_d, mine_i, other_i, halo_i,
                 blocks, diag, share, own_first, own_second, alpha_out, beta_out, field, wide, dots):
    step = pl.program_id(0)
    band = where[1]
    half = rows // 2
    node = scale.shape[1]
    shape = (vectors, node)
    stride = (2 * CAP + 2) * vectors

    @pl.when(step == 0)
    def _():
        alpha = jnp.zeros(shape, f32)
        energy = jnp.zeros(shape, f32)
        for g in range(groups):
            at = g * stride + 2 * CAP * vectors
            alpha = alpha + halo_i[at : at + vectors, :]
            energy = energy + halo_i[at + vectors : at + 2 * vectors, :]
        inverse = 1.0 / scale[...]
        alpha = jnp.broadcast_to(row_sum(alpha), shape) * inverse
        energy = jnp.broadcast_to(row_sum(energy), shape)
        beta = jnp.sqrt(jnp.maximum(energy - alpha * alpha, 0.0) + epsilon)
        alpha_out[...] = alpha
        beta_out[...] = beta
        over = 1.0 / beta
        core = jnp.bitwise_and(band, 1)

        def second_of(drive, image):
            return (image - alpha * (drive * inverse)) * over

        def one(p, carry):
            for place, drive, image in ((core * half + p, mine_d, mine_i), ((1 - core) * half + p, other_d, other_i)):
                value = second_of(drive[tile(p, vectors), :], image[tile(p, vectors), :])
                wide[tile(place, vectors), :] = value
                field[tile(place, vectors), :] = value.astype(bf16)
            return carry

        lax.fori_loop(0, half, one, 0, unroll=8)

        def row(g, carry):
            for k in range(2 * CAP):
                value = second_of(
                    halo_d[tile(g * (2 * CAP + 1) + k, vectors), :], halo_i[tile(g * (2 * CAP + 2) + k, vectors), :]
                )
                field[tile(rows + g * (2 * CAP) + k, vectors), :] = value.astype(bf16)
            return carry

        lax.fori_loop(0, groups, row, 0)
        dots[...] = jnp.zeros_like(dots)
        for v in range(width):
            at = band * width + v
            lift = inverse[0:1, :] * 0.0 + 1.0
            mine_row = mine_d[pl.ds(at, half, stride=vectors), :]
            other_row = other_d[pl.ds(at, half, stride=vectors), :]
            gain = jnp.broadcast_to(1.0 / scale[pl.ds(at, 1), :], mine_row.shape)
            own_first[v, pl.ds(pl.multiple_of(core * half, half), half), :] = mine_row * gain
            own_first[v, pl.ds(pl.multiple_of((1 - core) * half, half), half), :] = other_row * gain
            own_second[v] = wide[pl.ds(at, rows, stride=vectors), :]

    count = blocks.shape[0]
    base = step * count

    def some(chunk, carry):
        part = carry
        for u in range(UNROLL):
            inner = chunk * UNROLL + u
            row = base + inner
            value = times_transposed(field[tile(pick[row], vectors), :], blocks[inner, 0])
            part = part + value * field[tile(row, vectors), :].astype(f32)
        return part

    part = lax.fori_loop(0, count // UNROLL, some, jnp.zeros(shape, f32))
    own = diag.shape[0]
    first = band * (own * pl.num_programs(0)) + step * own
    core = jnp.bitwise_and(band, 1)
    gain = 1.0 / scale[...]
    beta = beta_out[...]
    acc = 2.0 * part
    for d in range(own):
        row = first + d
        value = times(field[tile(row, vectors), :], diag[d])
        acc = acc + value * field[tile(row, vectors), :].astype(f32)
        inside = row - (row // half) * half
        drive = jnp.where(
            row // half == core, mine_d[tile(inside, vectors), :], other_d[tile(inside, vectors), :]
        )
        acc = acc - (beta * wide[tile(row, vectors), :]) * (drive * gain)
    dots[...] += acc

    @pl.when(step == pl.num_programs(0) - 1)
    def _():
        across = lax.broadcasted_iota(i32, shape, 1)
        down = lax.broadcasted_iota(i32, shape, 0)
        column = jnp.broadcast_to(row_sum(dots[...]), shape)
        line = jnp.sum(jnp.where(across == down, column, 0.0), axis=0, keepdims=True)
        share[...] = jnp.broadcast_to(line, share.shape)


def block_specs(rows, node, diag_rows, steps):
    return [
        pl.BlockSpec((rows // steps, 1, node, node), lambda i: (i, 0, 0, 0)),
        pl.BlockSpec((diag_rows // steps, node, node), lambda i: (i, 0, 0)),
    ]


def apply_first(plans, gathered, halo, state, blocks, diag, arrived):
    pick, target, asked, where = plans
    rows, node = blocks.shape[0], blocks.shape[-1]
    vectors = gathered.shape[0] // rows
    groups = lax.axis_size("curve")
    half = jax.ShapeDtypeStruct((rows // 2 * vectors, node), f32)
    return pl.pallas_call(
        functools.partial(first_kernel, rows, vectors, groups),
        grid=(STEPS,),
        out_shape=[half, half],
        in_specs=[smem()] * 4 + [vmem()] * 3 + block_specs(rows, node, diag.shape[0], STEPS) + [vmem()],
        out_specs=[vmem()] * 2,
        scratch_shapes=[
            pltpu.VMEM(((rows + groups * 2 * CAP) * vectors, node), bf16),
            pltpu.VMEM(((rows + 1) * vectors, node), f32),
        ],
        name="operate_first",
    )(pick, target, asked, where, gathered, halo, state, blocks, diag, arrived)


def apply_second(plans, mine, other, halo, blocks, diag, arrived):
    pick, target, asked, where = plans
    rows, node = blocks.shape[0], blocks.shape[-1]
    groups = lax.axis_size("curve")
    vectors = halo.shape[0] // (groups * (2 * CAP + 1))
    half = jax.ShapeDtypeStruct((rows // 2 * vectors, node), f32)
    return pl.pallas_call(
        functools.partial(second_kernel, rows, vectors, groups),
        grid=(STEPS,),
        out_shape=[half, half, jax.ShapeDtypeStruct((vectors, node), f32)],
        in_specs=[smem()] * 4 + [vmem()] * 3 + block_specs(rows, node, diag.shape[0], STEPS) + [vmem()],
        out_specs=[vmem()] * 3,
        scratch_shapes=[
            pltpu.VMEM(((rows + groups * 2 * CAP) * vectors, node), bf16),
            pltpu.VMEM(((rows + 1) * vectors, node), f32),
        ],
        name="operate_second",
    )(pick, target, asked, where, mine, other, halo, blocks, diag, arrived)


def apply_third(plans, width, scale, drive, image, blocks, diag, devices):
    pick, target, asked, where = plans
    rows, node = blocks.shape[0], blocks.shape[-1]
    groups = lax.axis_size("curve")
    vectors = scale.shape[0]
    own = jax.ShapeDtypeStruct((width, rows, node), f32)
    one = jax.ShapeDtypeStruct((vectors, node), f32)
    return pl.pallas_call(
        functools.partial(third_kernel, rows, vectors, groups, width),
        grid=(STEPS,),
        out_shape=[jax.ShapeDtypeStruct((devices, node), f32), own, own, one, one],
        in_specs=[smem()] * 2 + [vmem()] * 7 + block_specs(rows, node, diag.shape[0], STEPS),
        out_specs=[vmem()] * 5,
        scratch_shapes=[
            pltpu.VMEM(((rows + groups * 2 * CAP) * vectors, node), bf16),
            pltpu.VMEM((rows * vectors, node), f32),
            pltpu.VMEM((vectors, node), f32),
        ],
        name="operate_third",
    )(pick, where, scale, *drive, *image, blocks, diag)


def encode_kernel(half, vectors, keep, came, code, wide):
    node = keep.shape[1]
    lanes = lax.broadcasted_iota(i32, (vectors, node), 1)
    for group in range(half // node):
        peak = jnp.zeros((vectors, node), f32)
        for p in range(node):
            at = (group * node + p) * vectors
            value = keep[at : at + vectors, :] + came[at : at + vectors, :]
            wide[at : at + vectors, :] = value
            peak = jnp.where(lanes == p, jnp.max(jnp.abs(value), axis=1, keepdims=True), peak)
        power = jnp.ceil(jnp.log2(jnp.maximum(peak, 1e-30)) * STEP) + 1.0
        start = half * vectors + group * vectors
        code[start : start + vectors, :] = power.astype(i32).astype(jnp.int16)
        gain = FULL * jnp.exp2(power * (-1.0 / STEP))
        for p in range(node):
            at = (group * node + p) * vectors
            scaled = wide[at : at + vectors, :] * gain[:, p : p + 1]
            code[at : at + vectors, :] = jnp.round(scaled).astype(i32).astype(jnp.int16)


def encode(keep, came, vectors):
    size, node = keep.shape
    half = size // vectors
    return pl.pallas_call(
        functools.partial(encode_kernel, half, vectors),
        out_shape=jax.ShapeDtypeStruct((size + half // node * vectors, node), jnp.int16),
        in_specs=[vmem()] * 2,
        out_specs=vmem(),
        scratch_shapes=[pltpu.VMEM((size, node), f32)],
        name="encode",
    )(keep, came)


def decode_kernel(half, vectors, weighted, *refs):
    if weighted:
        code, came, drive, out = refs
    else:
        code, came, out = refs
    node = code.shape[1]
    shape = (vectors, node)
    energy = jnp.zeros(shape, f32)
    cross = jnp.zeros(shape, f32)
    for group in range(half // node):
        start = half * vectors + group * vectors
        gains = [
            jnp.exp2(ref[start : start + vectors, :].astype(i32).astype(f32) * (1.0 / STEP)) * (1.0 / FULL)
            for ref in (code, came)
        ]
        for p in range(node):
            at = (group * node + p) * vectors
            one, two = [
                ref[at : at + vectors, :].astype(i32).astype(f32) * gain[:, p : p + 1]
                for ref, gain in zip((code, came), gains)
            ]
            value = one + two
            out[at : at + vectors, :] = value
            energy = energy + value * value
            if weighted:
                cross = cross + value * drive[at : at + vectors, :]
    at = half * vectors
    if weighted:
        out[at : at + vectors, :] = cross
        at = at + vectors
    out[at : at + vectors, :] = energy


def decode(code, came, vectors, drive=None):
    node = code.shape[1]
    extra = 1 if drive is None else 2
    half = code.shape[0] * node // (node + 1) // vectors
    inputs = (code, came) if drive is None else (code, came, drive)
    return pl.pallas_call(
        functools.partial(decode_kernel, half, vectors, drive is not None),
        out_shape=jax.ShapeDtypeStruct(((half + extra) * vectors, node), f32),
        in_specs=[vmem()] * len(inputs),
        out_specs=vmem(),
        name="decode",
    )(*inputs)


def pack_kernel(half, vectors, groups, extra, asked, origin, where, mine, other, message):
    core = jnp.bitwise_and(where[1], 1)
    each = 2 * CAP + extra

    def fetch(row):
        side = row // half
        inside = row - side * half
        return jnp.where(side == core, mine[tile(inside, vectors), :], other[tile(inside, vectors), :])

    sums = [
        mine[(half + e) * vectors : (half + e + 1) * vectors, :]
        + other[(half + e) * vectors : (half + e + 1) * vectors, :]
        for e in range(extra)
    ]

    def send(peer, carry):
        for k in range(CAP):
            slot = peer * CAP + k
            message[tile(peer * each + k, vectors), :] = fetch(jnp.maximum(asked[slot], 0))
            message[tile(peer * each + CAP + k, vectors), :] = fetch(origin[slot])
        for e in range(extra):
            message[tile(peer * each + 2 * CAP + e, vectors), :] = sums[e]
        return carry

    lax.fori_loop(0, groups, send, 0)


def pack(asked, origin, where, mine, other, vectors, extra):
    node = mine.shape[1]
    half = mine.shape[0] // vectors - extra
    groups = lax.axis_size("curve")
    return pl.pallas_call(
        functools.partial(pack_kernel, half, vectors, groups, extra),
        out_shape=jax.ShapeDtypeStruct((groups * (2 * CAP + extra) * vectors, node), f32),
        in_specs=[smem()] * 3 + [vmem()] * 2,
        out_specs=vmem(),
        name="pack",
    )(asked, origin, where, mine, other)


def finish_kernel(vectors, where, shares, scale, alpha, beta, state, first, second, out, one, two):
    shape = scale.shape
    across = lax.broadcasted_iota(i32, shape, 1)
    down = lax.broadcasted_iota(i32, shape, 0)
    line = jnp.broadcast_to(jnp.sum(shares[...], axis=0, keepdims=True), shape)
    alpha_second = jnp.broadcast_to(row_sum(jnp.where(across == down, line, 0.0)), shape)
    alpha_first, beta_first = alpha[...], beta[...]
    term_one = jnp.ones(shape, f32)
    term_two = jnp.zeros(shape, f32)
    total_one, total_two = term_one, term_two
    for turn in range(1, TAYLOR):
        factor = time_step / (turn + 1.0)
        next_one = factor * (alpha_first * term_one + beta_first * term_two)
        next_two = factor * (beta_first * term_one + alpha_second * term_two)
        term_one, term_two = next_one, next_two
        total_one, total_two = total_one + next_one, total_two + next_two
    one[...] = total_one
    two[...] = total_two
    width = state.shape[0]
    for v in range(width):
        at = where[1] * width + v
        spread_to = state.shape[1:]
        lift = jnp.broadcast_to(time_step * scale[pl.ds(at, 1), :], spread_to)
        weight_one = jnp.broadcast_to(one[pl.ds(at, 1), :], spread_to)
        weight_two = jnp.broadcast_to(two[pl.ds(at, 1), :], spread_to)
        out[v] = state[v] + lift * (weight_one * first[v] + weight_two * second[v])


def finish(where, shares, scale, alpha, beta, state, first, second):
    vectors, node = scale.shape
    return pl.pallas_call(
        functools.partial(finish_kernel, vectors),
        out_shape=jax.ShapeDtypeStruct(state.shape, f32),
        in_specs=[smem()] + [vmem()] * 7,
        out_specs=vmem(),
        scratch_shapes=[pltpu.VMEM((vectors, node), f32)] * 2,
        name="finish",
    )(where, shares, scale, alpha, beta, state, first, second)


def swap(array, bit):
    size = lax.axis_size("band")
    return lax.ppermute(array, "band", [(k, k ^ bit) for k in range(size)])


def exchange(array):
    return lax.all_to_all(array, "curve", split_axis=0, concat_axis=0, tiled=True)


def band_sum(keep, give, vectors, drive=None):
    code = encode(keep, swap(give, 1), vectors)
    mine = decode(code, swap(code, 2), vectors, drive)
    return mine, swap(mine, 1)


def body(state, blocks, diag_blocks, block_cols):
    groups = lax.axis_size("curve")
    devices = groups * lax.axis_size("band")
    width = state.shape[0]
    vectors = width * lax.axis_size("band")
    rounded = state.astype(bf16)
    across = swap(rounded, 2)
    parts = [rounded, swap(rounded, 1), across, swap(across, 1)]
    where = jnp.stack([lax.axis_index("curve"), lax.axis_index("band")]).astype(i32)
    pick, target, wanted, origin = plan(block_cols[:, 0], where)
    asked = exchange(wanted.reshape(groups, CAP)).reshape(-1)
    arrived = exchange(pick_blocks(origin, blocks))
    plans = (pick, target, asked, where)
    gathered, message = spread(parts, asked, origin, where)
    halo = exchange(message)
    keep, give = apply_first(plans, gathered, halo, state, blocks, diag_blocks, arrived)
    mine, other = band_sum(keep, give, vectors)
    halo = exchange(pack(asked, origin, where, mine, other, vectors, 1))
    drive = (mine, other, halo)
    keep, give, scale = apply_second(plans, mine, other, halo, blocks, diag_blocks, arrived)
    mine, other = band_sum(keep, give, vectors, mine)
    halo = exchange(pack(asked, origin, where, mine, other, vectors, 2))
    image = (mine, other, halo)
    share, first, second, alpha, beta = apply_third(plans, width, scale, drive, image, blocks, diag_blocks, devices)
    shares = lax.all_to_all(share, ("curve", "band"), split_axis=0, concat_axis=0, tiled=True)
    return finish(where, shares, scale, alpha, beta, state, first, second)


def solution(mesh):
    return jax.shard_map(
        body,
        mesh=mesh,
        in_specs=(
            P("band", "curve", None),
            P("curve", "band", None, None),
            P(("curve", "band"), None, None),
            P("curve", "band"),
        ),
        out_specs=P("band", "curve", None),
        check_vma=False,
    )
```

time: 538 us -> 239 us (0.44)
  other arithmetic: 186 us -> 2.37 us
  Pallas kernels: 0 us -> 99.5 us
  waiting for transfers between devices: 127 us -> 43.3 us
  matrix products: 61.8 us -> 0 us
  starting transfers between devices: 42.2 us -> 9.49 us
  local copies, waits for them, and re-layouts: 38.1 us -> 8.12 us
  between operations: 13.6 us -> 0.13 us
  blocking collectives: 64 us -> 74.6 us
    scatter-add x9 -> x0, other arithmetic: 165 us -> none  [the longest x3 94.3 us: local_product(): result = result.at[:, target, :].add(kept)]
    pallas_call x0 -> x13, Pallas kernels: none -> 99.5 us  [the longest x1 17.8 us: apply_second(): pl.pallas_call(functools.partial(second_kernel, rows, vectors, groups), g...]
    reduce_scatter x3 -> x0, waiting for transfers between devices: 94.4 us -> none  [operate(): lax.psum_scatter(local_product(whole, blocks, diag_blocks, plan), 'band',...]
    all_to_all x0 -> x5, blocking collectives: none -> 74.6 us  [the longest x4 64.1 us: exchange(): lax.all_to_all(array, 'curve', split_axis=0, concat_axis=0, tiled=True)]
    psum x3 -> x0, blocking collectives: 64 us -> none  [the longest x1 21.4 us: body(): lax.psum(jnp.sum(second * image_second, axis=(1, 2)), 'curve')]
    dot_general x9 -> x0, matrix products: 61.8 us -> none  [the longest x3 28.5 us: local_product(): jnp.einsum('rac,vrc->vra', stored, gathered, preferred_element_type=jnp.f...]
    ppermute x0 -> x9, waiting for transfers between devices: none -> 43.3 us  [swap(): return lax.ppermute(array, 'band', [(k, k ^ bit) for k in range(size)])]
    all_to_all x7 -> x1, starting transfers between devices: 41.8 us -> 3.37 us  [exchange(): lax.all_to_all(array, 'curve', split_axis=0, concat_axis=0, tiled=True)]
  transfers between devices with their start and end apart: 13 -> 10, of which waited for: 7 -> 7; matrix products, arithmetic and copies ran while one was open for 43% -> 1% of each run, Pallas kernels for 0% -> 11%
where the time goes in v1:
time: 239 us; the launch traced here: 238 us
  Pallas kernels  99.5 us (42%)
  blocking collectives  74.6 us (31%)
  waiting for transfers between devices  43.3 us (18%)
  starting transfers between devices  9.49 us (4%)
  local copies, waits for them, and re-layouts  8.12 us (3%)
    all_to_all x4, blocking collectives, exchange(): lax.all_to_all(array, 'curve', split_axis=0, concat_axis=0, tiled=True)  64.1 us
    ppermute x9, waiting for transfers between devices, swap(): return lax.ppermute(array, 'band', [(k, k ^ bit) for k in range(size)])  43.3 us
    pallas_call x1, Pallas kernels, apply_second(): pl.pallas_call(functools.partial(second_kernel, rows, vectors, groups), g...  17.8 us
    pallas_call x1, Pallas kernels, pick_blocks(): pl.pallas_call(functools.partial(pick_blocks_kernel, slots), out_shape=ja...  17.8 us
    pallas_call x1, Pallas kernels, apply_first(): pl.pallas_call(functools.partial(first_kernel, rows, vectors, groups), gr...  17.2 us
    pallas_call x1, Pallas kernels, apply_third(): pl.pallas_call(functools.partial(third_kernel, rows, vectors, groups, wid...  15.1 us
    all_to_all x1, blocking collectives, body(): lax.all_to_all(share, ('curve', 'band'), split_axis=0, concat_axis=0, til...  10.5 us
    pallas_call x1, Pallas kernels, plan(): pl.pallas_call(functools.partial(plan_kernel, rows, groups), out_shape=[j...  7.49 us
  transfers between devices with their start and end apart: 10, of which 7 were waited for; matrix products, arithmetic and copies ran while one was open for 1% of the time, Pallas kernels for 11%

profile of v1, /device:TPU:0, one launch (start us, length us, event | category | flops | bytes accessed | tf_op | source)
XLA Modules:
  0.0 237.6 jit_solution(14909115689665567645)
XLA Ops:
  1.1 3.0 %collective-permute-start.1 = (bf16[4,256,128]{2,1,0:T(8,128)(2,1)S(1)}, bf16[4,256,128]{2,1,0:T(8,128)(2,1)S(1)}, u32[]{:S(2)}, u32[]{:S(2)}) collective-permute-start(bf16[4,256,128]{2,1,0:T(8,128)(2,1)S(1)} %convert_element_type.3.refs_0_), channel_id=1, source_target_pairs={{0,2},{1,3},{2,0},{3,1},{4,6},{5,7},{6,4},{7,5},{8,10},{9,11},{10,... | collective-permute-start | bytes 786440 | tf_op jit(solution)/shard_map/ppermute | solution.py:614
  4.1 6.3 %collective-permute-done.1.refs_2_ = bf16[4,256,128]{2,1,0:T(8,128)(2,1)S(1)} collective-permute-done((bf16[4,256,128]{2,1,0:T(8,128)(2,1)S(1)}, bf16[4,256,128]{2,1,0:T(8,128)(2,1)S(1)}, u32[]{:S(2)}, u32[]{:S(2)}) %collective-permute-start.1) | collective-permute-done | bytes 262176 | tf_op jit(solution)/shard_map/ppermute | solution.py:614
  11.1 7.5 %plan.1 = (s32[256]{0:T(256)}, s32[256]{0:T(256)}, s32[16]{0:T(128)}, s32[16]{0:T(128)}) custom-call(s32[256]{0:T(256)} %bitcast.24, s32[2]{0:T(128)} %pad_add_fusion.where), custom_call_target="tpu_custom_call" | custom-call | tf_op jit(solution)/shard_map/plan/pallas_call | solution.py:96
  19.3 12.4 %all_to_all.58 = s32[8,1,2]{2,1,0:T(1,128)S(1)} all-to-all(s32[8,1,2]{2,1,0:T(1,128)S(1)} %bitcast.23), channel_id=1, replica_groups=mesh['curve'=8,'band'=4] {'curve'}, dimensions={0} | all-to-all | bytes 128 | tf_op jit(solution)/shard_map/all_to_all | solution.py:618
  34.3 3.7 %spread.1 = (bf16[4096,128]{1,0:T(8,128)(2,1)}, bf16[512,128]{1,0:T(8,128)(2,1)}) custom-call(s32[16]{0:T(128)} %reshape.16.asked, s32[16]{0:T(128)} %get-tuple-element.24.origin, s32[2]{0:T(128)} %pad_add_fusion.where, bf16[4,256,128]{2,1,0:T(8,128)(2,1)} %copy-done.4, bf16[4,256,128]{2,1,0:T(8,128)(2,1)} %copy-done.9, bf16[4,256,128]{2,1,0:T(8,128)(2,1)} %copy-done.8, ...), custom_call_target="tpu_custom_call" | custom-call | tf_op jit(solution)/shard_map/spread/pallas_call | solution.py:151
  37.9 3.4 %all-to-all-start.1 = ((bf16[8,64,128]{2,1,0:T(8,128)(2,1)}), bf16[8,64,128]{2,1,0:T(8,128)(2,1)S(1)}, u32[]{:S(2)}, u32[]{:S(2)}) async-start(bf16[8,64,128]{2,1,0:T(8,128)(2,1)} %bitcast.20), calls=%async_computation.1 | async-start | bytes 262144 | tf_op jit(solution)/shard_map/all_to_all | solution.py:618
  41.3 17.8 %pick_blocks.1 = bf16[16,128,128]{2,1,0:T(8,128)(2,1)} custom-call(s32[16]{0:T(128)} %get-tuple-element.24.origin, bf16[256,1,128,128]{3,2,1,0:T(8,128)(2,1)} %blocks.7), custom_call_target="tpu_custom_call" | custom-call | tf_op jit(solution)/shard_map/pick_blocks/pallas_call | solution.py:117
  59.1 19.5 %all_to_all.59.arrived = bf16[16,128,128]{2,1,0:T(8,128)(2,1)} all-to-all(bf16[16,128,128]{2,1,0:T(8,128)(2,1)} %pick_blocks.1), channel_id=1, replica_groups=mesh['curve'=8,'band'=4] {'curve'}, dimensions={0} | all-to-all | bytes 1048576 | tf_op jit(solution)/shard_map/all_to_all | solution.py:618
  78.6 17.2 %operate_first.1 = (f32[2048,128]{1,0:T(8,128)}, f32[2048,128]{1,0:T(8,128)}) custom-call(s32[256]{0:T(256)} %get-tuple-element.21.pick, s32[256]{0:T(256)} %get-tuple-element.22.target, s32[16]{0:T(128)} %reshape.16.asked, s32[2]{0:T(128)} %pad_add_fusion.where, bf16[4096,128]{1,0:T(8,128)(2,1)} %get-tuple-element.25.gathered, bf16[512,128]{1,0:T(8,128)(2,1)} %bitcast.19, ...), custom_call_target="tpu_custom_call" | custom-call | tf_op jit(solution)/shard_map/operate_first/pallas_call | solution.py:396
  95.9 2.9 %collective-permute-done.3.came = f32[2048,128]{1,0:T(8,128)S(1)} collective-permute-done((f32[2048,128]{1,0:T(8,128)}, f32[2048,128]{1,0:T(8,128)S(1)}, u32[]{:S(2)}, u32[]{:S(2)}) %collective-permute-start.3) | collective-permute-done | bytes 1048608 | tf_op jit(solution)/shard_map/ppermute | solution.py:614
  99.7 3.2 %encode.2.refs_0_ = s16[2064,128]{1,0:T(8,128)(2,1)} custom-call(f32[2048,128]{1,0:T(8,128)} %get-tuple-element.27.keep, f32[2048,128]{1,0:T(8,128)} %copy-done.2), custom_call_target="tpu_custom_call" | custom-call | tf_op jit(solution)/shard_map/encode/pallas_call | solution.py:475
  104.5 12.8 %collective-permute-done.4.refs_1_ = s16[2064,128]{1,0:T(8,128)(2,1)S(1)} collective-permute-done((s16[2064,128]{1,0:T(8,128)(2,1)}, s16[2064,128]{1,0:T(8,128)(2,1)S(1)}, u32[]{:S(2)}, u32[]{:S(2)}) %collective-permute-start.4) | collective-permute-done | bytes 528416 | tf_op jit(solution)/shard_map/ppermute | solution.py:614
  118.1 3.0 %decode.2.mine.refs_2_.mine_d = f32[2064,128]{1,0:T(8,128)} custom-call(s16[2064,128]{1,0:T(8,128)(2,1)} %encode.2.refs_0_, s16[2064,128]{1,0:T(8,128)(2,1)} %copy-done.6), custom_call_target="tpu_custom_call" | custom-call | tf_op jit(solution)/shard_map/decode/pallas_call | solution.py:523
  121.1 2.9 %collective-permute-done.5.other.other_d = f32[2064,128]{1,0:T(8,128)S(1)} collective-permute-done((f32[2064,128]{1,0:T(8,128)}, f32[2064,128]{1,0:T(8,128)S(1)}, u32[]{:S(2)}, u32[]{:S(2)}) %collective-permute-start.5) | collective-permute-done | bytes 1056800 | tf_op jit(solution)/shard_map/ppermute | solution.py:614
  127.4 15.6 %all_to_all.60 = f32[8,80,128]{2,1,0:T(8,128)} all-to-all(f32[8,80,128]{2,1,0:T(8,128)} %bitcast.18), channel_id=1, replica_groups=mesh['curve'=8,'band'=4] {'curve'}, dimensions={0} | all-to-all | bytes 655360 | tf_op jit(solution)/shard_map/all_to_all | solution.py:618
  143.0 17.8 %operate_second.1 = (f32[2048,128]{1,0:T(8,128)}, f32[2048,128]{1,0:T(8,128)}, f32[16,128]{1,0:T(8,128)}) custom-call(s32[256]{0:T(256)} %get-tuple-element.21.pick, s32[256]{0:T(256)} %get-tuple-element.22.target, s32[16]{0:T(128)} %reshape.16.asked, s32[2]{0:T(128)} %pad_add_fusion.where, f32[2064,128]{1,0:T(8,128)} %decode.2.mine.refs_2_.mine_d, ...), custom_call_target="tpu_custom_call" | custom-call | tf_op jit(solution)/shard_map/operate_second/pallas_call | solution.py:416
  160.9 2.9 %collective-permute-done.6.came = f32[2048,128]{1,0:T(8,128)S(1)} collective-permute-done((f32[2048,128]{1,0:T(8,128)}, f32[2048,128]{1,0:T(8,128)S(1)}, u32[]{:S(2)}, u32[]{:S(2)}) %collective-permute-start.6) | collective-permute-done | bytes 1048608 | tf_op jit(solution)/shard_map/ppermute | solution.py:614
  164.7 3.2 %encode.3.refs_0_ = s16[2064,128]{1,0:T(8,128)(2,1)} custom-call(f32[2048,128]{1,0:T(8,128)} %get-tuple-element.30.keep, f32[2048,128]{1,0:T(8,128)} %copy-done.3), custom_call_target="tpu_custom_call" | custom-call | tf_op jit(solution)/shard_map/encode/pallas_call | solution.py:475
  169.4 12.8 %collective-permute-done.7.refs_1_ = s16[2064,128]{1,0:T(8,128)(2,1)S(1)} collective-permute-done((s16[2064,128]{1,0:T(8,128)(2,1)}, s16[2064,128]{1,0:T(8,128)(2,1)S(1)}, u32[]{:S(2)}, u32[]{:S(2)}) %collective-permute-start.7) | collective-permute-done | bytes 528416 | tf_op jit(solution)/shard_map/ppermute | solution.py:614
  183.0 3.4 %decode.3.mine.mine_i = f32[2080,128]{1,0:T(8,128)} custom-call(s16[2064,128]{1,0:T(8,128)(2,1)} %encode.3.refs_0_, s16[2064,128]{1,0:T(8,128)(2,1)} %copy-done.5, f32[2064,128]{1,0:T(8,128)} %decode.2.mine.refs_2_.mine_d), custom_call_target="tpu_custom_call" | custom-call | tf_op jit(solution)/shard_map/decode/pallas_call | solution.py:523
  186.4 2.9 %collective-permute-done.8.other.other_i = f32[2080,128]{1,0:T(8,128)S(1)} collective-permute-done((f32[2080,128]{1,0:T(8,128)}, f32[2080,128]{1,0:T(8,128)S(1)}, u32[]{:S(2)}, u32[]{:S(2)}) %collective-permute-start.8) | collective-permute-done | bytes 1064992 | tf_op jit(solution)/shard_map/ppermute | solution.py:614
  192.8 16.7 %all_to_all.61 = f32[8,96,128]{2,1,0:T(8,128)} all-to-all(f32[8,96,128]{2,1,0:T(8,128)} %bitcast.16), channel_id=1, replica_groups=mesh['curve'=8,'band'=4] {'curve'}, dimensions={0} | all-to-all | bytes 786432 | tf_op jit(solution)/shard_map/all_to_all | solution.py:618
  209.5 15.1 %operate_third.1 = (f32[32,128]{1,0:T(8,128)}, f32[4,256,128]{2,1,0:T(8,128)}, f32[4,256,128]{2,1,0:T(8,128)}, f32[16,128]{1,0:T(8,128)}, f32[16,128]{1,0:T(8,128)}) custom-call(s32[256]{0:T(256)} %get-tuple-element.21.pick, s32[2]{0:T(128)} %pad_add_fusion.where, f32[16,128]{1,0:T(8,128)} %get-tuple-element.29.scale, ...), custom_call_target="tpu_custom_call" | custom-call | tf_op jit(solution)/shard_map/operate_third/pallas_call | solution.py:437
  224.6 10.5 %all_to_all.62 = f32[32,1,128]{2,1,0:T(1,128)} all-to-all(f32[32,1,128]{2,1,0:T(1,128)} %bitcast.22), channel_id=1, replica_groups=mesh['curve'=8,'band'=4] {'curve','band'}, dimensions={0} | all-to-all | bytes 32768 | tf_op jit(solution)/shard_map/all_to_all | solution.py:651
  (42 shorter events, 21.2 us)
Async XLA Ops:
  1.1 32.4 %copy-start.4 = (bf16[4,256,128]{2,1,0:T(8,128)(2,1)}, bf16[4,256,128]{2,1,0:T(8,128)(2,1)S(1)}, u32[]{:S(2)}) copy-start(bf16[4,256,128]{2,1,0:T(8,128)(2,1)S(1)} %convert_element_type.3.refs_0_) | copy-start | bytes 786436
  1.1 9.3 %collective-permute-start.1 = (bf16[4,256,128]{2,1,0:T(8,128)(2,1)S(1)}, bf16[4,256,128]{2,1,0:T(8,128)(2,1)S(1)}, u32[]{:S(2)}, u32[]{:S(2)}) collective-permute-start(bf16[4,256,128]{2,1,0:T(8,128)(2,1)S(1)} %convert_element_type.3.refs_0_), channel_id=1, source_target_pairs={{0,2},{1,3},{2,0},{3,1},{4,6},{5,7},{6,4},{7,5},{8,10},{9,11},{10,... | collective-permute-start | bytes 786440 | tf_op jit(solution)/shard_map/ppermute | solution.py:614
  4.1 29.3 %collective-permute-start = (bf16[4,256,128]{2,1,0:T(8,128)(2,1)S(1)}, bf16[4,256,128]{2,1,0:T(8,128)(2,1)S(1)}, u32[]{:S(2)}, u32[]{:S(2)}) collective-permute-start(bf16[4,256,128]{2,1,0:T(8,128)(2,1)S(1)} %convert_element_type.3.refs_0_), channel_id=1, source_target_pairs={{0,1},{1,0},{2,3},{3,2},{4,5},{5,4},{6,7},{7,6},{8,9},{9,8},{10,11... | collective-permute-start | bytes 786440 | tf_op jit(solution)/shard_map/ppermute | solution.py:614
  10.4 23.1 %copy-start.8 = (bf16[4,256,128]{2,1,0:T(8,128)(2,1)}, bf16[4,256,128]{2,1,0:T(8,128)(2,1)S(1)}, u32[]{:S(2)}) copy-start(bf16[4,256,128]{2,1,0:T(8,128)(2,1)S(1)} %collective-permute-done.1.refs_2_) | copy-start | bytes 786436
  10.4 23.0 %collective-permute-start.2 = (bf16[4,256,128]{2,1,0:T(8,128)(2,1)S(1)}, bf16[4,256,128]{2,1,0:T(8,128)(2,1)S(1)}, u32[]{:S(2)}, u32[]{:S(2)}) collective-permute-start(bf16[4,256,128]{2,1,0:T(8,128)(2,1)S(1)} %collective-permute-done.1.refs_2_), channel_id=1, source_target_pairs={{0,1},{1,0},{2,3},{3,2},{4,5},{5,4},{6,7},{7,6},{8,9},{9,8},{10,11... | collective-permute-start | bytes 786440 | tf_op jit(solution)/shard_map/ppermute | solution.py:614
  33.5 0.7 copy-start.9
  33.5 0.8 copy-start.10
  37.9 21.2 %all-to-all-start.1 = ((bf16[8,64,128]{2,1,0:T(8,128)(2,1)}), bf16[8,64,128]{2,1,0:T(8,128)(2,1)S(1)}, u32[]{:S(2)}, u32[]{:S(2)}) async-start(bf16[8,64,128]{2,1,0:T(8,128)(2,1)} %bitcast.20), calls=%async_computation.1 | async-start | bytes 262144 | tf_op jit(solution)/shard_map/all_to_all | solution.py:618
  59.1 19.5 %copy-start.7 = (bf16[8,64,128]{2,1,0:T(8,128)(2,1)}, bf16[8,64,128]{2,1,0:T(8,128)(2,1)S(1)}, u32[]{:S(2)}) copy-start(bf16[8,64,128]{2,1,0:T(8,128)(2,1)S(1)} %all-to-all-done.1) | copy-start | bytes 393220
  95.9 2.9 %collective-permute-start.3 = (f32[2048,128]{1,0:T(8,128)}, f32[2048,128]{1,0:T(8,128)S(1)}, u32[]{:S(2)}, u32[]{:S(2)}) collective-permute-start(f32[2048,128]{1,0:T(8,128)} %get-tuple-element.28), channel_id=1, source_target_pairs={{0,1},{1,0},{2,3},{3,2},{4,5},{5,4},{6,7},{7,6},{8,9},{9,8},{10,11... | collective-permute-start | bytes 3145736 | tf_op jit(solution)/shard_map/ppermute | solution.py:614
  98.7 1.0 copy-start.2
  103.0 14.3 %collective-permute-start.4 = (s16[2064,128]{1,0:T(8,128)(2,1)}, s16[2064,128]{1,0:T(8,128)(2,1)S(1)}, u32[]{:S(2)}, u32[]{:S(2)}) collective-permute-start(s16[2064,128]{1,0:T(8,128)(2,1)} %encode.2.refs_0_), channel_id=1, source_target_pairs={{0,2},{1,3},{2,0},{3,1},{4,6},{5,7},{6,4},{7,5},{8,10},{9,11},{10,... | collective-permute-start | bytes 1585160 | tf_op jit(solution)/shard_map/ppermute | solution.py:614
  117.2 0.8 copy-start.6
  121.1 2.9 %collective-permute-start.5 = (f32[2064,128]{1,0:T(8,128)}, f32[2064,128]{1,0:T(8,128)S(1)}, u32[]{:S(2)}, u32[]{:S(2)}) collective-permute-start(f32[2064,128]{1,0:T(8,128)} %decode.2.mine.refs_2_.mine_d), channel_id=1, source_target_pairs={{0,1},{1,0},{2,3},{3,2},{4,5},{5,4},{6,7},{7,6},{8,9},{9,8},{10,11... | collective-permute-start | bytes 3170312 | tf_op jit(solution)/shard_map/ppermute | solution.py:614
  123.9 1.0 copy-start
  160.8 2.9 %collective-permute-start.6 = (f32[2048,128]{1,0:T(8,128)}, f32[2048,128]{1,0:T(8,128)S(1)}, u32[]{:S(2)}, u32[]{:S(2)}) collective-permute-start(f32[2048,128]{1,0:T(8,128)} %get-tuple-element.31), channel_id=1, source_target_pairs={{0,1},{1,0},{2,3},{3,2},{4,5},{5,4},{6,7},{7,6},{8,9},{9,8},{10,11... | collective-permute-start | bytes 3145736 | tf_op jit(solution)/shard_map/ppermute | solution.py:614
  163.7 1.0 copy-start.3
  167.9 14.3 %collective-permute-start.7 = (s16[2064,128]{1,0:T(8,128)(2,1)}, s16[2064,128]{1,0:T(8,128)(2,1)S(1)}, u32[]{:S(2)}, u32[]{:S(2)}) collective-permute-start(s16[2064,128]{1,0:T(8,128)(2,1)} %encode.3.refs_0_), channel_id=1, source_target_pairs={{0,2},{1,3},{2,0},{3,1},{4,6},{5,7},{6,4},{7,5},{8,10},{9,11},{10,... | collective-permute-start | bytes 1585160 | tf_op jit(solution)/shard_map/ppermute | solution.py:614
  182.2 0.8 copy-start.5
  186.4 2.9 %collective-permute-start.8 = (f32[2080,128]{1,0:T(8,128)}, f32[2080,128]{1,0:T(8,128)S(1)}, u32[]{:S(2)}, u32[]{:S(2)}) collective-permute-start(f32[2080,128]{1,0:T(8,128)} %decode.3.mine.mine_i), channel_id=1, source_target_pairs={{0,1},{1,0},{2,3},{3,2},{4,5},{5,4},{6,7},{7,6},{8,9},{9,8},{10,11... | collective-permute-start | bytes 3194888 | tf_op jit(solution)/shard_map/ppermute | solution.py:614
  189.3 1.0 copy-start.1

commit v2 on v0

v2 whole, which is shorter than its diff:
```python
import functools

import jax
import jax.numpy as jnp
from jax import lax
from jax.experimental import pallas as pl
from jax.experimental.pallas import tpu as pltpu
from jax.sharding import PartitionSpec as P

CAP = 2
TAYLOR = 16
UNROLL = 32
CHUNKS = 2

epsilon = 1e-06
time_step = 0.5
quadratic = 1.0
STEP = 256.0
FULL = 32767.0

f32 = jnp.float32
bf16 = jnp.bfloat16
i32 = jnp.int32


def nonlinear(field):
    return quadratic * field * field - field * field * field


def tile(index, rows):
    return pl.ds(pl.multiple_of(index * rows, rows), rows)


def smem():
    return pl.BlockSpec(memory_space=pltpu.SMEM)


def vmem():
    return pl.BlockSpec(memory_space=pltpu.VMEM)


def anywhere():
    return pl.BlockSpec(memory_space=pl.ANY)


def params(mebibytes):
    return pltpu.CompilerParams(vmem_limit_bytes=mebibytes * 1024 * 1024)


def shaped(shape, dtype):
    return jax.ShapeDtypeStruct(shape, dtype)


def times(field, block):
    return lax.dot_general(field, block, (((1,), (0,)), ((), ())), preferred_element_type=f32)


def times_transposed(field, block):
    return lax.dot_general(field, block, (((1,), (1,)), ((), ())), preferred_element_type=f32)


def row_sum(part):
    return jnp.sum(part, axis=1, keepdims=True)


def as_line(column, shape):
    across = lax.broadcasted_iota(i32, shape, 1)
    down = lax.broadcasted_iota(i32, shape, 0)
    return jnp.sum(jnp.where(across == down, jnp.broadcast_to(column, shape), 0.0), axis=0, keepdims=True)


def as_column(line, shape, offset=0):
    across = lax.broadcasted_iota(i32, shape, 1)
    down = lax.broadcasted_iota(i32, shape, 0)
    picked = jnp.where(across == down + offset, jnp.broadcast_to(line, shape), 0.0)
    return jnp.broadcast_to(row_sum(picked), shape)


def core_of(band):
    return jnp.bitwise_and(band, 1)


def plan_kernel(cols, pick, target, wanted, origin):
    groups, lanes = wanted.shape
    rows = cols.shape[1]
    here = lax.axis_index("curve")
    column = cols[...]
    owner = column // rows
    inner = column - owner * rows
    shape = (groups, rows)
    peer = lax.broadcasted_iota(i32, shape, 0)
    place = lax.broadcasted_iota(i32, shape, 1).astype(f32)
    inside = jnp.broadcast_to(inner.astype(f32), shape)
    left = (jnp.broadcast_to(owner, shape) == peer) & (peer != here)
    number = jnp.zeros((1, rows), f32)
    lane = lax.broadcasted_iota(i32, (groups, lanes), 1)
    want = jnp.full((groups, lanes), -1.0, f32)
    source = jnp.zeros((groups, lanes), f32)
    none = float(rows)
    for k in range(CAP):
        least = jnp.min(jnp.where(left, place, none), axis=1, keepdims=True)
        hit = left & (place == least)
        left = left & (place != least)
        aim = row_sum(jnp.where(hit, inside, 0.0))
        want = jnp.where((lane == k) & (least < none), aim, want)
        source = jnp.where((lane == k) & (least < none), least, source)
        slot = (peer * (2 * CAP) + k).astype(f32)
        number = number + jnp.sum(jnp.where(hit, slot, 0.0), axis=0, keepdims=True)
    wanted[...] = want.astype(i32)
    origin[...] = source.astype(i32)
    pick[...] = jnp.where(owner == here, inner, rows + number.astype(i32))
    target[...] = jnp.where(owner == here, inner, rows)


def plan(cols):
    rows = cols.shape[1]
    groups = lax.axis_size("curve")
    return pl.pallas_call(
        plan_kernel,
        out_shape=[shaped((1, rows), i32)] * 2 + [shaped((groups, 128), i32)] * 2,
        in_specs=[vmem()],
        out_specs=[vmem()] * 4,
        compiler_params=params(8),
        name="plan",
    )(cols)


def spread_kernel(rows, vectors, groups, width, origin, blocks, *refs):
    count = vectors // width
    parts, (field, own, split, wide, sems) = refs[:count], refs[count:]
    slots = groups * CAP

    def fetch(slot):
        peer = slot // CAP
        row = origin[peer, slot - peer * CAP]
        return pltpu.make_async_copy(blocks.at[row, 0], own.at[slot], sems.at[slot])

    def begin(slot, carry):
        fetch(slot).start()
        return carry

    lax.fori_loop(0, slots, begin, 0)
    band = lax.axis_index("band")
    for k, part in enumerate(parts):
        start = jnp.bitwise_xor(band, k) * width
        for v in range(width):
            wide[pl.ds(start + v, rows, stride=vectors), :] = part[v].astype(f32)
    field[0 : rows * vectors, :] = wide[...].astype(bf16)
    field[rows * vectors :, :] = jnp.zeros((vectors, field.shape[1]), bf16)

    def end(slot, carry):
        fetch(slot).wait()
        return carry

    lax.fori_loop(0, slots, end, 0)

    def product(peer, carry):
        for k in range(CAP):
            value = times(field[tile(origin[peer, k], vectors), :], own[peer * CAP + k])
            high = value.astype(bf16)
            split[tile(peer * (2 * CAP) + k, vectors), :] = high
            split[tile(peer * (2 * CAP) + CAP + k, vectors), :] = (value - high.astype(f32)).astype(bf16)
        return carry

    lax.fori_loop(0, groups, product, 0)


def spread(parts, origin, blocks):
    width, rows, node = parts[0].shape
    groups = lax.axis_size("curve")
    slots = groups * CAP
    vectors = width * len(parts)
    return pl.pallas_call(
        functools.partial(spread_kernel, rows, vectors, groups, width),
        out_shape=[
            shaped(((rows + 1) * vectors, node), bf16),
            shaped((slots, node, node), bf16),
            shaped((slots * 2 * vectors, node), bf16),
        ],
        in_specs=[smem(), anywhere()] + [vmem()] * len(parts),
        out_specs=[vmem()] * 3,
        scratch_shapes=[pltpu.VMEM((rows * vectors, node), f32), pltpu.SemaphoreType.DMA((slots,))],
        compiler_params=params(16),
        name="spread",
    )(origin, blocks, *parts)


def reply_kernel(vectors, groups, asked, field, split, message):
    def send(peer, carry):
        at = peer * (3 * CAP)
        for k in range(CAP):
            message[tile(at + k, vectors), :] = field[tile(jnp.maximum(asked[peer, k], 0), vectors), :]
        for k in range(2 * CAP):
            message[tile(at + CAP + k, vectors), :] = split[tile(peer * (2 * CAP) + k, vectors), :]
        return carry

    lax.fori_loop(0, groups, send, 0)


def reply(asked, field, split, vectors):
    groups = lax.axis_size("curve")
    return pl.pallas_call(
        functools.partial(reply_kernel, vectors, groups),
        out_shape=shaped((groups * 3 * CAP * vectors, field.shape[1]), bf16),
        in_specs=[smem()] + [vmem()] * 2,
        out_specs=vmem(),
        compiler_params=params(16),
        name="reply",
    )(asked, field, split)


class Stream:
    def __init__(self, blocks, diag, held, held_diag, sems):
        self.blocks, self.diag, self.held, self.held_diag, self.sems = blocks, diag, held, held_diag, sems
        self.pieces = blocks.shape[0] // UNROLL
        self.own = diag.shape[0] // self.pieces

    def copies(self, piece):
        rows = pl.ds(piece * UNROLL, UNROLL)
        own = pl.ds(piece * self.own, self.own)
        return (
            pltpu.make_async_copy(self.blocks.at[rows, 0], self.held.at[rows], self.sems.at[0, piece]),
            pltpu.make_async_copy(self.diag.at[own], self.held_diag.at[own], self.sems.at[1, piece]),
        )

    def start(self):
        for piece in range(self.pieces):
            for copy in self.copies(piece):
                copy.start()

    def wait(self, piece):
        for copy in self.copies(piece):
            copy.wait()


def stream_scratch(blocks, diag):
    rows, node = blocks.shape[0], blocks.shape[-1]
    return [
        pltpu.VMEM((rows, node, node), bf16),
        pltpu.VMEM(diag.shape, bf16),
        pltpu.SemaphoreType.DMA((2, rows // UNROLL)),
    ]


def products(vectors, limit, pick, target, field, stream, total):
    band = lax.axis_index("band")

    def some(piece, carry):
        stream.wait(piece)
        forward, mirrored = [], []
        base = piece * UNROLL
        for u in range(UNROLL):
            row = base + u
            block = stream.held[row]
            source = pick[0, row]
            if limit is not None:
                source = jnp.minimum(source, limit)
            forward.append(times_transposed(field[tile(source, vectors), :], block))
            mirrored.append(times(field[tile(row, vectors), :], block))
        for u in range(UNROLL):
            total[tile(base + u, vectors), :] += forward[u]
            total[tile(target[0, base + u], vectors), :] += mirrored[u]
        own = stream.own
        first = band * (own * stream.pieces) + piece * own
        values = [times(field[tile(first + d, vectors), :], stream.held_diag[piece * own + d]) for d in range(own)]
        for d, value in enumerate(values):
            total[tile(first + d, vectors), :] += value
        return carry

    lax.fori_loop(0, stream.pieces, some, 0)


def give_out(rows, vectors, total, outs):
    core = core_of(lax.axis_index("band"))
    half = rows // 2
    size = half // CHUNKS * vectors
    for side in range(2):
        start = jnp.where(core == side, 0, half) * vectors
        for c in range(CHUNKS):
            outs[side * CHUNKS + c][...] = total[pl.ds(pl.multiple_of(start + c * size, size), size), :]


def local_kernel(rows, vectors, pick, target, field, state, blocks, diag, total, *scratch):
    stream = Stream(blocks, diag, *scratch)
    stream.start()
    total[...] = jnp.zeros_like(total)
    width = state.shape[0]
    band = lax.axis_index("band")
    for v in range(width):
        total[pl.ds(band * width + v, rows, stride=vectors), :] = nonlinear(state[v])
    products(vectors, rows, pick, target, field, stream, total)


def operate_local(pick, target, field, state, blocks, diag):
    rows, node = blocks.shape[0], blocks.shape[-1]
    vectors = field.shape[0] // (rows + 1)
    return pl.pallas_call(
        functools.partial(local_kernel, rows, vectors),
        out_shape=shaped(((rows + 1) * vectors, node), f32),
        in_specs=[smem()] * 2 + [vmem()] * 2 + [anywhere()] * 2,
        out_specs=vmem(),
        scratch_shapes=stream_scratch(blocks, diag),
        compiler_params=params(24),
        name="operate_local",
    )(pick, target, field, state, blocks, diag)


def settle_kernel(rows, vectors, groups, wanted, origin, asked, local, halo, own, *refs):
    outs, total = refs[:-1], refs[-1]
    total[...] = local[...]

    def some(peer, carry):
        at = peer * (3 * CAP)
        values = []
        for k in range(CAP):
            value = times_transposed(halo[tile(at + k, vectors), :], own[peer * CAP + k])
            values.append((jnp.where(wanted[peer, k] < 0, rows, origin[peer, k]), value))
        for k in range(CAP):
            value = halo[tile(at + CAP + k, vectors), :].astype(f32)
            value = value + halo[tile(at + 2 * CAP + k, vectors), :].astype(f32)
            values.append((jnp.where(asked[peer, k] < 0, rows, asked[peer, k]), value))
        for aim, value in values:
            total[tile(aim, vectors), :] += value
        return carry

    lax.fori_loop(0, groups, some, 0)
    give_out(rows, vectors, total, outs)


def chunk_shapes(rows, vectors, node):
    return [shaped((rows // 2 // CHUNKS * vectors, node), f32)] * (2 * CHUNKS)


def settle(wanted, origin, asked, local, halo, own, rows):
    node = local.shape[1]
    vectors = local.shape[0] // (rows + 1)
    groups = lax.axis_size("curve")
    outs = pl.pallas_call(
        functools.partial(settle_kernel, rows, vectors, groups),
        out_shape=chunk_shapes(rows, vectors, node),
        in_specs=[smem()] * 3 + [vmem()] * 3,
        out_specs=[vmem()] * (2 * CHUNKS),
        scratch_shapes=[pltpu.VMEM(local.shape, f32)],
        compiler_params=params(24),
        name="settle",
    )(wanted, origin, asked, local, halo, own)
    return outs[:CHUNKS], outs[CHUNKS:]


def second_kernel(rows, vectors, groups, pick, target, asked, *refs):
    arrays, (halo, arrived, blocks, diag), refs = refs[: 2 * CHUNKS], refs[2 * CHUNKS : 2 * CHUNKS + 4], refs[2 * CHUNKS + 4 :]
    outs, (scale, field, total), scratch = refs[: 2 * CHUNKS], refs[2 * CHUNKS : 2 * CHUNKS + 3], refs[2 * CHUNKS + 3 :]
    stream = Stream(blocks, diag, *scratch)
    stream.start()
    half = rows // 2
    each = half // CHUNKS
    message = halo.shape[0] // groups
    shape = scale.shape
    line = jnp.zeros((1, shape[1]), f32)
    for g in range(groups):
        at = g * message + 2 * CAP * vectors
        line = line + halo[at : at + 1, :]
    energy = as_column(line, shape)
    beta = jnp.sqrt(energy + epsilon)
    scale[...] = beta
    inverse = 1.0 / beta
    core = core_of(lax.axis_index("band"))
    for side in range(2):
        start = jnp.where(core == side, 0, half)
        for c in range(CHUNKS):
            array = arrays[side * CHUNKS + c]

            def one(p, carry, start=start, c=c, array=array):
                field[tile(start + c * each + p, vectors), :] = (array[tile(p, vectors), :] * inverse).astype(bf16)
                return carry

            lax.fori_loop(0, each, one, 0, unroll=16)

    def row(g, carry):
        for k in range(2 * CAP):
            at = pl.multiple_of(g * message + k * vectors, 8)
            value = halo[pl.ds(at, vectors), :] * inverse
            field[tile(rows + g * (2 * CAP) + k, vectors), :] = value.astype(bf16)
        return carry

    lax.fori_loop(0, groups, row, 0)
    total[...] = jnp.zeros_like(total)
    products(vectors, None, pick, target, field, stream, total)

    def some(peer, carry):
        values = []
        for k in range(CAP):
            place = rows + peer * (2 * CAP) + CAP + k
            aim = asked[peer, k]
            value = times(field[tile(place, vectors), :], arrived[peer * CAP + k])
            values.append((jnp.where(aim < 0, rows, aim), value))
        for aim, value in values:
            total[tile(aim, vectors), :] += value
        return carry

    lax.fori_loop(0, groups, some, 0)
    give_out(rows, vectors, total, outs)


def operate_second(pick, target, asked, arrays, halo, arrived, blocks, diag):
    rows, node = blocks.shape[0], blocks.shape[-1]
    groups = lax.axis_size("curve")
    message = halo.shape[0] // groups
    vectors = (message - 8) // (2 * CAP)
    outs = pl.pallas_call(
        functools.partial(second_kernel, rows, vectors, groups),
        out_shape=chunk_shapes(rows, vectors, node) + [shaped((vectors, node), f32)],
        in_specs=[smem()] * 3 + [vmem()] * (2 * CHUNKS + 2) + [anywhere()] * 2,
        out_specs=[vmem()] * (2 * CHUNKS + 1),
        scratch_shapes=[
            pltpu.VMEM(((rows + groups * 2 * CAP) * vectors, node), bf16),
            pltpu.VMEM(((rows + 1) * vectors, node), f32),
        ]
        + stream_scratch(blocks, diag),
        compiler_params=params(32),
        name="operate_second",
    )(pick, target, asked, *arrays, halo, arrived, blocks, diag)
    return outs[:CHUNKS], outs[CHUNKS : 2 * CHUNKS], outs[-1]


def third_kernel(rows, vectors, groups, width, pick, wanted, origin, *refs):
    count = 2 * CHUNKS
    drive, image, (own, blocks, diag), refs = refs[:count], refs[count : 2 * count], refs[2 * count : 2 * count + 3], refs[2 * count + 3 :]
    form, left, drive_own, image_own, field = refs[:5]
    stream = Stream(blocks, diag, *refs[5:])
    stream.start()
    half = rows // 2
    each = half // CHUNKS
    shape = form.shape
    band = lax.axis_index("band")
    core = core_of(band)
    for side in range(2):
        start = jnp.where(core == side, 0, half)
        for c in range(CHUNKS):
            array = image[side * CHUNKS + c]

            def one(p, carry, start=start, c=c, array=array):
                field[tile(start + c * each + p, vectors), :] = array[tile(p, vectors), :].astype(bf16)
                return carry

            lax.fori_loop(0, each, one, 0, unroll=16)
            for v in range(width):
                inside = pl.ds(pl.multiple_of(start + c * each, each), each)
                source = pl.ds(band * width + v, each, stride=vectors)
                drive_own[v, inside, :] = drive[side * CHUNKS + c][source, :]
                image_own[v, inside, :] = array[source, :]
    field[rows * vectors :, :] = jnp.zeros((vectors, shape[1]), bf16)

    def some(piece, parts):
        stream.wait(piece)
        twice, once = parts
        base = piece * UNROLL
        for u in range(UNROLL):
            row = base + u
            value = times(field[tile(row, vectors), :], stream.held[row])
            source = jnp.minimum(pick[0, row], rows)
            twice = twice + value * field[tile(source, vectors), :].astype(f32)
        for d in range(stream.own):
            row = (band * stream.pieces + piece) * stream.own + d
            here = field[tile(row, vectors), :]
            once = once + times(here, stream.held_diag[piece * stream.own + d]) * here.astype(f32)
        return twice, once

    nothing = jnp.zeros(shape, f32)
    twice, once = lax.fori_loop(0, stream.pieces, some, (nothing, nothing))
    form[...] = 2.0 * twice + once

    def remote(peer, carry):
        for k in range(CAP):
            value = times(field[tile(origin[peer, k], vectors), :], own[peer * CAP + k])
            left[tile(peer * CAP + k, vectors), :] = jnp.where(wanted[peer, k] < 0, 0.0, 2.0) * value
        return carry

    lax.fori_loop(0, groups, remote, 0)


def operate_third(pick, wanted, origin, drive, image, own, blocks, diag, width, vectors):
    rows, node = blocks.shape[0], blocks.shape[-1]
    groups = lax.axis_size("curve")
    mine = shaped((width, rows, node), f32)
    return pl.pallas_call(
        functools.partial(third_kernel, rows, vectors, groups, width),
        out_shape=[shaped((vectors, node), f32), shaped((groups * CAP * vectors, node), f32), mine, mine],
        in_specs=[smem()] * 3 + [vmem()] * (4 * CHUNKS + 1) + [anywhere()] * 2,
        out_specs=[vmem()] * 4,
        scratch_shapes=[pltpu.VMEM(((rows + 1) * vectors, node), bf16)] + stream_scratch(blocks, diag),
        compiler_params=params(32),
        name="operate_third",
    )(pick, wanted, origin, *drive, *image, own, blocks, diag)


def tail_kernel(each, vectors, form, left, halo, *refs):
    image, share = refs[:-1], refs[-1]
    shape = form.shape
    total = form[...]
    for slot in range(left.shape[0] // vectors):
        at = slot * vectors
        total = total + left[at : at + vectors, :] * halo[at : at + vectors, :].astype(f32)
    values = [total]
    for e in range(2):
        at = (each + e) * vectors
        value = image[0][at : at + vectors, :]
        for other in image[1:]:
            value = value + other[at : at + vectors, :]
        values.append(0.5 * value)
    line = jnp.zeros((1, shape[1]), f32)
    across = lax.broadcasted_iota(i32, shape, 1)
    down = lax.broadcasted_iota(i32, shape, 0)
    for e, value in enumerate(values):
        column = jnp.broadcast_to(row_sum(value), shape)
        line = line + jnp.sum(jnp.where(across == down + e * vectors, column, 0.0), axis=0, keepdims=True)
    share[...] = jnp.broadcast_to(line, share.shape)


def tail(form, left, halo, image, devices):
    vectors, node = form.shape
    each = image[0].shape[0] // vectors - 2
    return pl.pallas_call(
        functools.partial(tail_kernel, each, vectors),
        out_shape=shaped((devices, node), f32),
        in_specs=[vmem()] * (3 + len(image)),
        out_specs=vmem(),
        compiler_params=params(16),
        name="tail",
    )(form, left, halo, *image)


def code_tiles(each, node):
    return -(-each // node)


def encode_kernel(each, vectors, keep, came, code, wide):
    node = keep.shape[1]
    lanes = lax.broadcasted_iota(i32, (vectors, node), 1)
    for group in range(code_tiles(each, node)):
        inside = range(group * node, min(each, (group + 1) * node))
        peak = jnp.zeros((vectors, node), f32)
        for p in inside:
            at = p * vectors
            value = keep[at : at + vectors, :] + came[at : at + vectors, :]
            wide[at : at + vectors, :] = value
            peak = jnp.where(lanes == p - group * node, jnp.max(jnp.abs(value), axis=1, keepdims=True), peak)
        power = jnp.ceil(jnp.log2(jnp.maximum(peak, 1e-30)) * STEP) + 1.0
        start = (each + group) * vectors
        code[start : start + vectors, :] = power.astype(i32).astype(jnp.int16)
        gain = FULL * jnp.exp2(power * (-1.0 / STEP))
        for p in inside:
            at = p * vectors
            lane = p - group * node
            scaled = wide[at : at + vectors, :] * gain[:, lane : lane + 1]
            code[at : at + vectors, :] = jnp.round(scaled).astype(i32).astype(jnp.int16)


def encode(keep, came, vectors):
    size, node = keep.shape
    each = size // vectors
    return pl.pallas_call(
        functools.partial(encode_kernel, each, vectors),
        out_shape=shaped(((each + code_tiles(each, node)) * vectors, node), jnp.int16),
        in_specs=[vmem()] * 2,
        out_specs=vmem(),
        scratch_shapes=[pltpu.VMEM((size, node), f32)],
        compiler_params=params(12),
        name="encode",
    )(keep, came)


def decode_kernel(each, vectors, weighted, *refs):
    if weighted:
        code, came, drive, out = refs
    else:
        code, came, out = refs
    node = code.shape[1]
    shape = (vectors, node)
    energy = jnp.zeros(shape, f32)
    cross = jnp.zeros(shape, f32)
    for group in range(code_tiles(each, node)):
        start = (each + group) * vectors
        gains = [
            jnp.exp2(ref[start : start + vectors, :].astype(i32).astype(f32) * (1.0 / STEP)) * (1.0 / FULL)
            for ref in (code, came)
        ]
        for p in range(group * node, min(each, (group + 1) * node)):
            at = p * vectors
            lane = p - group * node
            one, two = [
                ref[at : at + vectors, :].astype(i32).astype(f32) * gain[:, lane : lane + 1]
                for ref, gain in zip((code, came), gains)
            ]
            value = one + two
            out[at : at + vectors, :] = value
            energy = energy + value * value
            if weighted:
                cross = cross + value * drive[at : at + vectors, :]
    at = each * vectors
    if weighted:
        out[at : at + vectors, :] = cross
        at = at + vectors
    out[at : at + vectors, :] = energy


def decode(code, came, vectors, each, drive=None):
    node = code.shape[1]
    extra = 1 if drive is None else 2
    inputs = (code, came) if drive is None else (code, came, drive)
    return pl.pallas_call(
        functools.partial(decode_kernel, each, vectors, drive is not None),
        out_shape=shaped(((each + extra) * vectors, node), f32),
        in_specs=[vmem()] * len(inputs),
        out_specs=vmem(),
        compiler_params=params(12),
        name="decode",
    )(*inputs)


def fetch_row(arrays, each, vectors, row):
    core = core_of(lax.axis_index("band"))
    half = each * CHUNKS
    side = row // half
    inside = row - side * half
    chunk = inside // each
    place = tile(inside - chunk * each, vectors)
    value = arrays[0][place, :]
    number = jnp.where(side == core, chunk, CHUNKS + chunk)
    for k in range(1, 2 * CHUNKS):
        value = jnp.where(number == k, arrays[k][place, :], value)
    return value


def pack_kernel(each, vectors, groups, asked, origin, *refs):
    arrays, message = refs[:-1], refs[-1]
    shape = (vectors, message.shape[1])
    sums = arrays[0][each * vectors :, :]
    for array in arrays[1:]:
        sums = sums + array[each * vectors :, :]
    line = jnp.broadcast_to(as_line(row_sum(sums), shape), shape)[0:8, :]
    size = 2 * CAP * vectors + 8

    def send(peer, carry):
        for k in range(2 * CAP):
            row = jnp.maximum(asked[peer, k], 0) if k < CAP else origin[peer, k - CAP]
            at = pl.multiple_of(peer * size + k * vectors, 8)
            message[pl.ds(at, vectors), :] = fetch_row(arrays, each, vectors, row)
        message[pl.ds(pl.multiple_of(peer * size + 2 * CAP * vectors, 8), 8), :] = line
        return carry

    lax.fori_loop(0, groups, send, 0)


def pack(asked, origin, arrays, vectors):
    node = arrays[0].shape[1]
    each = arrays[0].shape[0] // vectors - 1
    groups = lax.axis_size("curve")
    return pl.pallas_call(
        functools.partial(pack_kernel, each, vectors, groups),
        out_shape=shaped((groups * (2 * CAP * vectors + 8), node), f32),
        in_specs=[smem()] * 2 + [vmem()] * (2 * CHUNKS),
        out_specs=vmem(),
        compiler_params=params(16),
        name="pack",
    )(asked, origin, *arrays)


def pack_rounded_kernel(each, vectors, groups, asked, *refs):
    arrays, message = refs[:-1], refs[-1]

    def send(peer, carry):
        for k in range(CAP):
            value = fetch_row(arrays, each, vectors, jnp.maximum(asked[peer, k], 0))
            message[tile(peer * CAP + k, vectors), :] = value.astype(bf16)
        return carry

    lax.fori_loop(0, groups, send, 0)


def pack_rounded(asked, arrays, vectors):
    node = arrays[0].shape[1]
    each = arrays[0].shape[0] // vectors - 2
    groups = lax.axis_size("curve")
    return pl.pallas_call(
        functools.partial(pack_rounded_kernel, each, vectors, groups),
        out_shape=shaped((groups * CAP * vectors, node), bf16),
        in_specs=[smem()] + [vmem()] * (2 * CHUNKS),
        out_specs=vmem(),
        compiler_params=params(16),
        name="pack_rounded",
    )(asked, *arrays)


def finish_kernel(shares, scale, state, drive, image, out, one, two, lift, mix):
    shape = scale.shape
    vectors = shape[0]
    line = jnp.sum(shares[...], axis=0, keepdims=True)
    form, cross, energy = [as_column(line, shape, e * vectors) for e in range(3)]
    beta_zero = scale[...]
    unit = 1.0 - epsilon / (beta_zero * beta_zero)
    alpha_first = cross / beta_zero
    square = alpha_first * alpha_first
    beta_first = jnp.sqrt(jnp.maximum(energy - square * (2.0 - unit), 0.0) + epsilon)
    alpha_second = (form - 2.0 * alpha_first * energy + square * alpha_first) / (beta_first * beta_first)
    alpha_second = alpha_second - alpha_first * (1.0 - unit)
    term_one = jnp.ones(shape, f32)
    term_two = jnp.zeros(shape, f32)
    total_one, total_two = term_one, term_two
    for turn in range(1, TAYLOR):
        factor = time_step / (turn + 1.0)
        next_one = factor * (alpha_first * term_one + beta_first * term_two)
        next_two = factor * (beta_first * term_one + alpha_second * term_two)
        term_one, term_two = next_one, next_two
        total_one, total_two = total_one + next_one, total_two + next_two
    one[...] = time_step * total_one
    two[...] = time_step * beta_zero * total_two / beta_first
    mix[...] = alpha_first / beta_zero
    width = state.shape[0]
    for v in range(width):
        at = pl.ds(lax.axis_index("band") * width + v, 1)
        size = state.shape[1:]
        weight_one, weight_two, share = [jnp.broadcast_to(ref[at, :], size) for ref in (one, two, mix)]
        out[v] = state[v] + (weight_one * drive[v] + weight_two * (image[v] - share * drive[v]))


def finish(shares, scale, state, drive, image):
    return pl.pallas_call(
        finish_kernel,
        out_shape=shaped(state.shape, f32),
        in_specs=[vmem()] * 5,
        out_specs=vmem(),
        scratch_shapes=[pltpu.VMEM(scale.shape, f32)] * 4,
        compiler_params=params(16),
        name="finish",
    )(shares, scale, state, drive, image)


def swap(array, bit):
    size = lax.axis_size("band")
    return lax.ppermute(array, "band", [(k, k ^ bit) for k in range(size)])


def exchange(array):
    return lax.all_to_all(array, "curve", split_axis=0, concat_axis=0, tiled=True)


def band_sum(keep, give, vectors, drive=None):
    each = keep[0].shape[0] // vectors
    came = [swap(array, 1) for array in give]
    codes = [encode(one, two, vectors) for one, two in zip(keep, came)]
    across = [swap(code, 2) for code in codes]
    mine = [
        decode(code, other, vectors, each, None if drive is None else drive[c])
        for c, (code, other) in enumerate(zip(codes, across))
    ]
    return mine + [swap(array, 1) for array in mine]


def body(state, blocks, diag_blocks, block_cols):
    groups = lax.axis_size("curve")
    devices = groups * lax.axis_size("band")
    width, rows = state.shape[:2]
    vectors = width * lax.axis_size("band")
    rounded = state.astype(bf16)
    across = swap(rounded, 2)
    parts = [rounded, swap(rounded, 1), across, swap(across, 1)]
    pick, target, wanted, origin = plan(block_cols.reshape(1, rows))
    asked = exchange(wanted)
    field, own, split = spread(parts, origin, blocks)
    message = reply(asked, field, split, vectors)
    halo = exchange(message)
    local = operate_local(pick, target, field, state, blocks, diag_blocks)
    keep, give = settle(wanted, origin, asked, local, halo, own, rows)
    drive = band_sum(keep, give, vectors)
    arrived = exchange(own)
    halo = exchange(pack(asked, origin, drive, vectors))
    keep, give, scale = operate_second(pick, target, asked, drive, halo, arrived, blocks, diag_blocks)
    image = band_sum(keep, give, vectors, drive)
    halo = exchange(pack_rounded(asked, image, vectors))
    form, left, drive_own, image_own = operate_third(
        pick, wanted, origin, drive, image, own, blocks, diag_blocks, width, vectors
    )
    share = tail(form, left, halo, image[:CHUNKS], devices)
    shares = lax.all_to_all(share, ("curve", "band"), split_axis=0, concat_axis=0, tiled=True)
    return finish(shares, scale, state, drive_own, image_own)


def solution(mesh):
    return jax.shard_map(
        body,
        mesh=mesh,
        in_specs=(
            P("band", "curve", None),
            P("curve", "band", None, None),
            P(("curve", "band"), None, None),
            P("curve", "band"),
        ),
        out_specs=P("band", "curve", None),
        check_vma=False,
    )
```

time: 538 us -> 182 us (0.34)
  other arithmetic: 186 us -> 1.08 us
  waiting for transfers between devices: 127 us -> 32 us
  matrix products: 61.8 us -> 0 us
  Pallas kernels: 0 us -> 50.7 us
  blocking collectives: 64 us -> 29.1 us
  between operations: 13.6 us -> 0.3 us
  starting transfers between devices: 42.2 us -> 30.1 us
    scatter-add x9 -> x0, other arithmetic: 165 us -> none  [the longest x3 94.3 us: local_product(): result = result.at[:, target, :].add(kept)]
    reduce_scatter x3 -> x0, waiting for transfers between devices: 94.4 us -> none  [operate(): lax.psum_scatter(local_product(whole, blocks, diag_blocks, plan), 'band',...]
    psum x3 -> x0, blocking collectives: 64 us -> none  [the longest x1 21.4 us: body(): lax.psum(jnp.sum(second * image_second, axis=(1, 2)), 'curve')]
    dot_general x9 -> x0, matrix products: 61.8 us -> none  [the longest x3 28.5 us: local_product(): jnp.einsum('rac,vrc->vra', stored, gathered, preferred_element_type=jnp.f...]
    pallas_call x0 -> x19, Pallas kernels: none -> 50.7 us  [the longest x1 12.4 us: operate_second(): pl.pallas_call(functools.partial(second_kernel, rows, vectors, groups), o...]
    unnamed x6 -> x66, local copies, waits for them, and re-layouts: 0.01 us -> 37.4 us
    ppermute x0 -> x15, waiting for transfers between devices: none -> 32 us  [swap(): return lax.ppermute(array, 'band', [(k, k ^ bit) for k in range(size)])]
    all_to_all x0 -> x2, blocking collectives: none -> 29.1 us  [the longest x1 16.1 us: exchange(): lax.all_to_all(array, 'curve', split_axis=0, concat_axis=0, tiled=True)]
  transfers between devices with their start and end apart: 13 -> 19, of which waited for: 7 -> 8; matrix products, arithmetic and copies ran while one was open for 43% -> 0% of each run, Pallas kernels for 0% -> 17%
where the time goes in v2:
time: 182 us; the launch traced here: 181 us
  Pallas kernels  50.7 us (28%)
  local copies, waits for them, and re-layouts  37.4 us (21%)
  waiting for transfers between devices  32 us (18%)
  starting transfers between devices  30.1 us (17%)
  blocking collectives  29.1 us (16%)
    unnamed x66, local copies, waits for them, and re-layouts  37.4 us
    ppermute x15, waiting for transfers between devices, swap(): return lax.ppermute(array, 'band', [(k, k ^ bit) for k in range(size)])  32 us
    all_to_all x4, starting transfers between devices, exchange(): lax.all_to_all(array, 'curve', split_axis=0, concat_axis=0, tiled=True)  21.4 us
    all_to_all x1, blocking collectives, exchange(): lax.all_to_all(array, 'curve', split_axis=0, concat_axis=0, tiled=True)  16.1 us
    all_to_all x1, blocking collectives, body(): lax.all_to_all(share, ('curve', 'band'), split_axis=0, concat_axis=0, til...  12.9 us
    pallas_call x1, Pallas kernels, operate_second(): pl.pallas_call(functools.partial(second_kernel, rows, vectors, groups), o...  12.4 us
    pallas_call x1, Pallas kernels, operate_local(): pl.pallas_call(functools.partial(local_kernel, rows, vectors), out_shape=...  10.1 us
    ppermute x15, starting transfers between devices, swap(): return lax.ppermute(array, 'band', [(k, k ^ bit) for k in range(size)])  8.71 us
  transfers between devices with their start and end apart: 19, of which 8 were waited for; matrix products, arithmetic and copies ran while one was open for 0% of the time, Pallas kernels for 17%

profile of v2, /device:TPU:0, one launch (start us, length us, event | category | flops | bytes accessed | tf_op | source)
XLA Modules:
  0.0 180.7 jit_solution(15527806002039342386)
XLA Ops:
  1.1 3.0 %collective-permute-start.1 = (bf16[4,256,128]{2,1,0:T(8,128)(2,1)S(1)}, bf16[4,256,128]{2,1,0:T(8,128)(2,1)S(1)}, u32[]{:S(2)}, u32[]{:S(2)}) collective-permute-start(bf16[4,256,128]{2,1,0:T(8,128)(2,1)S(1)} %convert_element_type.3.refs_0_), channel_id=1, source_target_pairs={{0,2},{1,3},{2,0},{3,1},{4,6},{5,7},{6,4},{7,5},{8,10},{9,11},{10,... | collective-permute-start | bytes 786440 | tf_op jit(solution)/shard_map/ppermute | solution.py:741
  4.1 6.3 %collective-permute-done.1.refs_2_ = bf16[4,256,128]{2,1,0:T(8,128)(2,1)S(1)} collective-permute-done((bf16[4,256,128]{2,1,0:T(8,128)(2,1)S(1)}, bf16[4,256,128]{2,1,0:T(8,128)(2,1)S(1)}, u32[]{:S(2)}, u32[]{:S(2)}) %collective-permute-start.1) | collective-permute-done | bytes 262176 | tf_op jit(solution)/shard_map/ppermute | solution.py:741
  11.9 6.1 %all-to-all-start = ((s32[8,1,128]{2,1,0:T(1,128)}), s32[8,1,128]{2,1,0:T(1,128)S(1)}, u32[]{:S(2)}, u32[]{:S(2)}) async-start(s32[8,1,128]{2,1,0:T(1,128)} %bitcast.2), calls=%async_computation | async-start | bytes 8192 | tf_op jit(solution)/shard_map/all_to_all | solution.py:745
  18.1 3.4 %copy-done = bf16[256,1,128,128]{3,2,1,0:T(8,128)(2,1)S(1)} copy-done((bf16[256,1,128,128]{3,2,1,0:T(8,128)(2,1)S(1)}, bf16[256,1,128,128]{3,2,1,0:T(8,128)(2,1)}, u32[]{:S(2)}) %copy-start) | copy-done | bytes 8388632
  21.4 4.7 %spread.1 = (bf16[4112,128]{1,0:T(8,128)(2,1)S(1)}, bf16[16,128,128]{2,1,0:T(8,128)(2,1)}, bf16[512,128]{1,0:T(8,128)(2,1)S(1)}) custom-call(s32[8,128]{1,0:T(8,128)S(1)} %get-tuple-element.27.origin, bf16[256,1,128,128]{3,2,1,0:T(8,128)(2,1)S(1)} %copy-done, bf16[4,256,128]{2,1,0:T(8,128)(2,1)S(1)} %convert_element_type.3.refs_0_, ...), custom_call_target="tpu_custom_call" | custom-call | tf_op jit(solution)/shard_map/spread/pallas_call | solution.py:173
  29.9 6.0 %all-to-all-start.1 = ((bf16[8,96,128]{2,1,0:T(8,128)(2,1)}), bf16[8,96,128]{2,1,0:T(8,128)(2,1)S(1)}, u32[]{:S(2)}, u32[]{:S(2)}) async-start(bf16[8,96,128]{2,1,0:T(8,128)(2,1)} %bitcast.4), calls=%async_computation.1 | async-start | bytes 393216 | tf_op jit(solution)/shard_map/all_to_all | solution.py:745
  35.9 3.4 %copy-done.1 = bf16[256,1,128,128]{3,2,1,0:T(8,128)(2,1)S(1)} copy-done((bf16[256,1,128,128]{3,2,1,0:T(8,128)(2,1)S(1)}, bf16[256,1,128,128]{3,2,1,0:T(8,128)(2,1)}, u32[]{:S(2)}) %copy-start.1) | copy-done | bytes 8388632
  40.5 10.1 %operate_local.1.local = f32[4112,128]{1,0:T(8,128)S(1)} custom-call(s32[1,256]{1,0:T(1,128)S(1)} %get-tuple-element.25.pick, s32[1,256]{1,0:T(1,128)S(1)} %get-tuple-element.28.target, bf16[4112,128]{1,0:T(8,128)(2,1)S(1)} %copy-done.23, f32[4,256,128]{2,1,0:T(8,128)S(1)} %copy-done.19, bf16[256,1,128,128]{3,2,1,0:T(8,128)(2,1)S(1)} %copy-done.1, ...), custom_call_target="tpu_custom_call" | custom-call | tf_op jit(solution)/shard_map/operate_local/pallas_call | solution.py:297
  52.0 1.6 copy-done.12
  53.6 3.6 %settle.1 = (f32[1024,128]{1,0:T(8,128)S(1)}, f32[1024,128]{1,0:T(8,128)S(1)}, f32[1024,128]{1,0:T(8,128)}, f32[1024,128]{1,0:T(8,128)}) custom-call(s32[8,128]{1,0:T(8,128)} %get-tuple-element.26.wanted, s32[8,128]{1,0:T(8,128)S(1)} %get-tuple-element.27.origin, s32[8,128]{1,0:T(8,128)S(1)} %bitcast.20, f32[4112,128]{1,0:T(8,128)S(1)} %copy-done.12, ...), custom_call_target="tpu_custom_call" | custom-call | tf_op jit(solution)/shard_map/settle/pallas_call | solution.py:338
  57.7 6.0 %all-to-all-start.3 = ((bf16[16,128,128]{2,1,0:T(8,128)(2,1)}), bf16[16,128,128]{2,1,0:T(8,128)(2,1)}, u32[]{:S(2)}, u32[]{:S(2)}) async-start(bf16[16,128,128]{2,1,0:T(8,128)(2,1)} %get-tuple-element.31.own.refs_8_), calls=%async_computation.3 | async-start | bytes 1048576 | tf_op jit(solution)/shard_map/all_to_all | solution.py:745
  69.0 5.6 %collective-permute-done.6.refs_1_ = s16[1040,128]{1,0:T(8,128)(2,1)S(1)} collective-permute-done((s16[1040,128]{1,0:T(8,128)(2,1)S(1)}, s16[1040,128]{1,0:T(8,128)(2,1)S(1)}, u32[]{:S(2)}, u32[]{:S(2)}) %collective-permute-start.6) | collective-permute-done | bytes 266272 | tf_op jit(solution)/shard_map/ppermute | solution.py:741
  75.2 3.9 %collective-permute-done.4.refs_1_ = s16[1040,128]{1,0:T(8,128)(2,1)S(1)} collective-permute-done((s16[1040,128]{1,0:T(8,128)(2,1)S(1)}, s16[1040,128]{1,0:T(8,128)(2,1)S(1)}, u32[]{:S(2)}, u32[]{:S(2)}) %collective-permute-start.4) | collective-permute-done | bytes 266272 | tf_op jit(solution)/shard_map/ppermute | solution.py:741
  79.6 1.9 %collective-permute-done.7.refs_2_ = f32[1040,128]{1,0:T(8,128)S(1)} collective-permute-done((f32[1040,128]{1,0:T(8,128)S(1)}, f32[1040,128]{1,0:T(8,128)S(1)}, u32[]{:S(2)}, u32[]{:S(2)}) %collective-permute-start.7) | collective-permute-done | bytes 532512 | tf_op jit(solution)/shard_map/ppermute | solution.py:741
  84.4 16.1 %all_to_all.60 = f32[8,72,128]{2,1,0:T(8,128)S(1)} all-to-all(f32[8,72,128]{2,1,0:T(8,128)S(1)} %bitcast.15), channel_id=1, replica_groups=mesh['curve'=8,'band'=4] {'curve'}, dimensions={0} | all-to-all | bytes 589824 | tf_op jit(solution)/shard_map/all_to_all | solution.py:745
  100.5 3.4 %copy-done.2 = bf16[256,1,128,128]{3,2,1,0:T(8,128)(2,1)S(1)} copy-done((bf16[256,1,128,128]{3,2,1,0:T(8,128)(2,1)S(1)}, bf16[256,1,128,128]{3,2,1,0:T(8,128)(2,1)}, u32[]{:S(2)}) %copy-start.2) | copy-done | bytes 8388632
  106.0 12.4 %operate_second.1 = (f32[1024,128]{1,0:T(8,128)S(1)}, f32[1024,128]{1,0:T(8,128)S(1)}, f32[1024,128]{1,0:T(8,128)S(1)}, f32[1024,128]{1,0:T(8,128)S(1)}, f32[16,128]{1,0:T(8,128)S(1)}) custom-call(s32[1,256]{1,0:T(1,128)S(1)} %get-tuple-element.25.pick, s32[1,256]{1,0:T(1,128)S(1)} %get-tuple-element.28.target, s32[8,128]{1,0:T(8,128)S(1)} %bitcast.22, ...), custom_call_target="tpu_custom_call" | custom-call | tf_op jit(solution)/shard_map/operate_second/pallas_call | solution.py:410
  123.6 6.6 %collective-permute-done.12.refs_1_ = s16[1040,128]{1,0:T(8,128)(2,1)S(1)} collective-permute-done((s16[1040,128]{1,0:T(8,128)(2,1)S(1)}, s16[1040,128]{1,0:T(8,128)(2,1)S(1)}, u32[]{:S(2)}, u32[]{:S(2)}) %collective-permute-start.12) | collective-permute-done | bytes 266272 | tf_op jit(solution)/shard_map/ppermute | solution.py:741
  130.7 4.3 %collective-permute-done.10.refs_1_ = s16[1040,128]{1,0:T(8,128)(2,1)S(1)} collective-permute-done((s16[1040,128]{1,0:T(8,128)(2,1)S(1)}, s16[1040,128]{1,0:T(8,128)(2,1)S(1)}, u32[]{:S(2)}, u32[]{:S(2)}) %collective-permute-start.10) | collective-permute-done | bytes 266272 | tf_op jit(solution)/shard_map/ppermute | solution.py:741
  135.6 1.9 %collective-permute-done.13.refs_6_.refs_2_ = f32[1056,128]{1,0:T(8,128)S(1)} collective-permute-done((f32[1056,128]{1,0:T(8,128)S(1)}, f32[1056,128]{1,0:T(8,128)S(1)}, u32[]{:S(2)}, u32[]{:S(2)}) %collective-permute-start.13) | collective-permute-done | bytes 540704 | tf_op jit(solution)/shard_map/ppermute | solution.py:741
  139.1 3.4 %all-to-all-start.4 = ((bf16[8,32,128]{2,1,0:T(8,128)(2,1)}), bf16[8,32,128]{2,1,0:T(8,128)(2,1)S(1)}, u32[]{:S(2)}, u32[]{:S(2)}) async-start(bf16[8,32,128]{2,1,0:T(8,128)(2,1)} %bitcast.8), calls=%async_computation.4 | async-start | bytes 131072 | tf_op jit(solution)/shard_map/all_to_all | solution.py:745
  142.4 3.4 %copy-done.3 = bf16[256,1,128,128]{3,2,1,0:T(8,128)(2,1)S(1)} copy-done((bf16[256,1,128,128]{3,2,1,0:T(8,128)(2,1)S(1)}, bf16[256,1,128,128]{3,2,1,0:T(8,128)(2,1)}, u32[]{:S(2)}) %copy-start.3) | copy-done | bytes 8388632
  152.1 7.6 %operate_third.1 = (f32[16,128]{1,0:T(8,128)S(1)}, f32[256,128]{1,0:T(8,128)S(1)}, f32[4,256,128]{2,1,0:T(8,128)S(1)}, f32[4,256,128]{2,1,0:T(8,128)S(1)}) custom-call(s32[1,256]{1,0:T(1,128)S(1)} %get-tuple-element.25.pick, s32[8,128]{1,0:T(8,128)} %get-tuple-element.26.wanted, s32[8,128]{1,0:T(8,128)S(1)} %get-tuple-element.27.origin, ...), custom_call_target="tpu_custom_call" | custom-call | tf_op jit(solution)/shard_map/operate_third/pallas_call | solution.py:486
  163.5 12.9 %all_to_all.61 = f32[32,1,128]{2,1,0:T(1,128)S(1)} all-to-all(f32[32,1,128]{2,1,0:T(1,128)S(1)} %bitcast.25), channel_id=1, replica_groups=mesh['curve'=8,'band'=4] {'curve','band'}, dimensions={0} | all-to-all | bytes 32768 | tf_op jit(solution)/shard_map/all_to_all | solution.py:785
  (102 shorter events, 42.8 us)
Async XLA Ops:
  1.1 9.3 %collective-permute-start.1 = (bf16[4,256,128]{2,1,0:T(8,128)(2,1)S(1)}, bf16[4,256,128]{2,1,0:T(8,128)(2,1)S(1)}, u32[]{:S(2)}, u32[]{:S(2)}) collective-permute-start(bf16[4,256,128]{2,1,0:T(8,128)(2,1)S(1)} %convert_element_type.3.refs_0_), channel_id=1, source_target_pairs={{0,2},{1,3},{2,0},{3,1},{4,6},{5,7},{6,4},{7,5},{8,10},{9,11},{10,... | collective-permute-start | bytes 786440 | tf_op jit(solution)/shard_map/ppermute | solution.py:741
  4.1 13.9 %collective-permute-start = (bf16[4,256,128]{2,1,0:T(8,128)(2,1)S(1)}, bf16[4,256,128]{2,1,0:T(8,128)(2,1)S(1)}, u32[]{:S(2)}, u32[]{:S(2)}) collective-permute-start(bf16[4,256,128]{2,1,0:T(8,128)(2,1)S(1)} %convert_element_type.3.refs_0_), channel_id=1, source_target_pairs={{0,1},{1,0},{2,3},{3,2},{4,5},{5,4},{6,7},{7,6},{8,9},{9,8},{10,11... | collective-permute-start | bytes 786440 | tf_op jit(solution)/shard_map/ppermute | solution.py:741
  10.4 7.6 %collective-permute-start.2 = (bf16[4,256,128]{2,1,0:T(8,128)(2,1)S(1)}, bf16[4,256,128]{2,1,0:T(8,128)(2,1)S(1)}, u32[]{:S(2)}, u32[]{:S(2)}) collective-permute-start(bf16[4,256,128]{2,1,0:T(8,128)(2,1)S(1)} %collective-permute-done.1.refs_2_), channel_id=1, source_target_pairs={{0,1},{1,0},{2,3},{3,2},{4,5},{5,4},{6,7},{7,6},{8,9},{9,8},{10,11... | collective-permute-start | bytes 786440 | tf_op jit(solution)/shard_map/ppermute | solution.py:741
  11.9 15.2 %all-to-all-start = ((s32[8,1,128]{2,1,0:T(1,128)}), s32[8,1,128]{2,1,0:T(1,128)S(1)}, u32[]{:S(2)}, u32[]{:S(2)}) async-start(s32[8,1,128]{2,1,0:T(1,128)} %bitcast.2), calls=%async_computation | async-start | bytes 8192 | tf_op jit(solution)/shard_map/all_to_all | solution.py:745
  21.4 14.5 %copy-start.4 = (bf16[64,128,128]{2,1,0:T(8,128)(2,1)S(1)}, bf16[64,128,128]{2,1,0:T(8,128)(2,1)}, u32[]{:S(2)}) copy-start(bf16[64,128,128]{2,1,0:T(8,128)(2,1)} %refs_10_.1) | copy-start | bytes 6291460
  27.2 8.7 %copy-start.19 = (f32[4,256,128]{2,1,0:T(8,128)S(1)}, f32[4,256,128]{2,1,0:T(8,128)}, u32[]{:S(2)}) copy-start(f32[4,256,128]{2,1,0:T(8,128)} %state.3) | copy-start | bytes 1572868
  29.9 22.1 %all-to-all-start.1 = ((bf16[8,96,128]{2,1,0:T(8,128)(2,1)}), bf16[8,96,128]{2,1,0:T(8,128)(2,1)S(1)}, u32[]{:S(2)}, u32[]{:S(2)}) async-start(bf16[8,96,128]{2,1,0:T(8,128)(2,1)} %bitcast.4), calls=%async_computation.1 | async-start | bytes 393216 | tf_op jit(solution)/shard_map/all_to_all | solution.py:745
  57.2 6.5 %collective-permute-start.5 = (f32[1024,128]{1,0:T(8,128)}, f32[1024,128]{1,0:T(8,128)}, u32[]{:S(2)}, u32[]{:S(2)}) collective-permute-start(f32[1024,128]{1,0:T(8,128)} %get-tuple-element.35), channel_id=1, source_target_pairs={{0,1},{1,0},{2,3},{3,2},{4,5},{5,4},{6,7},{7,6},{8,9},{9,8},{10,11... | collective-permute-start | bytes 1572872 | tf_op jit(solution)/shard_map/ppermute | solution.py:741
  57.2 9.7 %collective-permute-start.3 = (f32[1024,128]{1,0:T(8,128)}, f32[1024,128]{1,0:T(8,128)}, u32[]{:S(2)}, u32[]{:S(2)}) collective-permute-start(f32[1024,128]{1,0:T(8,128)} %get-tuple-element.33), channel_id=1, source_target_pairs={{0,1},{1,0},{2,3},{3,2},{4,5},{5,4},{6,7},{7,6},{8,9},{9,8},{10,11... | collective-permute-start | bytes 1572872 | tf_op jit(solution)/shard_map/ppermute | solution.py:741
  57.7 26.7 %all-to-all-start.3 = ((bf16[16,128,128]{2,1,0:T(8,128)(2,1)}), bf16[16,128,128]{2,1,0:T(8,128)(2,1)}, u32[]{:S(2)}, u32[]{:S(2)}) async-start(bf16[16,128,128]{2,1,0:T(8,128)(2,1)} %get-tuple-element.31.own.refs_8_), calls=%async_computation.3 | async-start | bytes 1048576 | tf_op jit(solution)/shard_map/all_to_all | solution.py:745
  65.3 9.3 %collective-permute-start.6 = (s16[1040,128]{1,0:T(8,128)(2,1)S(1)}, s16[1040,128]{1,0:T(8,128)(2,1)S(1)}, u32[]{:S(2)}, u32[]{:S(2)}) collective-permute-start(s16[1040,128]{1,0:T(8,128)(2,1)S(1)} %encode.5.refs_0_), channel_id=1, source_target_pairs={{0,2},{1,3},{2,0},{3,1},{4,6},{5,7},{6,4},{7,5},{8,10},{9,11},{10,... | collective-permute-start | bytes 798728 | tf_op jit(solution)/shard_map/ppermute | solution.py:741
  68.5 10.6 %collective-permute-start.4 = (s16[1040,128]{1,0:T(8,128)(2,1)S(1)}, s16[1040,128]{1,0:T(8,128)(2,1)S(1)}, u32[]{:S(2)}, u32[]{:S(2)}) collective-permute-start(s16[1040,128]{1,0:T(8,128)(2,1)S(1)} %encode.4.refs_0_), channel_id=1, source_target_pairs={{0,2},{1,3},{2,0},{3,1},{4,6},{5,7},{6,4},{7,5},{8,10},{9,11},{10,... | collective-permute-start | bytes 798728 | tf_op jit(solution)/shard_map/ppermute | solution.py:741
  75.1 4.5 %collective-permute-start.8 = (f32[1040,128]{1,0:T(8,128)S(1)}, f32[1040,128]{1,0:T(8,128)S(1)}, u32[]{:S(2)}, u32[]{:S(2)}) collective-permute-start(f32[1040,128]{1,0:T(8,128)S(1)} %decode.5.refs_1_.refs_2_), channel_id=1, source_target_pairs={{0,1},{1,0},{2,3},{3,2},{4,5},{5,4},{6,7},{7,6},{8,9},{9,8},{10,11... | collective-permute-start | bytes 1597448 | tf_op jit(solution)/shard_map/ppermute | solution.py:741
  79.5 2.0 %collective-permute-start.7 = (f32[1040,128]{1,0:T(8,128)S(1)}, f32[1040,128]{1,0:T(8,128)S(1)}, u32[]{:S(2)}, u32[]{:S(2)}) collective-permute-start(f32[1040,128]{1,0:T(8,128)S(1)} %decode.4.refs_0_.refs_2_), channel_id=1, source_target_pairs={{0,1},{1,0},{2,3},{3,2},{4,5},{5,4},{6,7},{7,6},{8,9},{9,8},{10,11... | collective-permute-start | bytes 1597448 | tf_op jit(solution)/shard_map/ppermute | solution.py:741
  118.3 2.0 %collective-permute-start.11 = (f32[1024,128]{1,0:T(8,128)S(1)}, f32[1024,128]{1,0:T(8,128)S(1)}, u32[]{:S(2)}, u32[]{:S(2)}) collective-permute-start(f32[1024,128]{1,0:T(8,128)S(1)} %get-tuple-element.39), channel_id=1, source_target_pairs={{0,1},{1,0},{2,3},{3,2},{4,5},{5,4},{6,7},{7,6},{8,9},{9,8},{10,11... | collective-permute-start | bytes 1572872 | tf_op jit(solution)/shard_map/ppermute | solution.py:741
  118.4 4.0 %collective-permute-start.9 = (f32[1024,128]{1,0:T(8,128)S(1)}, f32[1024,128]{1,0:T(8,128)S(1)}, u32[]{:S(2)}, u32[]{:S(2)}) collective-permute-start(f32[1024,128]{1,0:T(8,128)S(1)} %get-tuple-element.37), channel_id=1, source_target_pairs={{0,1},{1,0},{2,3},{3,2},{4,5},{5,4},{6,7},{7,6},{8,9},{9,8},{10,11... | collective-permute-start | bytes 1572872 | tf_op jit(solution)/shard_map/ppermute | solution.py:741
  120.9 9.3 %collective-permute-start.12 = (s16[1040,128]{1,0:T(8,128)(2,1)S(1)}, s16[1040,128]{1,0:T(8,128)(2,1)S(1)}, u32[]{:S(2)}, u32[]{:S(2)}) collective-permute-start(s16[1040,128]{1,0:T(8,128)(2,1)S(1)} %encode.7.refs_0_), channel_id=1, source_target_pairs={{0,2},{1,3},{2,0},{3,1},{4,6},{5,7},{6,4},{7,5},{8,10},{9,11},{10,... | collective-permute-start | bytes 798728 | tf_op jit(solution)/shard_map/ppermute | solution.py:741
  123.0 12.1 %collective-permute-start.10 = (s16[1040,128]{1,0:T(8,128)(2,1)S(1)}, s16[1040,128]{1,0:T(8,128)(2,1)S(1)}, u32[]{:S(2)}, u32[]{:S(2)}) collective-permute-start(s16[1040,128]{1,0:T(8,128)(2,1)S(1)} %encode.6.refs_0_), channel_id=1, source_target_pairs={{0,2},{1,3},{2,0},{3,1},{4,6},{5,7},{6,4},{7,5},{8,10},{9,11},{10,... | collective-permute-start | bytes 798728 | tf_op jit(solution)/shard_map/ppermute | solution.py:741
  130.7 6.9 %copy-start.5 = (f32[1056,128]{1,0:T(8,128)}, f32[1056,128]{1,0:T(8,128)S(1)}, u32[]{:S(2)}) copy-start(f32[1056,128]{1,0:T(8,128)S(1)} %decode.7.refs_5_.refs_1_) | copy-start | bytes 1622020
  130.7 5.0 %collective-permute-start.14 = (f32[1056,128]{1,0:T(8,128)S(1)}, f32[1056,128]{1,0:T(8,128)S(1)}, u32[]{:S(2)}, u32[]{:S(2)}) collective-permute-start(f32[1056,128]{1,0:T(8,128)S(1)} %decode.7.refs_5_.refs_1_), channel_id=1, source_target_pairs={{0,1},{1,0},{2,3},{3,2},{4,5},{5,4},{6,7},{7,6},{8,9},{9,8},{10,11... | collective-permute-start | bytes 1622024 | tf_op jit(solution)/shard_map/ppermute | solution.py:741
  135.5 3.5 %copy-start.8 = (f32[1056,128]{1,0:T(8,128)}, f32[1056,128]{1,0:T(8,128)S(1)}, u32[]{:S(2)}) copy-start(f32[1056,128]{1,0:T(8,128)S(1)} %decode.6.refs_4_.refs_0_) | copy-start | bytes 1622020
  135.5 2.0 %collective-permute-start.13 = (f32[1056,128]{1,0:T(8,128)S(1)}, f32[1056,128]{1,0:T(8,128)S(1)}, u32[]{:S(2)}, u32[]{:S(2)}) collective-permute-start(f32[1056,128]{1,0:T(8,128)S(1)} %decode.6.refs_4_.refs_0_), channel_id=1, source_target_pairs={{0,1},{1,0},{2,3},{3,2},{4,5},{5,4},{6,7},{7,6},{8,9},{9,8},{10,11... | collective-permute-start | bytes 1622024 | tf_op jit(solution)/shard_map/ppermute | solution.py:741
  135.6 3.4 %copy-start.24 = (f32[1056,128]{1,0:T(8,128)}, f32[1056,128]{1,0:T(8,128)S(1)}, u32[]{:S(2)}) copy-start(f32[1056,128]{1,0:T(8,128)S(1)} %collective-permute-done.14.refs_7_.refs_3_) | copy-start | bytes 1622020
  139.1 22.2 %all-to-all-start.4 = ((bf16[8,32,128]{2,1,0:T(8,128)(2,1)}), bf16[8,32,128]{2,1,0:T(8,128)(2,1)S(1)}, u32[]{:S(2)}, u32[]{:S(2)}) async-start(bf16[8,32,128]{2,1,0:T(8,128)(2,1)} %bitcast.8), calls=%async_computation.4 | async-start | bytes 131072 | tf_op jit(solution)/shard_map/all_to_all | solution.py:745
  (28 other events, 39.0 us)

commit v3 on v2

--- a/solution.py
+++ b/solution.py
@@ -40,11 +40,15 @@
 
 
 def anywhere():
-    return pl.BlockSpec(memory_space=pl.ANY)
+    return pl.BlockSpec(memory_space=pltpu.HBM)
 
 
 def params(mebibytes):
     return pltpu.CompilerParams(vmem_limit_bytes=mebibytes * 1024 * 1024)
+
+
+def in_hbm(array):
+    return pltpu.with_memory_space_constraint(array, pltpu.HBM)
 
 
 def shaped(shape, dtype):
@@ -173,7 +177,7 @@
     return pl.pallas_call(
         functools.partial(spread_kernel, rows, vectors, groups, width),
         out_shape=[
-            shaped(((rows + 1) * vectors, node), bf16),
+            pltpu.HBM(((rows + 1) * vectors, node), bf16),
             shaped((slots, node, node), bf16),
             shaped((slots * 2 * vectors, node), bf16),
         ],
@@ -206,7 +210,7 @@
         out_specs=vmem(),
         compiler_params=params(16),
         name="reply",
-    )(asked, field, split)
+    )(asked, in_hbm(field), split)
 
 
 class Stream:
@@ -300,9 +304,9 @@
         in_specs=[smem()] * 2 + [vmem()] * 2 + [anywhere()] * 2,
         out_specs=vmem(),
         scratch_shapes=stream_scratch(blocks, diag),
-        compiler_params=params(24),
+        compiler_params=params(20),
         name="operate_local",
-    )(pick, target, field, state, blocks, diag)
+    )(pick, target, in_hbm(field), state, blocks, diag)
 
 
 def settle_kernel(rows, vectors, groups, wanted, origin, asked, local, halo, own, *refs):
@@ -341,7 +345,7 @@
         in_specs=[smem()] * 3 + [vmem()] * 3,
         out_specs=[vmem()] * (2 * CHUNKS),
         scratch_shapes=[pltpu.VMEM(local.shape, f32)],
-        compiler_params=params(24),
+        compiler_params=params(20),
         name="settle",
     )(wanted, origin, asked, local, halo, own)
     return outs[:CHUNKS], outs[CHUNKS:]
@@ -417,7 +421,7 @@
             pltpu.VMEM(((rows + 1) * vectors, node), f32),
         ]
         + stream_scratch(blocks, diag),
-        compiler_params=params(32),
+        compiler_params=params(22),
         name="operate_second",
     )(pick, target, asked, *arrays, halo, arrived, blocks, diag)
     return outs[:CHUNKS], outs[CHUNKS : 2 * CHUNKS], outs[-1]
@@ -482,16 +486,16 @@
 def operate_third(pick, wanted, origin, drive, image, own, blocks, diag, width, vectors):
     rows, node = blocks.shape[0], blocks.shape[-1]
     groups = lax.axis_size("curve")
-    mine = shaped((width, rows, node), f32)
+    mine = pltpu.HBM((width, rows, node), f32)
     return pl.pallas_call(
         functools.partial(third_kernel, rows, vectors, groups, width),
         out_shape=[shaped((vectors, node), f32), shaped((groups * CAP * vectors, node), f32), mine, mine],
         in_specs=[smem()] * 3 + [vmem()] * (4 * CHUNKS + 1) + [anywhere()] * 2,
         out_specs=[vmem()] * 4,
         scratch_shapes=[pltpu.VMEM(((rows + 1) * vectors, node), bf16)] + stream_scratch(blocks, diag),
-        compiler_params=params(32),
+        compiler_params=params(22),
         name="operate_third",
-    )(pick, wanted, origin, *drive, *image, own, blocks, diag)
+    )(pick, wanted, origin, *drive, *image[:CHUNKS], *map(in_hbm, image[CHUNKS:]), own, blocks, diag)
 
 
 def tail_kernel(each, vectors, form, left, halo, *refs):
@@ -733,7 +737,7 @@
         scratch_shapes=[pltpu.VMEM(scale.shape, f32)] * 4,
         compiler_params=params(16),
         name="finish",
-    )(shares, scale, state, drive, image)
+    )(shares, scale, state, in_hbm(drive), in_hbm(image))
 
 
 def swap(array, bit):
@@ -762,7 +766,10 @@
     devices = groups * lax.axis_size("band")
     width, rows = state.shape[:2]
     vectors = width * lax.axis_size("band")
+    blocks = in_hbm(blocks)
+    diag_blocks = in_hbm(diag_blocks)
     rounded = state.astype(bf16)
+    state = in_hbm(state)
     across = swap(rounded, 2)
     parts = [rounded, swap(rounded, 1), across, swap(across, 1)]
     pick, target, wanted, origin = plan(block_cols.reshape(1, rows))

time: 182 us -> 147 us (0.81)
  local copies, waits for them, and re-layouts: 37.4 us -> 1.5 us
  waiting for transfers between devices: 32 us -> 35.2 us
  starting transfers between devices: 30.1 us -> 28 us
    unnamed x66 -> x6, local copies, waits for them, and re-layouts: 37.4 us -> 1.5 us
    all_to_all x4, waiting for transfers between devices: 0.01 us -> 2.12 us  [exchange(): lax.all_to_all(array, 'curve', split_axis=0, concat_axis=0, tiled=True)]
    all_to_all x4, starting transfers between devices: 21.4 us -> 19.3 us  [exchange(): lax.all_to_all(array, 'curve', split_axis=0, concat_axis=0, tiled=True)]
    pallas_call x4, Pallas kernels: 4.26 us -> 2.2 us  [encode(): pl.pallas_call(functools.partial(encode_kernel, each, vectors), out_shape...]
  transfers between devices with their start and end apart: 19 -> 19, of which waited for: 8 -> 9; matrix products, arithmetic and copies ran while one was open for 0% -> 0% of each run, Pallas kernels for 17% -> 21%
where the time goes in v3:
time: 147 us
  Pallas kernels  51.5 us (35%)
  waiting for transfers between devices  35.2 us (24%)
  blocking collectives  29 us (20%)
  starting transfers between devices  28 us (19%)
  local copies, waits for them, and re-layouts  1.5 us (1%)
    ppermute x15, waiting for transfers between devices, swap(): return lax.ppermute(array, 'band', [(k, k ^ bit) for k in range(size)])  33 us
    all_to_all x4, starting transfers between devices, exchange(): lax.all_to_all(array, 'curve', split_axis=0, concat_axis=0, tiled=True)  19.3 us
    all_to_all x1, blocking collectives, exchange(): lax.all_to_all(array, 'curve', split_axis=0, concat_axis=0, tiled=True)  16.2 us
    all_to_all x1, blocking collectives, body(): lax.all_to_all(share, ('curve', 'band'), split_axis=0, concat_axis=0, til...  12.9 us
    pallas_call x1, Pallas kernels, operate_second(): pl.pallas_call(functools.partial(second_kernel, rows, vectors, groups), o...  11.7 us
    pallas_call x1, Pallas kernels, operate_local(): pl.pallas_call(functools.partial(local_kernel, rows, vectors), out_shape=...  11.2 us
    ppermute x15, starting transfers between devices, swap(): return lax.ppermute(array, 'band', [(k, k ^ bit) for k in range(size)])  8.71 us
    pallas_call x1, Pallas kernels, operate_third(): pl.pallas_call(functools.partial(third_kernel, rows, vectors, groups, wid...  8.46 us
  transfers between devices with their start and end apart: 19, of which 9 were waited for; matrix products, arithmetic and copies ran while one was open for 0% of the time, Pallas kernels for 21%

profile of v3, /device:TPU:0, one launch (start us, length us, event | category | flops | bytes accessed | tf_op | source)
XLA Modules:
  0.0 146.5 jit_solution(5063820006437072449)
XLA Ops:
  1.1 3.0 %collective-permute-start.1 = (bf16[4,256,128]{2,1,0:T(8,128)(2,1)S(1)}, bf16[4,256,128]{2,1,0:T(8,128)(2,1)S(1)}, u32[]{:S(2)}, u32[]{:S(2)}) collective-permute-start(bf16[4,256,128]{2,1,0:T(8,128)(2,1)S(1)} %convert_element_type.3.refs_0_), channel_id=1, source_target_pairs={{0,2},{1,3},{2,0},{3,1},{4,6},{5,7},{6,4},{7,5},{8,10},{9,11},{10,... | collective-permute-start | bytes 786440 | tf_op jit(solution)/shard_map/ppermute | solution.py:745
  4.1 6.3 %collective-permute-done.1.refs_2_ = bf16[4,256,128]{2,1,0:T(8,128)(2,1)S(1)} collective-permute-done((bf16[4,256,128]{2,1,0:T(8,128)(2,1)S(1)}, bf16[4,256,128]{2,1,0:T(8,128)(2,1)S(1)}, u32[]{:S(2)}, u32[]{:S(2)}) %collective-permute-start.1) | collective-permute-done | bytes 262176 | tf_op jit(solution)/shard_map/ppermute | solution.py:745
  11.9 6.1 %all-to-all-start = ((s32[8,1,128]{2,1,0:T(1,128)}), s32[8,1,128]{2,1,0:T(1,128)S(1)}, u32[]{:S(2)}, u32[]{:S(2)}) async-start(s32[8,1,128]{2,1,0:T(1,128)} %bitcast.2), calls=%async_computation | async-start | bytes 8192 | tf_op jit(solution)/shard_map/all_to_all | solution.py:749
  18.0 4.4 %spread.1 = (bf16[4112,128]{1,0:T(8,128)(2,1)}, bf16[16,128,128]{2,1,0:T(8,128)(2,1)}, bf16[512,128]{1,0:T(8,128)(2,1)S(1)}) custom-call(s32[8,128]{1,0:T(8,128)S(1)} %get-tuple-element.27.origin, bf16[256,1,128,128]{3,2,1,0:T(8,128)(2,1)} %refs_9_.1, bf16[4,256,128]{2,1,0:T(8,128)(2,1)S(1)} %convert_element_type.3.refs_0_, ...), custom_call_target="tpu_custom_call" | custom-call | tf_op jit(solution)/shard_map/spread/pallas_call | solution.py:177
  22.4 2.1 %all-to-all-done = s32[8,1,128]{2,1,0:T(1,128)S(1)} async-done(((s32[8,1,128]{2,1,0:T(1,128)}), s32[8,1,128]{2,1,0:T(1,128)S(1)}, u32[]{:S(2)}, u32[]{:S(2)}) %all-to-all-start) | async-done | bytes 4128 | tf_op jit(solution)/shard_map/all_to_all | solution.py:749
  24.5 2.1 %reply.1 = bf16[768,128]{1,0:T(8,128)(2,1)} custom-call(s32[8,128]{1,0:T(8,128)S(1)} %bitcast.19, bf16[4112,128]{1,0:T(8,128)(2,1)} %get-tuple-element.29.field, bf16[512,128]{1,0:T(8,128)(2,1)S(1)} %get-tuple-element.30.split), custom_call_target="tpu_custom_call" | custom-call | tf_op jit(solution)/shard_map/reply/pallas_call | solution.py:206
  26.6 3.9 %all-to-all-start.1 = ((bf16[8,96,128]{2,1,0:T(8,128)(2,1)}), bf16[8,96,128]{2,1,0:T(8,128)(2,1)S(1)}, u32[]{:S(2)}, u32[]{:S(2)}) async-start(bf16[8,96,128]{2,1,0:T(8,128)(2,1)} %bitcast.4), calls=%async_computation.1 | async-start | bytes 393216 | tf_op jit(solution)/shard_map/all_to_all | solution.py:749
  30.5 11.2 %operate_local.1.local = f32[4112,128]{1,0:T(8,128)S(1)} custom-call(s32[1,256]{1,0:T(1,128)S(1)} %get-tuple-element.25.pick, s32[1,256]{1,0:T(1,128)S(1)} %get-tuple-element.28.target, bf16[4112,128]{1,0:T(8,128)(2,1)} %get-tuple-element.29.field, f32[4,256,128]{2,1,0:T(8,128)} %state.3, bf16[256,1,128,128]{3,2,1,0:T(8,128)(2,1)} %refs_9_.1, ...), custom_call_target="tpu_custom_call" | custom-call | tf_op jit(solution)/shard_map/operate_local/pallas_call | solution.py:301
  41.7 3.6 %settle.1 = (f32[1024,128]{1,0:T(8,128)S(1)}, f32[1024,128]{1,0:T(8,128)S(1)}, f32[1024,128]{1,0:T(8,128)}, f32[1024,128]{1,0:T(8,128)}) custom-call(s32[8,128]{1,0:T(8,128)} %get-tuple-element.26.wanted, s32[8,128]{1,0:T(8,128)S(1)} %get-tuple-element.27.origin, s32[8,128]{1,0:T(8,128)S(1)} %bitcast.20, f32[4112,128]{1,0:T(8,128)S(1)} %operate_local.1.local, ...), custom_call_target="tpu_custom_call" | custom-call | tf_op jit(solution)/shard_map/settle/pallas_call | solution.py:342
  45.8 6.0 %all-to-all-start.3 = ((bf16[16,128,128]{2,1,0:T(8,128)(2,1)}), bf16[16,128,128]{2,1,0:T(8,128)(2,1)S(1)}, u32[]{:S(2)}, u32[]{:S(2)}) async-start(bf16[16,128,128]{2,1,0:T(8,128)(2,1)} %get-tuple-element.31.own.refs_8_), calls=%async_computation.3 | async-start | bytes 1048576 | tf_op jit(solution)/shard_map/all_to_all | solution.py:749
  52.4 1.5 %collective-permute-start.6 = (s16[1040,128]{1,0:T(8,128)(2,1)S(1)}, s16[1040,128]{1,0:T(8,128)(2,1)S(1)}, u32[]{:S(2)}, u32[]{:S(2)}) collective-permute-start(s16[1040,128]{1,0:T(8,128)(2,1)S(1)} %encode.5.refs_0_), channel_id=1, source_target_pairs={{0,2},{1,3},{2,0},{3,1},{4,6},{5,7},{6,4},{7,5},{8,10},{9,11},{10,... | collective-permute-start | bytes 798728 | tf_op jit(solution)/shard_map/ppermute | solution.py:745
  55.1 6.6 %collective-permute-done.6.refs_1_ = s16[1040,128]{1,0:T(8,128)(2,1)S(1)} collective-permute-done((s16[1040,128]{1,0:T(8,128)(2,1)S(1)}, s16[1040,128]{1,0:T(8,128)(2,1)S(1)}, u32[]{:S(2)}, u32[]{:S(2)}) %collective-permute-start.6) | collective-permute-done | bytes 266272 | tf_op jit(solution)/shard_map/ppermute | solution.py:745
  62.2 3.9 %collective-permute-done.4.refs_1_ = s16[1040,128]{1,0:T(8,128)(2,1)S(1)} collective-permute-done((s16[1040,128]{1,0:T(8,128)(2,1)S(1)}, s16[1040,128]{1,0:T(8,128)(2,1)S(1)}, u32[]{:S(2)}, u32[]{:S(2)}) %collective-permute-start.4) | collective-permute-done | bytes 266272 | tf_op jit(solution)/shard_map/ppermute | solution.py:745
  66.7 1.9 %collective-permute-done.7.refs_2_ = f32[1040,128]{1,0:T(8,128)S(1)} collective-permute-done((f32[1040,128]{1,0:T(8,128)S(1)}, f32[1040,128]{1,0:T(8,128)S(1)}, u32[]{:S(2)}, u32[]{:S(2)}) %collective-permute-start.7) | collective-permute-done | bytes 532512 | tf_op jit(solution)/shard_map/ppermute | solution.py:745
  69.9 16.2 %all_to_all.60 = f32[8,72,128]{2,1,0:T(8,128)S(1)} all-to-all(f32[8,72,128]{2,1,0:T(8,128)S(1)} %bitcast.15), channel_id=1, replica_groups=mesh['curve'=8,'band'=4] {'curve'}, dimensions={0} | all-to-all | bytes 589824 | tf_op jit(solution)/shard_map/all_to_all | solution.py:749
  86.0 11.7 %operate_second.1 = (f32[1024,128]{1,0:T(8,128)S(1)}, f32[1024,128]{1,0:T(8,128)S(1)}, f32[1024,128]{1,0:T(8,128)S(1)}, f32[1024,128]{1,0:T(8,128)S(1)}, f32[16,128]{1,0:T(8,128)S(1)}) custom-call(s32[1,256]{1,0:T(1,128)S(1)} %get-tuple-element.25.pick, s32[1,256]{1,0:T(1,128)S(1)} %get-tuple-element.28.target, s32[8,128]{1,0:T(8,128)S(1)} %bitcast.22, ...), custom_call_target="tpu_custom_call" | custom-call | tf_op jit(solution)/shard_map/operate_second/pallas_call | solution.py:414
  103.0 6.6 %collective-permute-done.12.refs_1_ = s16[1040,128]{1,0:T(8,128)(2,1)S(1)} collective-permute-done((s16[1040,128]{1,0:T(8,128)(2,1)S(1)}, s16[1040,128]{1,0:T(8,128)(2,1)S(1)}, u32[]{:S(2)}, u32[]{:S(2)}) %collective-permute-start.12) | collective-permute-done | bytes 266272 | tf_op jit(solution)/shard_map/ppermute | solution.py:745
  110.1 4.3 %collective-permute-done.10.refs_1_ = s16[1040,128]{1,0:T(8,128)(2,1)S(1)} collective-permute-done((s16[1040,128]{1,0:T(8,128)(2,1)S(1)}, s16[1040,128]{1,0:T(8,128)(2,1)S(1)}, u32[]{:S(2)}, u32[]{:S(2)}) %collective-permute-start.10) | collective-permute-done | bytes 266272 | tf_op jit(solution)/shard_map/ppermute | solution.py:745
  115.0 1.9 %collective-permute-done.13.refs_6_.refs_2_ = f32[1056,128]{1,0:T(8,128)S(1)} collective-permute-done((f32[1056,128]{1,0:T(8,128)S(1)}, f32[1056,128]{1,0:T(8,128)S(1)}, u32[]{:S(2)}, u32[]{:S(2)}) %collective-permute-start.13) | collective-permute-done | bytes 540704 | tf_op jit(solution)/shard_map/ppermute | solution.py:745
  116.9 1.5 %pack_rounded.1 = bf16[256,128]{1,0:T(8,128)(2,1)} custom-call(s32[8,128]{1,0:T(8,128)S(1)} %bitcast.23, f32[1056,128]{1,0:T(8,128)S(1)} %decode.6.refs_4_.refs_0_, f32[1056,128]{1,0:T(8,128)S(1)} %decode.7.refs_5_.refs_1_, f32[1056,128]{1,0:T(8,128)S(1)} %collective-permute-done.13.refs_6_.refs_2_, f32[1056,128]{1,0:T(8,128)S(1)} %collective-permute-done.14.refs_7_.refs_3_), custom_call_target="tpu_custom_call" | custom-call | tf_op jit(solution)/shard_map/pack_rounded/pallas_call | solution.py:689
  119.3 3.3 %all-to-all-start.4 = ((bf16[8,32,128]{2,1,0:T(8,128)(2,1)}), bf16[8,32,128]{2,1,0:T(8,128)(2,1)S(1)}, u32[]{:S(2)}, u32[]{:S(2)}) async-start(bf16[8,32,128]{2,1,0:T(8,128)(2,1)} %bitcast.8), calls=%async_computation.4 | async-start | bytes 131072 | tf_op jit(solution)/shard_map/all_to_all | solution.py:749
  122.6 8.5 %operate_third.1 = (f32[16,128]{1,0:T(8,128)S(1)}, f32[256,128]{1,0:T(8,128)S(1)}, f32[4,256,128]{2,1,0:T(8,128)}, f32[4,256,128]{2,1,0:T(8,128)}) custom-call(s32[1,256]{1,0:T(1,128)S(1)} %get-tuple-element.25.pick, s32[8,128]{1,0:T(8,128)} %get-tuple-element.26.wanted, s32[8,128]{1,0:T(8,128)S(1)} %get-tuple-element.27.origin, ...), custom_call_target="tpu_custom_call" | custom-call | tf_op jit(solution)/shard_map/operate_third/pallas_call | solution.py:490
  131.2 12.9 %all_to_all.61 = f32[32,1,128]{2,1,0:T(1,128)S(1)} all-to-all(f32[32,1,128]{2,1,0:T(1,128)S(1)} %bitcast.25), channel_id=1, replica_groups=mesh['curve'=8,'band'=4] {'curve','band'}, dimensions={0} | all-to-all | bytes 32768 | tf_op jit(solution)/shard_map/all_to_all | solution.py:792
  144.1 2.5 %finish.1 = f32[4,256,128]{2,1,0:T(8,128)} custom-call(f32[32,128]{1,0:T(8,128)S(1)} %bitcast.24, f32[16,128]{1,0:T(8,128)S(1)} %get-tuple-element.42.scale, f32[4,256,128]{2,1,0:T(8,128)} %state.3, f32[4,256,128]{2,1,0:T(8,128)} %get-tuple-element.43.drive, f32[4,256,128]{2,1,0:T(8,128)} %get-tuple-element.44.image), custom_call_target="tpu_custom_call" | custom-call | tf_op jit(solution)/shard_map/finish/pallas_call | solution.py:732
  (42 shorter events, 14.3 us)
Async XLA Ops:
  1.1 9.3 %collective-permute-start.1 = (bf16[4,256,128]{2,1,0:T(8,128)(2,1)S(1)}, bf16[4,256,128]{2,1,0:T(8,128)(2,1)S(1)}, u32[]{:S(2)}, u32[]{:S(2)}) collective-permute-start(bf16[4,256,128]{2,1,0:T(8,128)(2,1)S(1)} %convert_element_type.3.refs_0_), channel_id=1, source_target_pairs={{0,2},{1,3},{2,0},{3,1},{4,6},{5,7},{6,4},{7,5},{8,10},{9,11},{10,... | collective-permute-start | bytes 786440 | tf_op jit(solution)/shard_map/ppermute | solution.py:745
  4.1 13.9 %collective-permute-start = (bf16[4,256,128]{2,1,0:T(8,128)(2,1)S(1)}, bf16[4,256,128]{2,1,0:T(8,128)(2,1)S(1)}, u32[]{:S(2)}, u32[]{:S(2)}) collective-permute-start(bf16[4,256,128]{2,1,0:T(8,128)(2,1)S(1)} %convert_element_type.3.refs_0_), channel_id=1, source_target_pairs={{0,1},{1,0},{2,3},{3,2},{4,5},{5,4},{6,7},{7,6},{8,9},{9,8},{10,11... | collective-permute-start | bytes 786440 | tf_op jit(solution)/shard_map/ppermute | solution.py:745
  10.4 7.6 %collective-permute-start.2 = (bf16[4,256,128]{2,1,0:T(8,128)(2,1)S(1)}, bf16[4,256,128]{2,1,0:T(8,128)(2,1)S(1)}, u32[]{:S(2)}, u32[]{:S(2)}) collective-permute-start(bf16[4,256,128]{2,1,0:T(8,128)(2,1)S(1)} %collective-permute-done.1.refs_2_), channel_id=1, source_target_pairs={{0,1},{1,0},{2,3},{3,2},{4,5},{5,4},{6,7},{7,6},{8,9},{9,8},{10,11... | collective-permute-start | bytes 786440 | tf_op jit(solution)/shard_map/ppermute | solution.py:745
  10.4 0.7 copy-start.2
  11.9 12.6 %all-to-all-start = ((s32[8,1,128]{2,1,0:T(1,128)}), s32[8,1,128]{2,1,0:T(1,128)S(1)}, u32[]{:S(2)}, u32[]{:S(2)}) async-start(s32[8,1,128]{2,1,0:T(1,128)} %bitcast.2), calls=%async_computation | async-start | bytes 8192 | tf_op jit(solution)/shard_map/all_to_all | solution.py:749
  26.6 15.1 %all-to-all-start.1 = ((bf16[8,96,128]{2,1,0:T(8,128)(2,1)}), bf16[8,96,128]{2,1,0:T(8,128)(2,1)S(1)}, u32[]{:S(2)}, u32[]{:S(2)}) async-start(bf16[8,96,128]{2,1,0:T(8,128)(2,1)} %bitcast.4), calls=%async_computation.1 | async-start | bytes 393216 | tf_op jit(solution)/shard_map/all_to_all | solution.py:749
  45.3 6.5 %collective-permute-start.5 = (f32[1024,128]{1,0:T(8,128)}, f32[1024,128]{1,0:T(8,128)S(1)}, u32[]{:S(2)}, u32[]{:S(2)}) collective-permute-start(f32[1024,128]{1,0:T(8,128)} %get-tuple-element.35), channel_id=1, source_target_pairs={{0,1},{1,0},{2,3},{3,2},{4,5},{5,4},{6,7},{7,6},{8,9},{9,8},{10,11... | collective-permute-start | bytes 1572872 | tf_op jit(solution)/shard_map/ppermute | solution.py:745
  45.3 8.6 %collective-permute-start.3 = (f32[1024,128]{1,0:T(8,128)}, f32[1024,128]{1,0:T(8,128)S(1)}, u32[]{:S(2)}, u32[]{:S(2)}) collective-permute-start(f32[1024,128]{1,0:T(8,128)} %get-tuple-element.33), channel_id=1, source_target_pairs={{0,1},{1,0},{2,3},{3,2},{4,5},{5,4},{6,7},{7,6},{8,9},{9,8},{10,11... | collective-permute-start | bytes 1572872 | tf_op jit(solution)/shard_map/ppermute | solution.py:745
  45.8 24.1 %all-to-all-start.3 = ((bf16[16,128,128]{2,1,0:T(8,128)(2,1)}), bf16[16,128,128]{2,1,0:T(8,128)(2,1)S(1)}, u32[]{:S(2)}, u32[]{:S(2)}) async-start(bf16[16,128,128]{2,1,0:T(8,128)(2,1)} %get-tuple-element.31.own.refs_8_), calls=%async_computation.3 | async-start | bytes 1048576 | tf_op jit(solution)/shard_map/all_to_all | solution.py:749
  52.4 9.3 %collective-permute-start.6 = (s16[1040,128]{1,0:T(8,128)(2,1)S(1)}, s16[1040,128]{1,0:T(8,128)(2,1)S(1)}, u32[]{:S(2)}, u32[]{:S(2)}) collective-permute-start(s16[1040,128]{1,0:T(8,128)(2,1)S(1)} %encode.5.refs_0_), channel_id=1, source_target_pairs={{0,2},{1,3},{2,0},{3,1},{4,6},{5,7},{6,4},{7,5},{8,10},{9,11},{10,... | collective-permute-start | bytes 798728 | tf_op jit(solution)/shard_map/ppermute | solution.py:745
  54.5 11.7 %collective-permute-start.4 = (s16[1040,128]{1,0:T(8,128)(2,1)S(1)}, s16[1040,128]{1,0:T(8,128)(2,1)S(1)}, u32[]{:S(2)}, u32[]{:S(2)}) collective-permute-start(s16[1040,128]{1,0:T(8,128)(2,1)S(1)} %encode.4.refs_0_), channel_id=1, source_target_pairs={{0,2},{1,3},{2,0},{3,1},{4,6},{5,7},{6,4},{7,5},{8,10},{9,11},{10,... | collective-permute-start | bytes 798728 | tf_op jit(solution)/shard_map/ppermute | solution.py:745
  62.2 4.5 %collective-permute-start.8 = (f32[1040,128]{1,0:T(8,128)S(1)}, f32[1040,128]{1,0:T(8,128)S(1)}, u32[]{:S(2)}, u32[]{:S(2)}) collective-permute-start(f32[1040,128]{1,0:T(8,128)S(1)} %decode.5.refs_1_.refs_2_), channel_id=1, source_target_pairs={{0,1},{1,0},{2,3},{3,2},{4,5},{5,4},{6,7},{7,6},{8,9},{9,8},{10,11... | collective-permute-start | bytes 1597448 | tf_op jit(solution)/shard_map/ppermute | solution.py:745
  66.6 2.0 %collective-permute-start.7 = (f32[1040,128]{1,0:T(8,128)S(1)}, f32[1040,128]{1,0:T(8,128)S(1)}, u32[]{:S(2)}, u32[]{:S(2)}) collective-permute-start(f32[1040,128]{1,0:T(8,128)S(1)} %decode.4.refs_0_.refs_2_), channel_id=1, source_target_pairs={{0,1},{1,0},{2,3},{3,2},{4,5},{5,4},{6,7},{7,6},{8,9},{9,8},{10,11... | collective-permute-start | bytes 1597448 | tf_op jit(solution)/shard_map/ppermute | solution.py:745
  97.7 2.0 %collective-permute-start.11 = (f32[1024,128]{1,0:T(8,128)S(1)}, f32[1024,128]{1,0:T(8,128)S(1)}, u32[]{:S(2)}, u32[]{:S(2)}) collective-permute-start(f32[1024,128]{1,0:T(8,128)S(1)} %get-tuple-element.39), channel_id=1, source_target_pairs={{0,1},{1,0},{2,3},{3,2},{4,5},{5,4},{6,7},{7,6},{8,9},{9,8},{10,11... | collective-permute-start | bytes 1572872 | tf_op jit(solution)/shard_map/ppermute | solution.py:745
  97.8 4.0 %collective-permute-start.9 = (f32[1024,128]{1,0:T(8,128)S(1)}, f32[1024,128]{1,0:T(8,128)S(1)}, u32[]{:S(2)}, u32[]{:S(2)}) collective-permute-start(f32[1024,128]{1,0:T(8,128)S(1)} %get-tuple-element.37), channel_id=1, source_target_pairs={{0,1},{1,0},{2,3},{3,2},{4,5},{5,4},{6,7},{7,6},{8,9},{9,8},{10,11... | collective-permute-start | bytes 1572872 | tf_op jit(solution)/shard_map/ppermute | solution.py:745
  100.3 9.3 %collective-permute-start.12 = (s16[1040,128]{1,0:T(8,128)(2,1)S(1)}, s16[1040,128]{1,0:T(8,128)(2,1)S(1)}, u32[]{:S(2)}, u32[]{:S(2)}) collective-permute-start(s16[1040,128]{1,0:T(8,128)(2,1)S(1)} %encode.7.refs_0_), channel_id=1, source_target_pairs={{0,2},{1,3},{2,0},{3,1},{4,6},{5,7},{6,4},{7,5},{8,10},{9,11},{10,... | collective-permute-start | bytes 798728 | tf_op jit(solution)/shard_map/ppermute | solution.py:745
  102.3 12.1 %collective-permute-start.10 = (s16[1040,128]{1,0:T(8,128)(2,1)S(1)}, s16[1040,128]{1,0:T(8,128)(2,1)S(1)}, u32[]{:S(2)}, u32[]{:S(2)}) collective-permute-start(s16[1040,128]{1,0:T(8,128)(2,1)S(1)} %encode.6.refs_0_), channel_id=1, source_target_pairs={{0,2},{1,3},{2,0},{3,1},{4,6},{5,7},{6,4},{7,5},{8,10},{9,11},{10,... | collective-permute-start | bytes 798728 | tf_op jit(solution)/shard_map/ppermute | solution.py:745
  110.0 5.0 %collective-permute-start.14 = (f32[1056,128]{1,0:T(8,128)S(1)}, f32[1056,128]{1,0:T(8,128)S(1)}, u32[]{:S(2)}, u32[]{:S(2)}) collective-permute-start(f32[1056,128]{1,0:T(8,128)S(1)} %decode.7.refs_5_.refs_1_), channel_id=1, source_target_pairs={{0,1},{1,0},{2,3},{3,2},{4,5},{5,4},{6,7},{7,6},{8,9},{9,8},{10,11... | collective-permute-start | bytes 1622024 | tf_op jit(solution)/shard_map/ppermute | solution.py:745
  114.9 2.0 %collective-permute-start.13 = (f32[1056,128]{1,0:T(8,128)S(1)}, f32[1056,128]{1,0:T(8,128)S(1)}, u32[]{:S(2)}, u32[]{:S(2)}) collective-permute-start(f32[1056,128]{1,0:T(8,128)S(1)} %decode.6.refs_4_.refs_0_), channel_id=1, source_target_pairs={{0,1},{1,0},{2,3},{3,2},{4,5},{5,4},{6,7},{7,6},{8,9},{9,8},{10,11... | collective-permute-start | bytes 1622024 | tf_op jit(solution)/shard_map/ppermute | solution.py:745
  116.9 1.5 %copy-start.1 = (f32[1056,128]{1,0:T(8,128)}, f32[1056,128]{1,0:T(8,128)S(1)}, u32[]{:S(2)}) copy-start(f32[1056,128]{1,0:T(8,128)S(1)} %collective-permute-done.13.refs_6_.refs_2_) | copy-start | bytes 1622020
  118.4 0.8 copy-start
  119.3 11.8 %all-to-all-start.4 = ((bf16[8,32,128]{2,1,0:T(8,128)(2,1)}), bf16[8,32,128]{2,1,0:T(8,128)(2,1)S(1)}, u32[]{:S(2)}, u32[]{:S(2)}) async-start(bf16[8,32,128]{2,1,0:T(8,128)(2,1)} %bitcast.8), calls=%async_computation.4 | async-start | bytes 131072 | tf_op jit(solution)/shard_map/all_to_all | solution.py:749

commit v4 on v3

--- a/solution.py
+++ b/solution.py
@@ -7,6 +7,7 @@
 from jax.experimental.pallas import tpu as pltpu
 from jax.sharding import PartitionSpec as P
 
+
 CAP = 2
 TAYLOR = 16
 UNROLL = 32
@@ -61,6 +62,22 @@
 
 def times_transposed(field, block):
     return lax.dot_general(field, block, (((1,), (1,)), ((), ())), preferred_element_type=f32)
+
+
+def two(one, other):
+    nothing = jnp.zeros_like(one)
+    upper = jnp.concatenate([one, nothing], axis=1)
+    return jnp.concatenate([upper, jnp.concatenate([nothing, other], axis=1)], axis=0)
+
+
+def times_two(one, other, blocks):
+    value = times(two(one, other), blocks.reshape(-1, blocks.shape[-1]))
+    return value[: one.shape[0]], value[one.shape[0] :]
+
+
+def times_two_transposed(one, other, first, second):
+    value = times(two(one, other), jnp.concatenate([first.T, second.T], axis=0))
+    return value[: one.shape[0]], value[one.shape[0] :]
 
 
 def row_sum(part):
@@ -249,24 +266,29 @@
 def products(vectors, limit, pick, target, field, stream, total):
     band = lax.axis_index("band")
 
+    def at(row):
+        return field[tile(row, vectors), :]
+
+    def source(row):
+        place = pick[0, row]
+        return at(place if limit is None else jnp.minimum(place, limit))
+
     def some(piece, carry):
         stream.wait(piece)
         forward, mirrored = [], []
         base = piece * UNROLL
-        for u in range(UNROLL):
+        for u in range(0, UNROLL, 2):
             row = base + u
-            block = stream.held[row]
-            source = pick[0, row]
-            if limit is not None:
-                source = jnp.minimum(source, limit)
-            forward.append(times_transposed(field[tile(source, vectors), :], block))
-            mirrored.append(times(field[tile(row, vectors), :], block))
+            forward += times_two_transposed(source(row), source(row + 1), stream.held[row], stream.held[row + 1])
+            mirrored += times_two(at(row), at(row + 1), stream.held[pl.ds(row, 2)])
+        own = stream.own
+        first = band * (own * stream.pieces) + piece * own
+        values = []
+        for d in range(0, own, 2):
+            values += times_two(at(first + d), at(first + d + 1), stream.held_diag[pl.ds(piece * own + d, 2)])
         for u in range(UNROLL):
             total[tile(base + u, vectors), :] += forward[u]
             total[tile(target[0, base + u], vectors), :] += mirrored[u]
-        own = stream.own
-        first = band * (own * stream.pieces) + piece * own
-        values = [times(field[tile(first + d, vectors), :], stream.held_diag[piece * own + d]) for d in range(own)]
         for d, value in enumerate(values):
             total[tile(first + d, vectors), :] += value
         return carry
@@ -455,19 +477,24 @@
                 image_own[v, inside, :] = array[source, :]
     field[rows * vectors :, :] = jnp.zeros((vectors, shape[1]), bf16)
 
+    def at(row):
+        return field[tile(row, vectors), :]
+
     def some(piece, parts):
         stream.wait(piece)
         twice, once = parts
         base = piece * UNROLL
-        for u in range(UNROLL):
+        for u in range(0, UNROLL, 2):
             row = base + u
-            value = times(field[tile(row, vectors), :], stream.held[row])
-            source = jnp.minimum(pick[0, row], rows)
-            twice = twice + value * field[tile(source, vectors), :].astype(f32)
-        for d in range(stream.own):
+            values = times_two(at(row), at(row + 1), stream.held[pl.ds(row, 2)])
+            for k, value in enumerate(values):
+                source = jnp.minimum(pick[0, row + k], rows)
+                twice = twice + value * at(source).astype(f32)
+        for d in range(0, stream.own, 2):
             row = (band * stream.pieces + piece) * stream.own + d
-            here = field[tile(row, vectors), :]
-            once = once + times(here, stream.held_diag[piece * stream.own + d]) * here.astype(f32)
+            here, there = at(row), at(row + 1)
+            one, other = times_two(here, there, stream.held_diag[pl.ds(piece * stream.own + d, 2)])
+            once = once + one * here.astype(f32) + other * there.astype(f32)
         return twice, once
 
     nothing = jnp.zeros(shape, f32)
@@ -753,7 +780,9 @@
     each = keep[0].shape[0] // vectors
     came = [swap(array, 1) for array in give]
     codes = [encode(one, two, vectors) for one, two in zip(keep, came)]
-    across = [swap(code, 2) for code in codes]
+    across = []
+    for code in codes:
+        across.append(swap(code, 2))
     mine = [
         decode(code, other, vectors, each, None if drive is None else drive[c])
         for c, (code, other) in enumerate(zip(codes, across))
@@ -771,9 +800,11 @@
     rounded = state.astype(bf16)
     state = in_hbm(state)
     across = swap(rounded, 2)
-    parts = [rounded, swap(rounded, 1), across, swap(across, 1)]
+    beside = swap(rounded, 1)
     pick, target, wanted, origin = plan(block_cols.reshape(1, rows))
     asked = exchange(wanted)
+    corner = swap(across, 1)
+    parts = [rounded, beside, across, corner]
     field, own, split = spread(parts, origin, blocks)
     message = reply(asked, field, split, vectors)
     halo = exchange(message)

time: 147 us -> 138 us (0.939)
  Pallas kernels: 51.5 us -> 42.2 us
    pallas_call x1, Pallas kernels: 11.2 us -> 6.88 us  [operate_local(): pl.pallas_call(functools.partial(local_kernel, rows, vectors), out_shape=...]
    pallas_call x1, Pallas kernels: 11.7 us -> 7.41 us  [operate_second(): pl.pallas_call(functools.partial(second_kernel, rows, vectors, groups), o...]
  transfers between devices with their start and end apart: 19 -> 19, of which waited for: 9 -> 10; matrix products, arithmetic and copies ran while one was open for 0% -> 0% of each run, Pallas kernels for 21% -> 18%
where the time goes in v4:
time: 138 us; the launch traced here: 137 us
  Pallas kernels  42.2 us (31%)
  waiting for transfers between devices  36.3 us (26%)
  blocking collectives  29.1 us (21%)
  starting transfers between devices  26.9 us (19%)
  local copies, waits for them, and re-layouts  1.5 us (1%)
    ppermute x15, waiting for transfers between devices, swap(): return lax.ppermute(array, 'band', [(k, k ^ bit) for k in range(size)])  33 us
    all_to_all x4, starting transfers between devices, exchange(): lax.all_to_all(array, 'curve', split_axis=0, concat_axis=0, tiled=True)  18.1 us
    all_to_all x1, blocking collectives, exchange(): lax.all_to_all(array, 'curve', split_axis=0, concat_axis=0, tiled=True)  16.2 us
    all_to_all x1, blocking collectives, body(): lax.all_to_all(share, ('curve', 'band'), split_axis=0, concat_axis=0, til...  12.9 us
    ppermute x15, starting transfers between devices, swap(): return lax.ppermute(array, 'band', [(k, k ^ bit) for k in range(size)])  8.71 us
    pallas_call x1, Pallas kernels, operate_third(): pl.pallas_call(functools.partial(third_kernel, rows, vectors, groups, wid...  7.72 us
    pallas_call x1, Pallas kernels, operate_second(): pl.pallas_call(functools.partial(second_kernel, rows, vectors, groups), o...  7.41 us
    pallas_call x1, Pallas kernels, operate_local(): pl.pallas_call(functools.partial(local_kernel, rows, vectors), out_shape=...  6.88 us
  transfers between devices with their start and end apart: 19, of which 10 were waited for; matrix products, arithmetic and copies ran while one was open for 0% of the time, Pallas kernels for 18%

profile of v4, /device:TPU:0, one launch (start us, length us, event | category | flops | bytes accessed | tf_op | source)
XLA Modules:
  0.0 137.2 jit_solution(7424084587504635685)
XLA Ops:
  1.1 3.0 %collective-permute-start.1 = (bf16[4,256,128]{2,1,0:T(8,128)(2,1)S(1)}, bf16[4,256,128]{2,1,0:T(8,128)(2,1)S(1)}, u32[]{:S(2)}, u32[]{:S(2)}) collective-permute-start(bf16[4,256,128]{2,1,0:T(8,128)(2,1)S(1)} %convert_element_type.3.refs_0_), channel_id=1, source_target_pairs={{0,2},{1,3},{2,0},{3,1},{4,6},{5,7},{6,4},{7,5},{8,10},{9,11},{10,... | collective-permute-start | bytes 786440 | tf_op jit(solution)/shard_map/ppermute | solution.py:772
  4.1 6.3 %collective-permute-done.1.refs_2_ = bf16[4,256,128]{2,1,0:T(8,128)(2,1)S(1)} collective-permute-done((bf16[4,256,128]{2,1,0:T(8,128)(2,1)S(1)}, bf16[4,256,128]{2,1,0:T(8,128)(2,1)S(1)}, u32[]{:S(2)}, u32[]{:S(2)}) %collective-permute-start.1) | collective-permute-done | bytes 262176 | tf_op jit(solution)/shard_map/ppermute | solution.py:772
  11.9 6.1 %all-to-all-start = ((s32[8,1,128]{2,1,0:T(1,128)}), s32[8,1,128]{2,1,0:T(1,128)S(1)}, u32[]{:S(2)}, u32[]{:S(2)}) async-start(s32[8,1,128]{2,1,0:T(1,128)} %bitcast.2), calls=%async_computation | async-start | bytes 8192 | tf_op jit(solution)/shard_map/all_to_all | solution.py:776
  18.0 4.4 %spread.1 = (bf16[4112,128]{1,0:T(8,128)(2,1)}, bf16[16,128,128]{2,1,0:T(8,128)(2,1)}, bf16[512,128]{1,0:T(8,128)(2,1)S(1)}) custom-call(s32[8,128]{1,0:T(8,128)S(1)} %get-tuple-element.27.origin, bf16[256,1,128,128]{3,2,1,0:T(8,128)(2,1)} %refs_9_.1, bf16[4,256,128]{2,1,0:T(8,128)(2,1)S(1)} %convert_element_type.3.refs_0_, ...), custom_call_target="tpu_custom_call" | custom-call | tf_op jit(solution)/shard_map/spread/pallas_call | solution.py:194
  22.4 2.1 %all-to-all-done = s32[8,1,128]{2,1,0:T(1,128)S(1)} async-done(((s32[8,1,128]{2,1,0:T(1,128)}), s32[8,1,128]{2,1,0:T(1,128)S(1)}, u32[]{:S(2)}, u32[]{:S(2)}) %all-to-all-start) | async-done | bytes 4128 | tf_op jit(solution)/shard_map/all_to_all | solution.py:776
  24.5 2.1 %reply.1 = bf16[768,128]{1,0:T(8,128)(2,1)} custom-call(s32[8,128]{1,0:T(8,128)S(1)} %bitcast.19, bf16[4112,128]{1,0:T(8,128)(2,1)} %get-tuple-element.29.field, bf16[512,128]{1,0:T(8,128)(2,1)S(1)} %get-tuple-element.30.split), custom_call_target="tpu_custom_call" | custom-call | tf_op jit(solution)/shard_map/reply/pallas_call | solution.py:223
  26.6 3.9 %all-to-all-start.1 = ((bf16[8,96,128]{2,1,0:T(8,128)(2,1)}), bf16[8,96,128]{2,1,0:T(8,128)(2,1)S(1)}, u32[]{:S(2)}, u32[]{:S(2)}) async-start(bf16[8,96,128]{2,1,0:T(8,128)(2,1)} %bitcast.4), calls=%async_computation.1 | async-start | bytes 393216 | tf_op jit(solution)/shard_map/all_to_all | solution.py:776
  30.5 6.9 %operate_local.1.local = f32[4112,128]{1,0:T(8,128)S(1)} custom-call(s32[1,256]{1,0:T(1,128)S(1)} %get-tuple-element.25.pick, s32[1,256]{1,0:T(1,128)S(1)} %get-tuple-element.28.target, bf16[4112,128]{1,0:T(8,128)(2,1)} %get-tuple-element.29.field, f32[4,256,128]{2,1,0:T(8,128)} %state.3, bf16[256,1,128,128]{3,2,1,0:T(8,128)(2,1)} %refs_9_.1, ...), custom_call_target="tpu_custom_call" | custom-call | tf_op jit(solution)/shard_map/operate_local/pallas_call | solution.py:323
  38.5 3.6 %settle.1 = (f32[1024,128]{1,0:T(8,128)S(1)}, f32[1024,128]{1,0:T(8,128)S(1)}, f32[1024,128]{1,0:T(8,128)}, f32[1024,128]{1,0:T(8,128)}) custom-call(s32[8,128]{1,0:T(8,128)} %get-tuple-element.26.wanted, s32[8,128]{1,0:T(8,128)S(1)} %get-tuple-element.27.origin, s32[8,128]{1,0:T(8,128)S(1)} %bitcast.20, f32[4112,128]{1,0:T(8,128)S(1)} %operate_local.1.local, ...), custom_call_target="tpu_custom_call" | custom-call | tf_op jit(solution)/shard_map/settle/pallas_call | solution.py:364
  42.7 4.8 %all-to-all-start.3 = ((bf16[16,128,128]{2,1,0:T(8,128)(2,1)}), bf16[16,128,128]{2,1,0:T(8,128)(2,1)S(1)}, u32[]{:S(2)}, u32[]{:S(2)}) async-start(bf16[16,128,128]{2,1,0:T(8,128)(2,1)} %get-tuple-element.31.own.refs_8_), calls=%async_computation.3 | async-start | bytes 1048576 | tf_op jit(solution)/shard_map/all_to_all | solution.py:776
  48.0 1.6 %collective-permute-start.6 = (s16[1040,128]{1,0:T(8,128)(2,1)S(1)}, s16[1040,128]{1,0:T(8,128)(2,1)S(1)}, u32[]{:S(2)}, u32[]{:S(2)}) collective-permute-start(s16[1040,128]{1,0:T(8,128)(2,1)S(1)} %encode.5.refs_0_), channel_id=1, source_target_pairs={{0,2},{1,3},{2,0},{3,1},{4,6},{5,7},{6,4},{7,5},{8,10},{9,11},{10,... | collective-permute-start | bytes 798728 | tf_op jit(solution)/shard_map/ppermute | solution.py:772
  50.8 6.6 %collective-permute-done.6.refs_1_ = s16[1040,128]{1,0:T(8,128)(2,1)S(1)} collective-permute-done((s16[1040,128]{1,0:T(8,128)(2,1)S(1)}, s16[1040,128]{1,0:T(8,128)(2,1)S(1)}, u32[]{:S(2)}, u32[]{:S(2)}) %collective-permute-start.6) | collective-permute-done | bytes 266272 | tf_op jit(solution)/shard_map/ppermute | solution.py:772
  57.9 3.9 %collective-permute-done.4.refs_1_ = s16[1040,128]{1,0:T(8,128)(2,1)S(1)} collective-permute-done((s16[1040,128]{1,0:T(8,128)(2,1)S(1)}, s16[1040,128]{1,0:T(8,128)(2,1)S(1)}, u32[]{:S(2)}, u32[]{:S(2)}) %collective-permute-start.4) | collective-permute-done | bytes 266272 | tf_op jit(solution)/shard_map/ppermute | solution.py:772
  62.4 1.9 %collective-permute-done.7.refs_2_ = f32[1040,128]{1,0:T(8,128)S(1)} collective-permute-done((f32[1040,128]{1,0:T(8,128)S(1)}, f32[1040,128]{1,0:T(8,128)S(1)}, u32[]{:S(2)}, u32[]{:S(2)}) %collective-permute-start.7) | collective-permute-done | bytes 532512 | tf_op jit(solution)/shard_map/ppermute | solution.py:772
  65.5 16.2 %all_to_all.60 = f32[8,72,128]{2,1,0:T(8,128)S(1)} all-to-all(f32[8,72,128]{2,1,0:T(8,128)S(1)} %bitcast.15), channel_id=1, replica_groups=mesh['curve'=8,'band'=4] {'curve'}, dimensions={0} | all-to-all | bytes 589824 | tf_op jit(solution)/shard_map/all_to_all | solution.py:776
  81.7 7.4 %operate_second.1 = (f32[1024,128]{1,0:T(8,128)S(1)}, f32[1024,128]{1,0:T(8,128)S(1)}, f32[1024,128]{1,0:T(8,128)S(1)}, f32[1024,128]{1,0:T(8,128)S(1)}, f32[16,128]{1,0:T(8,128)S(1)}) custom-call(s32[1,256]{1,0:T(1,128)S(1)} %get-tuple-element.25.pick, s32[1,256]{1,0:T(1,128)S(1)} %get-tuple-element.28.target, s32[8,128]{1,0:T(8,128)S(1)} %bitcast.22, ...), custom_call_target="tpu_custom_call" | custom-call | tf_op jit(solution)/shard_map/operate_second/pallas_call | solution.py:436
  91.6 1.6 %collective-permute-start.12 = (s16[1040,128]{1,0:T(8,128)(2,1)S(1)}, s16[1040,128]{1,0:T(8,128)(2,1)S(1)}, u32[]{:S(2)}, u32[]{:S(2)}) collective-permute-start(s16[1040,128]{1,0:T(8,128)(2,1)S(1)} %encode.7.refs_0_), channel_id=1, source_target_pairs={{0,2},{1,3},{2,0},{3,1},{4,6},{5,7},{6,4},{7,5},{8,10},{9,11},{10,... | collective-permute-start | bytes 798728 | tf_op jit(solution)/shard_map/ppermute | solution.py:772
  94.4 6.6 %collective-permute-done.12.refs_1_ = s16[1040,128]{1,0:T(8,128)(2,1)S(1)} collective-permute-done((s16[1040,128]{1,0:T(8,128)(2,1)S(1)}, s16[1040,128]{1,0:T(8,128)(2,1)S(1)}, u32[]{:S(2)}, u32[]{:S(2)}) %collective-permute-start.12) | collective-permute-done | bytes 266272 | tf_op jit(solution)/shard_map/ppermute | solution.py:772
  101.5 4.3 %collective-permute-done.10.refs_1_ = s16[1040,128]{1,0:T(8,128)(2,1)S(1)} collective-permute-done((s16[1040,128]{1,0:T(8,128)(2,1)S(1)}, s16[1040,128]{1,0:T(8,128)(2,1)S(1)}, u32[]{:S(2)}, u32[]{:S(2)}) %collective-permute-start.10) | collective-permute-done | bytes 266272 | tf_op jit(solution)/shard_map/ppermute | solution.py:772
  106.4 1.9 %collective-permute-done.13.refs_6_.refs_2_ = f32[1056,128]{1,0:T(8,128)S(1)} collective-permute-done((f32[1056,128]{1,0:T(8,128)S(1)}, f32[1056,128]{1,0:T(8,128)S(1)}, u32[]{:S(2)}, u32[]{:S(2)}) %collective-permute-start.13) | collective-permute-done | bytes 540704 | tf_op jit(solution)/shard_map/ppermute | solution.py:772
  110.6 3.3 %all-to-all-start.4 = ((bf16[8,32,128]{2,1,0:T(8,128)(2,1)}), bf16[8,32,128]{2,1,0:T(8,128)(2,1)S(1)}, u32[]{:S(2)}, u32[]{:S(2)}) async-start(bf16[8,32,128]{2,1,0:T(8,128)(2,1)} %bitcast.8), calls=%async_computation.4 | async-start | bytes 131072 | tf_op jit(solution)/shard_map/all_to_all | solution.py:776
  114.0 7.7 %operate_third.1 = (f32[16,128]{1,0:T(8,128)S(1)}, f32[256,128]{1,0:T(8,128)S(1)}, f32[4,256,128]{2,1,0:T(8,128)}, f32[4,256,128]{2,1,0:T(8,128)}) custom-call(s32[1,256]{1,0:T(1,128)S(1)} %get-tuple-element.25.pick, s32[8,128]{1,0:T(8,128)} %get-tuple-element.26.wanted, s32[8,128]{1,0:T(8,128)S(1)} %get-tuple-element.27.origin, ...), custom_call_target="tpu_custom_call" | custom-call | tf_op jit(solution)/shard_map/operate_third/pallas_call | solution.py:517
  121.8 12.9 %all_to_all.61 = f32[32,1,128]{2,1,0:T(1,128)S(1)} all-to-all(f32[32,1,128]{2,1,0:T(1,128)S(1)} %bitcast.25), channel_id=1, replica_groups=mesh['curve'=8,'band'=4] {'curve','band'}, dimensions={0} | all-to-all | bytes 32768 | tf_op jit(solution)/shard_map/all_to_all | solution.py:823
  134.8 2.5 %finish.1 = f32[4,256,128]{2,1,0:T(8,128)} custom-call(f32[32,128]{1,0:T(8,128)S(1)} %bitcast.24, f32[16,128]{1,0:T(8,128)S(1)} %get-tuple-element.42.scale, f32[4,256,128]{2,1,0:T(8,128)} %state.3, f32[4,256,128]{2,1,0:T(8,128)} %get-tuple-element.43.drive, f32[4,256,128]{2,1,0:T(8,128)} %get-tuple-element.44.image), custom_call_target="tpu_custom_call" | custom-call | tf_op jit(solution)/shard_map/finish/pallas_call | solution.py:759
  (42 shorter events, 15.4 us)
Async XLA Ops:
  1.1 9.3 %collective-permute-start.1 = (bf16[4,256,128]{2,1,0:T(8,128)(2,1)S(1)}, bf16[4,256,128]{2,1,0:T(8,128)(2,1)S(1)}, u32[]{:S(2)}, u32[]{:S(2)}) collective-permute-start(bf16[4,256,128]{2,1,0:T(8,128)(2,1)S(1)} %convert_element_type.3.refs_0_), channel_id=1, source_target_pairs={{0,2},{1,3},{2,0},{3,1},{4,6},{5,7},{6,4},{7,5},{8,10},{9,11},{10,... | collective-permute-start | bytes 786440 | tf_op jit(solution)/shard_map/ppermute | solution.py:772
  4.1 13.9 %collective-permute-start = (bf16[4,256,128]{2,1,0:T(8,128)(2,1)S(1)}, bf16[4,256,128]{2,1,0:T(8,128)(2,1)S(1)}, u32[]{:S(2)}, u32[]{:S(2)}) collective-permute-start(bf16[4,256,128]{2,1,0:T(8,128)(2,1)S(1)} %convert_element_type.3.refs_0_), channel_id=1, source_target_pairs={{0,1},{1,0},{2,3},{3,2},{4,5},{5,4},{6,7},{7,6},{8,9},{9,8},{10,11... | collective-permute-start | bytes 786440 | tf_op jit(solution)/shard_map/ppermute | solution.py:772
  10.4 7.6 %collective-permute-start.2 = (bf16[4,256,128]{2,1,0:T(8,128)(2,1)S(1)}, bf16[4,256,128]{2,1,0:T(8,128)(2,1)S(1)}, u32[]{:S(2)}, u32[]{:S(2)}) collective-permute-start(bf16[4,256,128]{2,1,0:T(8,128)(2,1)S(1)} %collective-permute-done.1.refs_2_), channel_id=1, source_target_pairs={{0,1},{1,0},{2,3},{3,2},{4,5},{5,4},{6,7},{7,6},{8,9},{9,8},{10,11... | collective-permute-start | bytes 786440 | tf_op jit(solution)/shard_map/ppermute | solution.py:772
  10.4 0.7 copy-start.2
  11.9 12.6 %all-to-all-start = ((s32[8,1,128]{2,1,0:T(1,128)}), s32[8,1,128]{2,1,0:T(1,128)S(1)}, u32[]{:S(2)}, u32[]{:S(2)}) async-start(s32[8,1,128]{2,1,0:T(1,128)} %bitcast.2), calls=%async_computation | async-start | bytes 8192 | tf_op jit(solution)/shard_map/all_to_all | solution.py:776
  26.6 12.0 %all-to-all-start.1 = ((bf16[8,96,128]{2,1,0:T(8,128)(2,1)}), bf16[8,96,128]{2,1,0:T(8,128)(2,1)S(1)}, u32[]{:S(2)}, u32[]{:S(2)}) async-start(bf16[8,96,128]{2,1,0:T(8,128)(2,1)} %bitcast.4), calls=%async_computation.1 | async-start | bytes 393216 | tf_op jit(solution)/shard_map/all_to_all | solution.py:776
  42.2 5.3 %collective-permute-start.5 = (f32[1024,128]{1,0:T(8,128)}, f32[1024,128]{1,0:T(8,128)S(1)}, u32[]{:S(2)}, u32[]{:S(2)}) collective-permute-start(f32[1024,128]{1,0:T(8,128)} %get-tuple-element.35), channel_id=1, source_target_pairs={{0,1},{1,0},{2,3},{3,2},{4,5},{5,4},{6,7},{7,6},{8,9},{9,8},{10,11... | collective-permute-start | bytes 1572872 | tf_op jit(solution)/shard_map/ppermute | solution.py:772
  42.2 7.5 %collective-permute-start.3 = (f32[1024,128]{1,0:T(8,128)}, f32[1024,128]{1,0:T(8,128)S(1)}, u32[]{:S(2)}, u32[]{:S(2)}) collective-permute-start(f32[1024,128]{1,0:T(8,128)} %get-tuple-element.33), channel_id=1, source_target_pairs={{0,1},{1,0},{2,3},{3,2},{4,5},{5,4},{6,7},{7,6},{8,9},{9,8},{10,11... | collective-permute-start | bytes 1572872 | tf_op jit(solution)/shard_map/ppermute | solution.py:772
  42.7 22.9 %all-to-all-start.3 = ((bf16[16,128,128]{2,1,0:T(8,128)(2,1)}), bf16[16,128,128]{2,1,0:T(8,128)(2,1)S(1)}, u32[]{:S(2)}, u32[]{:S(2)}) async-start(bf16[16,128,128]{2,1,0:T(8,128)(2,1)} %get-tuple-element.31.own.refs_8_), calls=%async_computation.3 | async-start | bytes 1048576 | tf_op jit(solution)/shard_map/all_to_all | solution.py:776
  48.0 9.3 %collective-permute-start.6 = (s16[1040,128]{1,0:T(8,128)(2,1)S(1)}, s16[1040,128]{1,0:T(8,128)(2,1)S(1)}, u32[]{:S(2)}, u32[]{:S(2)}) collective-permute-start(s16[1040,128]{1,0:T(8,128)(2,1)S(1)} %encode.5.refs_0_), channel_id=1, source_target_pairs={{0,2},{1,3},{2,0},{3,1},{4,6},{5,7},{6,4},{7,5},{8,10},{9,11},{10,... | collective-permute-start | bytes 798728 | tf_op jit(solution)/shard_map/ppermute | solution.py:772
  50.2 11.7 %collective-permute-start.4 = (s16[1040,128]{1,0:T(8,128)(2,1)S(1)}, s16[1040,128]{1,0:T(8,128)(2,1)S(1)}, u32[]{:S(2)}, u32[]{:S(2)}) collective-permute-start(s16[1040,128]{1,0:T(8,128)(2,1)S(1)} %encode.4.refs_0_), channel_id=1, source_target_pairs={{0,2},{1,3},{2,0},{3,1},{4,6},{5,7},{6,4},{7,5},{8,10},{9,11},{10,... | collective-permute-start | bytes 798728 | tf_op jit(solution)/shard_map/ppermute | solution.py:772
  57.8 4.5 %collective-permute-start.8 = (f32[1040,128]{1,0:T(8,128)S(1)}, f32[1040,128]{1,0:T(8,128)S(1)}, u32[]{:S(2)}, u32[]{:S(2)}) collective-permute-start(f32[1040,128]{1,0:T(8,128)S(1)} %decode.5.refs_1_.refs_2_), channel_id=1, source_target_pairs={{0,1},{1,0},{2,3},{3,2},{4,5},{5,4},{6,7},{7,6},{8,9},{9,8},{10,11... | collective-permute-start | bytes 1597448 | tf_op jit(solution)/shard_map/ppermute | solution.py:772
  62.3 2.0 %collective-permute-start.7 = (f32[1040,128]{1,0:T(8,128)S(1)}, f32[1040,128]{1,0:T(8,128)S(1)}, u32[]{:S(2)}, u32[]{:S(2)}) collective-permute-start(f32[1040,128]{1,0:T(8,128)S(1)} %decode.4.refs_0_.refs_2_), channel_id=1, source_target_pairs={{0,1},{1,0},{2,3},{3,2},{4,5},{5,4},{6,7},{7,6},{8,9},{9,8},{10,11... | collective-permute-start | bytes 1597448 | tf_op jit(solution)/shard_map/ppermute | solution.py:772
  89.1 2.0 %collective-permute-start.11 = (f32[1024,128]{1,0:T(8,128)S(1)}, f32[1024,128]{1,0:T(8,128)S(1)}, u32[]{:S(2)}, u32[]{:S(2)}) collective-permute-start(f32[1024,128]{1,0:T(8,128)S(1)} %get-tuple-element.39), channel_id=1, source_target_pairs={{0,1},{1,0},{2,3},{3,2},{4,5},{5,4},{6,7},{7,6},{8,9},{9,8},{10,11... | collective-permute-start | bytes 1572872 | tf_op jit(solution)/shard_map/ppermute | solution.py:772
  89.2 4.0 %collective-permute-start.9 = (f32[1024,128]{1,0:T(8,128)S(1)}, f32[1024,128]{1,0:T(8,128)S(1)}, u32[]{:S(2)}, u32[]{:S(2)}) collective-permute-start(f32[1024,128]{1,0:T(8,128)S(1)} %get-tuple-element.37), channel_id=1, source_target_pairs={{0,1},{1,0},{2,3},{3,2},{4,5},{5,4},{6,7},{7,6},{8,9},{9,8},{10,11... | collective-permute-start | bytes 1572872 | tf_op jit(solution)/shard_map/ppermute | solution.py:772
  91.6 9.3 %collective-permute-start.12 = (s16[1040,128]{1,0:T(8,128)(2,1)S(1)}, s16[1040,128]{1,0:T(8,128)(2,1)S(1)}, u32[]{:S(2)}, u32[]{:S(2)}) collective-permute-start(s16[1040,128]{1,0:T(8,128)(2,1)S(1)} %encode.7.refs_0_), channel_id=1, source_target_pairs={{0,2},{1,3},{2,0},{3,1},{4,6},{5,7},{6,4},{7,5},{8,10},{9,11},{10,... | collective-permute-start | bytes 798728 | tf_op jit(solution)/shard_map/ppermute | solution.py:772
  93.8 12.1 %collective-permute-start.10 = (s16[1040,128]{1,0:T(8,128)(2,1)S(1)}, s16[1040,128]{1,0:T(8,128)(2,1)S(1)}, u32[]{:S(2)}, u32[]{:S(2)}) collective-permute-start(s16[1040,128]{1,0:T(8,128)(2,1)S(1)} %encode.6.refs_0_), channel_id=1, source_target_pairs={{0,2},{1,3},{2,0},{3,1},{4,6},{5,7},{6,4},{7,5},{8,10},{9,11},{10,... | collective-permute-start | bytes 798728 | tf_op jit(solution)/shard_map/ppermute | solution.py:772
  101.4 5.0 %collective-permute-start.14 = (f32[1056,128]{1,0:T(8,128)S(1)}, f32[1056,128]{1,0:T(8,128)S(1)}, u32[]{:S(2)}, u32[]{:S(2)}) collective-permute-start(f32[1056,128]{1,0:T(8,128)S(1)} %decode.7.refs_5_.refs_1_), channel_id=1, source_target_pairs={{0,1},{1,0},{2,3},{3,2},{4,5},{5,4},{6,7},{7,6},{8,9},{9,8},{10,11... | collective-permute-start | bytes 1622024 | tf_op jit(solution)/shard_map/ppermute | solution.py:772
  106.3 2.0 %collective-permute-start.13 = (f32[1056,128]{1,0:T(8,128)S(1)}, f32[1056,128]{1,0:T(8,128)S(1)}, u32[]{:S(2)}, u32[]{:S(2)}) collective-permute-start(f32[1056,128]{1,0:T(8,128)S(1)} %decode.6.refs_4_.refs_0_), channel_id=1, source_target_pairs={{0,1},{1,0},{2,3},{3,2},{4,5},{5,4},{6,7},{7,6},{8,9},{9,8},{10,11... | collective-permute-start | bytes 1622024 | tf_op jit(solution)/shard_map/ppermute | solution.py:772
  108.3 1.5 %copy-start.1 = (f32[1056,128]{1,0:T(8,128)}, f32[1056,128]{1,0:T(8,128)S(1)}, u32[]{:S(2)}) copy-start(f32[1056,128]{1,0:T(8,128)S(1)} %collective-permute-done.13.refs_6_.refs_2_) | copy-start | bytes 1622020
  109.8 0.8 copy-start
  110.6 11.1 %all-to-all-start.4 = ((bf16[8,32,128]{2,1,0:T(8,128)(2,1)}), bf16[8,32,128]{2,1,0:T(8,128)(2,1)S(1)}, u32[]{:S(2)}, u32[]{:S(2)}) async-start(bf16[8,32,128]{2,1,0:T(8,128)(2,1)} %bitcast.8), calls=%async_computation.4 | async-start | bytes 131072 | tf_op jit(solution)/shard_map/all_to_all | solution.py:776

commit v5 on v4

--- a/solution.py
+++ b/solution.py
@@ -60,10 +60,6 @@
     return lax.dot_general(field, block, (((1,), (0,)), ((), ())), preferred_element_type=f32)
 
 
-def times_transposed(field, block):
-    return lax.dot_general(field, block, (((1,), (1,)), ((), ())), preferred_element_type=f32)
-
-
 def two(one, other):
     nothing = jnp.zeros_like(one)
     upper = jnp.concatenate([one, nothing], axis=1)
@@ -82,12 +78,6 @@
 
 def row_sum(part):
     return jnp.sum(part, axis=1, keepdims=True)
-
-
-def as_line(column, shape):
-    across = lax.broadcasted_iota(i32, shape, 1)
-    down = lax.broadcasted_iota(i32, shape, 0)
-    return jnp.sum(jnp.where(across == down, jnp.broadcast_to(column, shape), 0.0), axis=0, keepdims=True)
 
 
 def as_column(line, shape, offset=0):
@@ -176,14 +166,14 @@
     lax.fori_loop(0, slots, end, 0)
 
     def product(peer, carry):
-        for k in range(CAP):
-            value = times(field[tile(origin[peer, k], vectors), :], own[peer * CAP + k])
+        fields = [field[tile(origin[peer, k], vectors), :] for k in range(CAP)]
+        for k, value in enumerate(times_two(*fields, own[pl.ds(peer * CAP, CAP)])):
             high = value.astype(bf16)
             split[tile(peer * (2 * CAP) + k, vectors), :] = high
             split[tile(peer * (2 * CAP) + CAP + k, vectors), :] = (value - high.astype(f32)).astype(bf16)
         return carry
 
-    lax.fori_loop(0, groups, product, 0)
+    lax.fori_loop(0, groups, product, 0, unroll=8)
 
 
 def spread(parts, origin, blocks):
@@ -338,8 +328,8 @@
     def some(peer, carry):
         at = peer * (3 * CAP)
         values = []
-        for k in range(CAP):
-            value = times_transposed(halo[tile(at + k, vectors), :], own[peer * CAP + k])
+        fields = [halo[tile(at + k, vectors), :] for k in range(CAP)]
+        for k, value in enumerate(times_two_transposed(*fields, own[peer * CAP], own[peer * CAP + 1])):
             values.append((jnp.where(wanted[peer, k] < 0, rows, origin[peer, k]), value))
         for k in range(CAP):
             value = halo[tile(at + CAP + k, vectors), :].astype(f32)
@@ -349,7 +339,7 @@
             total[tile(aim, vectors), :] += value
         return carry
 
-    lax.fori_loop(0, groups, some, 0)
+    lax.fori_loop(0, groups, some, 0, unroll=8)
     give_out(rows, vectors, total, outs)
 
 
@@ -380,13 +370,16 @@
     stream.start()
     half = rows // 2
     each = half // CHUNKS
-    message = halo.shape[0] // groups
+    size = 2 * CAP + 1
     shape = scale.shape
-    line = jnp.zeros((1, shape[1]), f32)
-    for g in range(groups):
-        at = g * message + 2 * CAP * vectors
-        line = line + halo[at : at + 1, :]
-    energy = as_column(line, shape)
+
+    def gather(g, energy):
+        last = from_code(halo[tile(g * size + 2 * CAP, vectors), :])
+        digits = last[:, 2 * CAP + 1 : 2 * CAP + 2] + last[:, 2 * CAP + 2 : 2 * CAP + 3] * (1.0 / FULL)
+        return energy + digits * scale_of(last)[:, 2 * CAP : 2 * CAP + 1]
+
+    energy = lax.fori_loop(0, groups, gather, jnp.zeros((vectors, 1), f32), unroll=8)
+    energy = jnp.broadcast_to(energy * (1.0 / FULL), shape)
     beta = jnp.sqrt(energy + epsilon)
     scale[...] = beta
     inverse = 1.0 / beta
@@ -403,36 +396,32 @@
             lax.fori_loop(0, each, one, 0, unroll=16)
 
     def row(g, carry):
+        gains = scale_of(from_code(halo[tile(g * size + 2 * CAP, vectors), :])) * (1.0 / FULL)
         for k in range(2 * CAP):
-            at = pl.multiple_of(g * message + k * vectors, 8)
-            value = halo[pl.ds(at, vectors), :] * inverse
+            value = from_code(halo[tile(g * size + k, vectors), :]) * gains[:, k : k + 1] * inverse
             field[tile(rows + g * (2 * CAP) + k, vectors), :] = value.astype(bf16)
         return carry
 
-    lax.fori_loop(0, groups, row, 0)
+    lax.fori_loop(0, groups, row, 0, unroll=4)
     total[...] = jnp.zeros_like(total)
     products(vectors, None, pick, target, field, stream, total)
 
     def some(peer, carry):
-        values = []
-        for k in range(CAP):
-            place = rows + peer * (2 * CAP) + CAP + k
+        place = rows + peer * (2 * CAP) + CAP
+        fields = [field[tile(place + k, vectors), :] for k in range(CAP)]
+        for k, value in enumerate(times_two(*fields, arrived[pl.ds(peer * CAP, CAP)])):
             aim = asked[peer, k]
-            value = times(field[tile(place, vectors), :], arrived[peer * CAP + k])
-            values.append((jnp.where(aim < 0, rows, aim), value))
-        for aim, value in values:
-            total[tile(aim, vectors), :] += value
-        return carry
-
-    lax.fori_loop(0, groups, some, 0)
+            total[tile(jnp.where(aim < 0, rows, aim), vectors), :] += value
+        return carry
+
+    lax.fori_loop(0, groups, some, 0, unroll=8)
     give_out(rows, vectors, total, outs)
 
 
 def operate_second(pick, target, asked, arrays, halo, arrived, blocks, diag):
     rows, node = blocks.shape[0], blocks.shape[-1]
     groups = lax.axis_size("curve")
-    message = halo.shape[0] // groups
-    vectors = (message - 8) // (2 * CAP)
+    vectors = halo.shape[0] // (groups * (2 * CAP + 1))
     outs = pl.pallas_call(
         functools.partial(second_kernel, rows, vectors, groups),
         out_shape=chunk_shapes(rows, vectors, node) + [shaped((vectors, node), f32)],
@@ -502,12 +491,12 @@
     form[...] = 2.0 * twice + once
 
     def remote(peer, carry):
-        for k in range(CAP):
-            value = times(field[tile(origin[peer, k], vectors), :], own[peer * CAP + k])
+        fields = [at(origin[peer, k]) for k in range(CAP)]
+        for k, value in enumerate(times_two(*fields, own[pl.ds(peer * CAP, CAP)])):
             left[tile(peer * CAP + k, vectors), :] = jnp.where(wanted[peer, k] < 0, 0.0, 2.0) * value
         return carry
 
-    lax.fori_loop(0, groups, remote, 0)
+    lax.fori_loop(0, groups, remote, 0, unroll=8)
 
 
 def operate_third(pick, wanted, origin, drive, image, own, blocks, diag, width, vectors):
@@ -576,15 +565,15 @@
             value = keep[at : at + vectors, :] + came[at : at + vectors, :]
             wide[at : at + vectors, :] = value
             peak = jnp.where(lanes == p - group * node, jnp.max(jnp.abs(value), axis=1, keepdims=True), peak)
-        power = jnp.ceil(jnp.log2(jnp.maximum(peak, 1e-30)) * STEP) + 1.0
+        power = scale_power(peak)
         start = (each + group) * vectors
-        code[start : start + vectors, :] = power.astype(i32).astype(jnp.int16)
-        gain = FULL * jnp.exp2(power * (-1.0 / STEP))
+        code[start : start + vectors, :] = as_code(power)
+        gain = FULL * scale_of(-power)
         for p in inside:
             at = p * vectors
             lane = p - group * node
             scaled = wide[at : at + vectors, :] * gain[:, lane : lane + 1]
-            code[at : at + vectors, :] = jnp.round(scaled).astype(i32).astype(jnp.int16)
+            code[at : at + vectors, :] = as_code(jnp.round(scaled))
 
 
 def encode(keep, came, vectors):
@@ -613,14 +602,14 @@
     for group in range(code_tiles(each, node)):
         start = (each + group) * vectors
         gains = [
-            jnp.exp2(ref[start : start + vectors, :].astype(i32).astype(f32) * (1.0 / STEP)) * (1.0 / FULL)
+            scale_of(from_code(ref[start : start + vectors, :])) * (1.0 / FULL)
             for ref in (code, came)
         ]
         for p in range(group * node, min(each, (group + 1) * node)):
             at = p * vectors
             lane = p - group * node
             one, two = [
-                ref[at : at + vectors, :].astype(i32).astype(f32) * gain[:, lane : lane + 1]
+                from_code(ref[at : at + vectors, :]) * gain[:, lane : lane + 1]
                 for ref, gain in zip((code, came), gains)
             ]
             value = one + two
@@ -663,24 +652,49 @@
     return value
 
 
+def scale_power(peak):
+    return jnp.ceil(jnp.log2(jnp.maximum(peak, 1e-30)) * STEP) + 1.0
+
+
+def scale_of(power):
+    return jnp.exp2(power * (1.0 / STEP))
+
+
+def as_code(value):
+    return value.astype(i32).astype(jnp.int16)
+
+
+def from_code(code):
+    return code.astype(i32).astype(f32)
+
+
 def pack_kernel(each, vectors, groups, asked, origin, *refs):
     arrays, message = refs[:-1], refs[-1]
     shape = (vectors, message.shape[1])
+    lanes = lax.broadcasted_iota(i32, shape, 1)
     sums = arrays[0][each * vectors :, :]
     for array in arrays[1:]:
         sums = sums + array[each * vectors :, :]
-    line = jnp.broadcast_to(as_line(row_sum(sums), shape), shape)[0:8, :]
-    size = 2 * CAP * vectors + 8
+    energy = jnp.broadcast_to(row_sum(sums), shape)
+    power = scale_power(energy)
+    digits = energy * (FULL * scale_of(-power))
+    high = jnp.floor(digits)
+    low = jnp.round((digits - high) * FULL)
+    extra = jnp.where(lanes == 2 * CAP, power, jnp.where(lanes == 2 * CAP + 1, high, low))
+    size = 2 * CAP + 1
 
     def send(peer, carry):
+        last = extra
         for k in range(2 * CAP):
             row = jnp.maximum(asked[peer, k], 0) if k < CAP else origin[peer, k - CAP]
-            at = pl.multiple_of(peer * size + k * vectors, 8)
-            message[pl.ds(at, vectors), :] = fetch_row(arrays, each, vectors, row)
-        message[pl.ds(pl.multiple_of(peer * size + 2 * CAP * vectors, 8), 8), :] = line
-        return carry
-
-    lax.fori_loop(0, groups, send, 0)
+            value = fetch_row(arrays, each, vectors, row)
+            power = scale_power(jnp.broadcast_to(jnp.max(jnp.abs(value), axis=1, keepdims=True), shape))
+            message[tile(peer * size + k, vectors), :] = as_code(jnp.round(value * (FULL * scale_of(-power))))
+            last = jnp.where(lanes == k, power, last)
+        message[tile(peer * size + 2 * CAP, vectors), :] = as_code(last)
+        return carry
+
+    lax.fori_loop(0, groups, send, 0, unroll=4)
 
 
 def pack(asked, origin, arrays, vectors):
@@ -689,7 +703,7 @@
     groups = lax.axis_size("curve")
     return pl.pallas_call(
         functools.partial(pack_kernel, each, vectors, groups),
-        out_shape=shaped((groups * (2 * CAP * vectors + 8), node), f32),
+        out_shape=shaped((groups * (2 * CAP + 1) * vectors, node), jnp.int16),
         in_specs=[smem()] * 2 + [vmem()] * (2 * CHUNKS),
         out_specs=vmem(),
         compiler_params=params(16),
@@ -723,7 +737,14 @@
     )(asked, *arrays)
 
 
-def finish_kernel(shares, scale, state, drive, image, out, one, two, lift, mix):
+def finish_kernel(shares, scale, state_in, drive_in, image_in, out, one, two, mix, state, drive, image, sems):
+    copies = [
+        [pltpu.make_async_copy(source.at[v], place.at[v], sems.at[k, v]) for v in range(out.shape[0])]
+        for k, (source, place) in enumerate(((state_in, state), (drive_in, drive), (image_in, image)))
+    ]
+    for column in copies:
+        for copy in column:
+            copy.start()
     shape = scale.shape
     vectors = shape[0]
     line = jnp.sum(shares[...], axis=0, keepdims=True)
@@ -752,6 +773,8 @@
         at = pl.ds(lax.axis_index("band") * width + v, 1)
         size = state.shape[1:]
         weight_one, weight_two, share = [jnp.broadcast_to(ref[at, :], size) for ref in (one, two, mix)]
+        for column in copies:
+            column[v].wait()
         out[v] = state[v] + (weight_one * drive[v] + weight_two * (image[v] - share * drive[v]))
 
 
@@ -759,9 +782,11 @@
     return pl.pallas_call(
         finish_kernel,
         out_shape=shaped(state.shape, f32),
-        in_specs=[vmem()] * 5,
+        in_specs=[vmem()] * 2 + [anywhere()] * 3,
         out_specs=vmem(),
-        scratch_shapes=[pltpu.VMEM(scale.shape, f32)] * 4,
+        scratch_shapes=[pltpu.VMEM(scale.shape, f32)] * 3
+        + [pltpu.VMEM(state.shape, f32)] * 3
+        + [pltpu.SemaphoreType.DMA((3, state.shape[0]))],
         compiler_params=params(16),
         name="finish",
     )(shares, scale, state, in_hbm(drive), in_hbm(image))

time: 138 us -> 132 us (0.957)
  Pallas kernels: 42.2 us -> 38.5 us
  blocking collectives: 29.1 us -> 26.2 us
    all_to_all x1, blocking collectives: 16.2 us -> 13.3 us  [exchange(): lax.all_to_all(array, 'curve', split_axis=0, concat_axis=0, tiled=True)]
where the time goes in v5:
time: 132 us; the launch traced here: 131 us
  Pallas kernels  38.5 us (29%)
  waiting for transfers between devices  37 us (28%)
  starting transfers between devices  26.6 us (20%)
  blocking collectives  26.2 us (20%)
  local copies, waits for them, and re-layouts  1.5 us (1%)
    ppermute x15, waiting for transfers between devices, swap(): return lax.ppermute(array, 'band', [(k, k ^ bit) for k in range(size)])  33 us
    all_to_all x4, starting transfers between devices, exchange(): lax.all_to_all(array, 'curve', split_axis=0, concat_axis=0, tiled=True)  17.9 us
    all_to_all x1, blocking collectives, exchange(): lax.all_to_all(array, 'curve', split_axis=0, concat_axis=0, tiled=True)  13.3 us
    all_to_all x1, blocking collectives, body(): lax.all_to_all(share, ('curve', 'band'), split_axis=0, concat_axis=0, til...  12.9 us
    ppermute x15, starting transfers between devices, swap(): return lax.ppermute(array, 'band', [(k, k ^ bit) for k in range(size)])  8.71 us
    pallas_call x1, Pallas kernels, operate_local(): pl.pallas_call(functools.partial(local_kernel, rows, vectors), out_shape=...  6.89 us
    pallas_call x1, Pallas kernels, operate_third(): pl.pallas_call(functools.partial(third_kernel, rows, vectors, groups, wid...  6.81 us
    pallas_call x1, Pallas kernels, operate_second(): pl.pallas_call(functools.partial(second_kernel, rows, vectors, groups), o...  6.52 us
  transfers between devices with their start and end apart: 19, of which 10 were waited for; matrix products, arithmetic and copies ran while one was open for 0% of the time, Pallas kernels for 18%

profile of v5, /device:TPU:0, one launch (start us, length us, event | category | flops | bytes accessed | tf_op | source)
XLA Modules:
  0.0 131.0 jit_solution(6010674023413635649)
XLA Ops:
  1.1 3.0 %collective-permute-start.1 = (bf16[4,256,128]{2,1,0:T(8,128)(2,1)S(1)}, bf16[4,256,128]{2,1,0:T(8,128)(2,1)S(1)}, u32[]{:S(2)}, u32[]{:S(2)}) collective-permute-start(bf16[4,256,128]{2,1,0:T(8,128)(2,1)S(1)} %convert_element_type.3.refs_0_), channel_id=1, source_target_pairs={{0,2},{1,3},{2,0},{3,1},{4,6},{5,7},{6,4},{7,5},{8,10},{9,11},{10,... | collective-permute-start | bytes 786440 | tf_op jit(solution)/shard_map/ppermute | solution.py:797
  4.1 6.3 %collective-permute-done.1.refs_2_ = bf16[4,256,128]{2,1,0:T(8,128)(2,1)S(1)} collective-permute-done((bf16[4,256,128]{2,1,0:T(8,128)(2,1)S(1)}, bf16[4,256,128]{2,1,0:T(8,128)(2,1)S(1)}, u32[]{:S(2)}, u32[]{:S(2)}) %collective-permute-start.1) | collective-permute-done | bytes 262176 | tf_op jit(solution)/shard_map/ppermute | solution.py:797
  11.9 6.1 %all-to-all-start = ((s32[8,1,128]{2,1,0:T(1,128)}), s32[8,1,128]{2,1,0:T(1,128)S(1)}, u32[]{:S(2)}, u32[]{:S(2)}) async-start(s32[8,1,128]{2,1,0:T(1,128)} %bitcast.2), calls=%async_computation | async-start | bytes 8192 | tf_op jit(solution)/shard_map/all_to_all | solution.py:801
  18.0 3.4 %spread.1 = (bf16[4112,128]{1,0:T(8,128)(2,1)}, bf16[16,128,128]{2,1,0:T(8,128)(2,1)}, bf16[512,128]{1,0:T(8,128)(2,1)S(1)}) custom-call(s32[8,128]{1,0:T(8,128)S(1)} %get-tuple-element.27.origin, bf16[256,1,128,128]{3,2,1,0:T(8,128)(2,1)} %refs_9_.1, bf16[4,256,128]{2,1,0:T(8,128)(2,1)S(1)} %convert_element_type.3.refs_0_, ...), custom_call_target="tpu_custom_call" | custom-call | tf_op jit(solution)/shard_map/spread/pallas_call | solution.py:184
  21.5 3.1 %all-to-all-done = s32[8,1,128]{2,1,0:T(1,128)S(1)} async-done(((s32[8,1,128]{2,1,0:T(1,128)}), s32[8,1,128]{2,1,0:T(1,128)S(1)}, u32[]{:S(2)}, u32[]{:S(2)}) %all-to-all-start) | async-done | bytes 4128 | tf_op jit(solution)/shard_map/all_to_all | solution.py:801
  24.5 2.1 %reply.1 = bf16[768,128]{1,0:T(8,128)(2,1)} custom-call(s32[8,128]{1,0:T(8,128)S(1)} %bitcast.19, bf16[4112,128]{1,0:T(8,128)(2,1)} %get-tuple-element.29.field, bf16[512,128]{1,0:T(8,128)(2,1)S(1)} %get-tuple-element.30.split), custom_call_target="tpu_custom_call" | custom-call | tf_op jit(solution)/shard_map/reply/pallas_call | solution.py:213
  26.6 3.4 %all-to-all-start.1 = ((bf16[8,96,128]{2,1,0:T(8,128)(2,1)}), bf16[8,96,128]{2,1,0:T(8,128)(2,1)S(1)}, u32[]{:S(2)}, u32[]{:S(2)}) async-start(bf16[8,96,128]{2,1,0:T(8,128)(2,1)} %bitcast.4), calls=%async_computation.1 | async-start | bytes 393216 | tf_op jit(solution)/shard_map/all_to_all | solution.py:801
  30.0 6.9 %operate_local.1.local = f32[4112,128]{1,0:T(8,128)S(1)} custom-call(s32[1,256]{1,0:T(1,128)S(1)} %get-tuple-element.25.pick, s32[1,256]{1,0:T(1,128)S(1)} %get-tuple-element.28.target, bf16[4112,128]{1,0:T(8,128)(2,1)} %get-tuple-element.29.field, f32[4,256,128]{2,1,0:T(8,128)} %state_in.1, bf16[256,1,128,128]{3,2,1,0:T(8,128)(2,1)} %refs_9_.1, ...), custom_call_target="tpu_custom_call" | custom-call | tf_op jit(solution)/shard_map/operate_local/pallas_call | solution.py:313
  37.7 2.5 %settle.1 = (f32[1024,128]{1,0:T(8,128)S(1)}, f32[1024,128]{1,0:T(8,128)S(1)}, f32[1024,128]{1,0:T(8,128)}, f32[1024,128]{1,0:T(8,128)}) custom-call(s32[8,128]{1,0:T(8,128)} %get-tuple-element.26.wanted, s32[8,128]{1,0:T(8,128)S(1)} %get-tuple-element.27.origin, s32[8,128]{1,0:T(8,128)S(1)} %bitcast.20, f32[4112,128]{1,0:T(8,128)S(1)} %operate_local.1.local, ...), custom_call_target="tpu_custom_call" | custom-call | tf_op jit(solution)/shard_map/settle/pallas_call | solution.py:354
  40.8 5.1 %all-to-all-start.3 = ((bf16[16,128,128]{2,1,0:T(8,128)(2,1)}), bf16[16,128,128]{2,1,0:T(8,128)(2,1)S(1)}, u32[]{:S(2)}, u32[]{:S(2)}) async-start(bf16[16,128,128]{2,1,0:T(8,128)(2,1)} %get-tuple-element.31.own.refs_8_), calls=%async_computation.3 | async-start | bytes 1048576 | tf_op jit(solution)/shard_map/all_to_all | solution.py:801
  46.4 1.6 %collective-permute-start.6 = (s16[1040,128]{1,0:T(8,128)(2,1)S(1)}, s16[1040,128]{1,0:T(8,128)(2,1)S(1)}, u32[]{:S(2)}, u32[]{:S(2)}) collective-permute-start(s16[1040,128]{1,0:T(8,128)(2,1)S(1)} %encode.5.refs_0_), channel_id=1, source_target_pairs={{0,2},{1,3},{2,0},{3,1},{4,6},{5,7},{6,4},{7,5},{8,10},{9,11},{10,... | collective-permute-start | bytes 798728 | tf_op jit(solution)/shard_map/ppermute | solution.py:797
  49.1 6.6 %collective-permute-done.6.refs_1_ = s16[1040,128]{1,0:T(8,128)(2,1)S(1)} collective-permute-done((s16[1040,128]{1,0:T(8,128)(2,1)S(1)}, s16[1040,128]{1,0:T(8,128)(2,1)S(1)}, u32[]{:S(2)}, u32[]{:S(2)}) %collective-permute-start.6) | collective-permute-done | bytes 266272 | tf_op jit(solution)/shard_map/ppermute | solution.py:797
  56.3 3.9 %collective-permute-done.4.refs_1_ = s16[1040,128]{1,0:T(8,128)(2,1)S(1)} collective-permute-done((s16[1040,128]{1,0:T(8,128)(2,1)S(1)}, s16[1040,128]{1,0:T(8,128)(2,1)S(1)}, u32[]{:S(2)}, u32[]{:S(2)}) %collective-permute-start.4) | collective-permute-done | bytes 266272 | tf_op jit(solution)/shard_map/ppermute | solution.py:797
  60.7 1.9 %collective-permute-done.7.refs_2_ = f32[1040,128]{1,0:T(8,128)S(1)} collective-permute-done((f32[1040,128]{1,0:T(8,128)S(1)}, f32[1040,128]{1,0:T(8,128)S(1)}, u32[]{:S(2)}, u32[]{:S(2)}) %collective-permute-start.7) | collective-permute-done | bytes 532512 | tf_op jit(solution)/shard_map/ppermute | solution.py:797
  64.1 13.3 %all_to_all.60 = s16[8,80,128]{2,1,0:T(8,128)(2,1)S(1)} all-to-all(s16[8,80,128]{2,1,0:T(8,128)(2,1)S(1)} %bitcast.16), channel_id=1, replica_groups=mesh['curve'=8,'band'=4] {'curve'}, dimensions={0} | all-to-all | bytes 327680 | tf_op jit(solution)/shard_map/all_to_all | solution.py:801
  77.4 6.5 %operate_second.1 = (f32[1024,128]{1,0:T(8,128)S(1)}, f32[1024,128]{1,0:T(8,128)S(1)}, f32[1024,128]{1,0:T(8,128)S(1)}, f32[1024,128]{1,0:T(8,128)S(1)}, f32[16,128]{1,0:T(8,128)S(1)}) custom-call(s32[1,256]{1,0:T(1,128)S(1)} %get-tuple-element.25.pick, s32[1,256]{1,0:T(1,128)S(1)} %get-tuple-element.28.target, s32[8,128]{1,0:T(8,128)S(1)} %bitcast.22, ...), custom_call_target="tpu_custom_call" | custom-call | tf_op jit(solution)/shard_map/operate_second/pallas_call | solution.py:425
  86.4 1.6 %collective-permute-start.12 = (s16[1040,128]{1,0:T(8,128)(2,1)S(1)}, s16[1040,128]{1,0:T(8,128)(2,1)S(1)}, u32[]{:S(2)}, u32[]{:S(2)}) collective-permute-start(s16[1040,128]{1,0:T(8,128)(2,1)S(1)} %encode.7.refs_0_), channel_id=1, source_target_pairs={{0,2},{1,3},{2,0},{3,1},{4,6},{5,7},{6,4},{7,5},{8,10},{9,11},{10,... | collective-permute-start | bytes 798728 | tf_op jit(solution)/shard_map/ppermute | solution.py:797
  89.1 6.6 %collective-permute-done.12.refs_1_ = s16[1040,128]{1,0:T(8,128)(2,1)S(1)} collective-permute-done((s16[1040,128]{1,0:T(8,128)(2,1)S(1)}, s16[1040,128]{1,0:T(8,128)(2,1)S(1)}, u32[]{:S(2)}, u32[]{:S(2)}) %collective-permute-start.12) | collective-permute-done | bytes 266272 | tf_op jit(solution)/shard_map/ppermute | solution.py:797
  96.3 4.3 %collective-permute-done.10.refs_1_ = s16[1040,128]{1,0:T(8,128)(2,1)S(1)} collective-permute-done((s16[1040,128]{1,0:T(8,128)(2,1)S(1)}, s16[1040,128]{1,0:T(8,128)(2,1)S(1)}, u32[]{:S(2)}, u32[]{:S(2)}) %collective-permute-start.10) | collective-permute-done | bytes 266272 | tf_op jit(solution)/shard_map/ppermute | solution.py:797
  101.2 1.9 %collective-permute-done.13.refs_6_.refs_2_ = f32[1056,128]{1,0:T(8,128)S(1)} collective-permute-done((f32[1056,128]{1,0:T(8,128)S(1)}, f32[1056,128]{1,0:T(8,128)S(1)}, u32[]{:S(2)}, u32[]{:S(2)}) %collective-permute-start.13) | collective-permute-done | bytes 540704 | tf_op jit(solution)/shard_map/ppermute | solution.py:797
  105.4 3.3 %all-to-all-start.4 = ((bf16[8,32,128]{2,1,0:T(8,128)(2,1)}), bf16[8,32,128]{2,1,0:T(8,128)(2,1)S(1)}, u32[]{:S(2)}, u32[]{:S(2)}) async-start(bf16[8,32,128]{2,1,0:T(8,128)(2,1)} %bitcast.8), calls=%async_computation.4 | async-start | bytes 131072 | tf_op jit(solution)/shard_map/all_to_all | solution.py:801
  108.8 6.8 %operate_third.1 = (f32[16,128]{1,0:T(8,128)S(1)}, f32[256,128]{1,0:T(8,128)S(1)}, f32[4,256,128]{2,1,0:T(8,128)}, f32[4,256,128]{2,1,0:T(8,128)}) custom-call(s32[1,256]{1,0:T(1,128)S(1)} %get-tuple-element.25.pick, s32[8,128]{1,0:T(8,128)} %get-tuple-element.26.wanted, s32[8,128]{1,0:T(8,128)S(1)} %get-tuple-element.27.origin, ...), custom_call_target="tpu_custom_call" | custom-call | tf_op jit(solution)/shard_map/operate_third/pallas_call | solution.py:506
  115.7 12.9 %all_to_all.61 = f32[32,1,128]{2,1,0:T(1,128)S(1)} all-to-all(f32[32,1,128]{2,1,0:T(1,128)S(1)} %bitcast.25), channel_id=1, replica_groups=mesh['curve'=8,'band'=4] {'curve','band'}, dimensions={0} | all-to-all | bytes 32768 | tf_op jit(solution)/shard_map/all_to_all | solution.py:848
  128.6 2.4 %finish.1 = f32[4,256,128]{2,1,0:T(8,128)} custom-call(f32[32,128]{1,0:T(8,128)S(1)} %bitcast.24, f32[16,128]{1,0:T(8,128)S(1)} %get-tuple-element.42.scale, f32[4,256,128]{2,1,0:T(8,128)} %state_in.1, f32[4,256,128]{2,1,0:T(8,128)} %get-tuple-element.43.drive_in, f32[4,256,128]{2,1,0:T(8,128)} %get-tuple-element.44.image_in), custom_call_target="tpu_custom_call" | custom-call | tf_op jit(solution)/shard_map/finish/pallas_call | solution.py:782
  (42 shorter events, 15.3 us)
Async XLA Ops:
  1.1 9.3 %collective-permute-start.1 = (bf16[4,256,128]{2,1,0:T(8,128)(2,1)S(1)}, bf16[4,256,128]{2,1,0:T(8,128)(2,1)S(1)}, u32[]{:S(2)}, u32[]{:S(2)}) collective-permute-start(bf16[4,256,128]{2,1,0:T(8,128)(2,1)S(1)} %convert_element_type.3.refs_0_), channel_id=1, source_target_pairs={{0,2},{1,3},{2,0},{3,1},{4,6},{5,7},{6,4},{7,5},{8,10},{9,11},{10,... | collective-permute-start | bytes 786440 | tf_op jit(solution)/shard_map/ppermute | solution.py:797
  4.1 13.9 %collective-permute-start = (bf16[4,256,128]{2,1,0:T(8,128)(2,1)S(1)}, bf16[4,256,128]{2,1,0:T(8,128)(2,1)S(1)}, u32[]{:S(2)}, u32[]{:S(2)}) collective-permute-start(bf16[4,256,128]{2,1,0:T(8,128)(2,1)S(1)} %convert_element_type.3.refs_0_), channel_id=1, source_target_pairs={{0,1},{1,0},{2,3},{3,2},{4,5},{5,4},{6,7},{7,6},{8,9},{9,8},{10,11... | collective-permute-start | bytes 786440 | tf_op jit(solution)/shard_map/ppermute | solution.py:797
  10.4 7.6 %collective-permute-start.2 = (bf16[4,256,128]{2,1,0:T(8,128)(2,1)S(1)}, bf16[4,256,128]{2,1,0:T(8,128)(2,1)S(1)}, u32[]{:S(2)}, u32[]{:S(2)}) collective-permute-start(bf16[4,256,128]{2,1,0:T(8,128)(2,1)S(1)} %collective-permute-done.1.refs_2_), channel_id=1, source_target_pairs={{0,1},{1,0},{2,3},{3,2},{4,5},{5,4},{6,7},{7,6},{8,9},{9,8},{10,11... | collective-permute-start | bytes 786440 | tf_op jit(solution)/shard_map/ppermute | solution.py:797
  10.4 0.7 copy-start.2
  11.9 12.6 %all-to-all-start = ((s32[8,1,128]{2,1,0:T(1,128)}), s32[8,1,128]{2,1,0:T(1,128)S(1)}, u32[]{:S(2)}, u32[]{:S(2)}) async-start(s32[8,1,128]{2,1,0:T(1,128)} %bitcast.2), calls=%async_computation | async-start | bytes 8192 | tf_op jit(solution)/shard_map/all_to_all | solution.py:801
  26.6 11.1 %all-to-all-start.1 = ((bf16[8,96,128]{2,1,0:T(8,128)(2,1)}), bf16[8,96,128]{2,1,0:T(8,128)(2,1)S(1)}, u32[]{:S(2)}, u32[]{:S(2)}) async-start(bf16[8,96,128]{2,1,0:T(8,128)(2,1)} %bitcast.4), calls=%async_computation.1 | async-start | bytes 393216 | tf_op jit(solution)/shard_map/all_to_all | solution.py:801
  40.2 5.6 %collective-permute-start.5 = (f32[1024,128]{1,0:T(8,128)}, f32[1024,128]{1,0:T(8,128)S(1)}, u32[]{:S(2)}, u32[]{:S(2)}) collective-permute-start(f32[1024,128]{1,0:T(8,128)} %get-tuple-element.35), channel_id=1, source_target_pairs={{0,1},{1,0},{2,3},{3,2},{4,5},{5,4},{6,7},{7,6},{8,9},{9,8},{10,11... | collective-permute-start | bytes 1572872 | tf_op jit(solution)/shard_map/ppermute | solution.py:797
  40.2 7.7 %collective-permute-start.3 = (f32[1024,128]{1,0:T(8,128)}, f32[1024,128]{1,0:T(8,128)S(1)}, u32[]{:S(2)}, u32[]{:S(2)}) collective-permute-start(f32[1024,128]{1,0:T(8,128)} %get-tuple-element.33), channel_id=1, source_target_pairs={{0,1},{1,0},{2,3},{3,2},{4,5},{5,4},{6,7},{7,6},{8,9},{9,8},{10,11... | collective-permute-start | bytes 1572872 | tf_op jit(solution)/shard_map/ppermute | solution.py:797
  40.8 23.3 %all-to-all-start.3 = ((bf16[16,128,128]{2,1,0:T(8,128)(2,1)}), bf16[16,128,128]{2,1,0:T(8,128)(2,1)S(1)}, u32[]{:S(2)}, u32[]{:S(2)}) async-start(bf16[16,128,128]{2,1,0:T(8,128)(2,1)} %get-tuple-element.31.own.refs_8_), calls=%async_computation.3 | async-start | bytes 1048576 | tf_op jit(solution)/shard_map/all_to_all | solution.py:801
  46.4 9.3 %collective-permute-start.6 = (s16[1040,128]{1,0:T(8,128)(2,1)S(1)}, s16[1040,128]{1,0:T(8,128)(2,1)S(1)}, u32[]{:S(2)}, u32[]{:S(2)}) collective-permute-start(s16[1040,128]{1,0:T(8,128)(2,1)S(1)} %encode.5.refs_0_), channel_id=1, source_target_pairs={{0,2},{1,3},{2,0},{3,1},{4,6},{5,7},{6,4},{7,5},{8,10},{9,11},{10,... | collective-permute-start | bytes 798728 | tf_op jit(solution)/shard_map/ppermute | solution.py:797
  48.5 11.7 %collective-permute-start.4 = (s16[1040,128]{1,0:T(8,128)(2,1)S(1)}, s16[1040,128]{1,0:T(8,128)(2,1)S(1)}, u32[]{:S(2)}, u32[]{:S(2)}) collective-permute-start(s16[1040,128]{1,0:T(8,128)(2,1)S(1)} %encode.4.refs_0_), channel_id=1, source_target_pairs={{0,2},{1,3},{2,0},{3,1},{4,6},{5,7},{6,4},{7,5},{8,10},{9,11},{10,... | collective-permute-start | bytes 798728 | tf_op jit(solution)/shard_map/ppermute | solution.py:797
  56.2 4.5 %collective-permute-start.8 = (f32[1040,128]{1,0:T(8,128)S(1)}, f32[1040,128]{1,0:T(8,128)S(1)}, u32[]{:S(2)}, u32[]{:S(2)}) collective-permute-start(f32[1040,128]{1,0:T(8,128)S(1)} %decode.5.refs_1_.refs_2_), channel_id=1, source_target_pairs={{0,1},{1,0},{2,3},{3,2},{4,5},{5,4},{6,7},{7,6},{8,9},{9,8},{10,11... | collective-permute-start | bytes 1597448 | tf_op jit(solution)/shard_map/ppermute | solution.py:797
  60.7 2.0 %collective-permute-start.7 = (f32[1040,128]{1,0:T(8,128)S(1)}, f32[1040,128]{1,0:T(8,128)S(1)}, u32[]{:S(2)}, u32[]{:S(2)}) collective-permute-start(f32[1040,128]{1,0:T(8,128)S(1)} %decode.4.refs_0_.refs_2_), channel_id=1, source_target_pairs={{0,1},{1,0},{2,3},{3,2},{4,5},{5,4},{6,7},{7,6},{8,9},{9,8},{10,11... | collective-permute-start | bytes 1597448 | tf_op jit(solution)/shard_map/ppermute | solution.py:797
  83.9 2.0 %collective-permute-start.11 = (f32[1024,128]{1,0:T(8,128)S(1)}, f32[1024,128]{1,0:T(8,128)S(1)}, u32[]{:S(2)}, u32[]{:S(2)}) collective-permute-start(f32[1024,128]{1,0:T(8,128)S(1)} %get-tuple-element.39), channel_id=1, source_target_pairs={{0,1},{1,0},{2,3},{3,2},{4,5},{5,4},{6,7},{7,6},{8,9},{9,8},{10,11... | collective-permute-start | bytes 1572872 | tf_op jit(solution)/shard_map/ppermute | solution.py:797
  84.0 4.0 %collective-permute-start.9 = (f32[1024,128]{1,0:T(8,128)S(1)}, f32[1024,128]{1,0:T(8,128)S(1)}, u32[]{:S(2)}, u32[]{:S(2)}) collective-permute-start(f32[1024,128]{1,0:T(8,128)S(1)} %get-tuple-element.37), channel_id=1, source_target_pairs={{0,1},{1,0},{2,3},{3,2},{4,5},{5,4},{6,7},{7,6},{8,9},{9,8},{10,11... | collective-permute-start | bytes 1572872 | tf_op jit(solution)/shard_map/ppermute | solution.py:797
  86.4 9.3 %collective-permute-start.12 = (s16[1040,128]{1,0:T(8,128)(2,1)S(1)}, s16[1040,128]{1,0:T(8,128)(2,1)S(1)}, u32[]{:S(2)}, u32[]{:S(2)}) collective-permute-start(s16[1040,128]{1,0:T(8,128)(2,1)S(1)} %encode.7.refs_0_), channel_id=1, source_target_pairs={{0,2},{1,3},{2,0},{3,1},{4,6},{5,7},{6,4},{7,5},{8,10},{9,11},{10,... | collective-permute-start | bytes 798728 | tf_op jit(solution)/shard_map/ppermute | solution.py:797
  88.5 12.1 %collective-permute-start.10 = (s16[1040,128]{1,0:T(8,128)(2,1)S(1)}, s16[1040,128]{1,0:T(8,128)(2,1)S(1)}, u32[]{:S(2)}, u32[]{:S(2)}) collective-permute-start(s16[1040,128]{1,0:T(8,128)(2,1)S(1)} %encode.6.refs_0_), channel_id=1, source_target_pairs={{0,2},{1,3},{2,0},{3,1},{4,6},{5,7},{6,4},{7,5},{8,10},{9,11},{10,... | collective-permute-start | bytes 798728 | tf_op jit(solution)/shard_map/ppermute | solution.py:797
  96.2 5.0 %collective-permute-start.14 = (f32[1056,128]{1,0:T(8,128)S(1)}, f32[1056,128]{1,0:T(8,128)S(1)}, u32[]{:S(2)}, u32[]{:S(2)}) collective-permute-start(f32[1056,128]{1,0:T(8,128)S(1)} %decode.7.refs_5_.refs_1_), channel_id=1, source_target_pairs={{0,1},{1,0},{2,3},{3,2},{4,5},{5,4},{6,7},{7,6},{8,9},{9,8},{10,11... | collective-permute-start | bytes 1622024 | tf_op jit(solution)/shard_map/ppermute | solution.py:797
  101.1 2.0 %collective-permute-start.13 = (f32[1056,128]{1,0:T(8,128)S(1)}, f32[1056,128]{1,0:T(8,128)S(1)}, u32[]{:S(2)}, u32[]{:S(2)}) collective-permute-start(f32[1056,128]{1,0:T(8,128)S(1)} %decode.6.refs_4_.refs_0_), channel_id=1, source_target_pairs={{0,1},{1,0},{2,3},{3,2},{4,5},{5,4},{6,7},{7,6},{8,9},{9,8},{10,11... | collective-permute-start | bytes 1622024 | tf_op jit(solution)/shard_map/ppermute | solution.py:797
  103.1 1.5 %copy-start.1 = (f32[1056,128]{1,0:T(8,128)}, f32[1056,128]{1,0:T(8,128)S(1)}, u32[]{:S(2)}) copy-start(f32[1056,128]{1,0:T(8,128)S(1)} %collective-permute-done.13.refs_6_.refs_2_) | copy-start | bytes 1622020
  104.6 0.8 copy-start
  105.4 10.2 %all-to-all-start.4 = ((bf16[8,32,128]{2,1,0:T(8,128)(2,1)}), bf16[8,32,128]{2,1,0:T(8,128)(2,1)S(1)}, u32[]{:S(2)}, u32[]{:S(2)}) async-start(bf16[8,32,128]{2,1,0:T(8,128)(2,1)} %bitcast.8), calls=%async_computation.4 | async-start | bytes 131072 | tf_op jit(solution)/shard_map/all_to_all | solution.py:801

commit v6 on v5

--- a/solution.py
+++ b/solution.py
@@ -91,7 +91,8 @@
     return jnp.bitwise_and(band, 1)
 
 
-def plan_kernel(cols, pick, target, wanted, origin):
+def plan_kernel(cols, state, rounded, pick, target, wanted, origin):
+    rounded[...] = state[...].astype(bf16)
     groups, lanes = wanted.shape
     rows = cols.shape[1]
     here = lax.axis_index("curve")
@@ -123,17 +124,17 @@
     target[...] = jnp.where(owner == here, inner, rows)
 
 
-def plan(cols):
+def plan(cols, state):
     rows = cols.shape[1]
     groups = lax.axis_size("curve")
     return pl.pallas_call(
         plan_kernel,
-        out_shape=[shaped((1, rows), i32)] * 2 + [shaped((groups, 128), i32)] * 2,
-        in_specs=[vmem()],
-        out_specs=[vmem()] * 4,
+        out_shape=[shaped(state.shape, bf16)] + [shaped((1, rows), i32)] * 2 + [shaped((groups, 128), i32)] * 2,
+        in_specs=[vmem()] * 2,
+        out_specs=[vmem()] * 5,
         compiler_params=params(8),
         name="plan",
-    )(cols)
+    )(in_hbm(cols), state)
 
 
 def spread_kernel(rows, vectors, groups, width, origin, blocks, *refs):
@@ -205,7 +206,7 @@
             message[tile(at + CAP + k, vectors), :] = split[tile(peer * (2 * CAP) + k, vectors), :]
         return carry
 
-    lax.fori_loop(0, groups, send, 0)
+    lax.fori_loop(0, groups, send, 0, unroll=8)
 
 
 def reply(asked, field, split, vectors):
@@ -514,8 +515,7 @@
     )(pick, wanted, origin, *drive, *image[:CHUNKS], *map(in_hbm, image[CHUNKS:]), own, blocks, diag)
 
 
-def tail_kernel(each, vectors, form, left, halo, *refs):
-    image, share = refs[:-1], refs[-1]
+def tail_kernel(each, vectors, form, left, halo, image, share):
     shape = form.shape
     total = form[...]
     for slot in range(left.shape[0] // vectors):
@@ -524,10 +524,7 @@
     values = [total]
     for e in range(2):
         at = (each + e) * vectors
-        value = image[0][at : at + vectors, :]
-        for other in image[1:]:
-            value = value + other[at : at + vectors, :]
-        values.append(0.5 * value)
+        values.append(0.5 * image[at : at + vectors, :])
     line = jnp.zeros((1, shape[1]), f32)
     across = lax.broadcasted_iota(i32, shape, 1)
     down = lax.broadcasted_iota(i32, shape, 0)
@@ -539,15 +536,15 @@
 
 def tail(form, left, halo, image, devices):
     vectors, node = form.shape
-    each = image[0].shape[0] // vectors - 2
+    each = image.shape[0] // vectors - 2
     return pl.pallas_call(
         functools.partial(tail_kernel, each, vectors),
         out_shape=shaped((devices, node), f32),
-        in_specs=[vmem()] * (3 + len(image)),
+        in_specs=[vmem()] * 4,
         out_specs=vmem(),
         compiler_params=params(16),
         name="tail",
-    )(form, left, halo, *image)
+    )(form, left, halo, image)
 
 
 def code_tiles(each, node):
@@ -590,15 +587,20 @@
     )(keep, came)
 
 
-def decode_kernel(each, vectors, weighted, *refs):
-    if weighted:
-        code, came, drive, out = refs
-    else:
-        code, came, out = refs
+def decode_kernel(each, vectors, weighted, chained, *refs):
+    code, came, out = refs[0], refs[1], refs[-1]
+    drive = refs[2] if weighted else None
     node = code.shape[1]
     shape = (vectors, node)
     energy = jnp.zeros(shape, f32)
     cross = jnp.zeros(shape, f32)
+    if chained:
+        before = refs[-2]
+        at = each * vectors
+        if weighted:
+            cross = before[at : at + vectors, :]
+            at = at + vectors
+        energy = before[at : at + vectors, :]
     for group in range(code_tiles(each, node)):
         start = (each + group) * vectors
         gains = [
@@ -624,12 +626,12 @@
     out[at : at + vectors, :] = energy
 
 
-def decode(code, came, vectors, each, drive=None):
+def decode(code, came, vectors, each, drive=None, before=None):
     node = code.shape[1]
     extra = 1 if drive is None else 2
-    inputs = (code, came) if drive is None else (code, came, drive)
-    return pl.pallas_call(
-        functools.partial(decode_kernel, each, vectors, drive is not None),
+    inputs = [array for array in (code, came, drive, before) if array is not None]
+    return pl.pallas_call(
+        functools.partial(decode_kernel, each, vectors, drive is not None, before is not None),
         out_shape=shaped(((each + extra) * vectors, node), f32),
         in_specs=[vmem()] * len(inputs),
         out_specs=vmem(),
@@ -672,9 +674,7 @@
     arrays, message = refs[:-1], refs[-1]
     shape = (vectors, message.shape[1])
     lanes = lax.broadcasted_iota(i32, shape, 1)
-    sums = arrays[0][each * vectors :, :]
-    for array in arrays[1:]:
-        sums = sums + array[each * vectors :, :]
+    sums = arrays[CHUNKS - 1][each * vectors :, :] + arrays[2 * CHUNKS - 1][each * vectors :, :]
     energy = jnp.broadcast_to(row_sum(sums), shape)
     power = scale_power(energy)
     digits = energy * (FULL * scale_of(-power))
@@ -712,7 +712,12 @@
 
 
 def pack_rounded_kernel(each, vectors, groups, asked, *refs):
-    arrays, message = refs[:-1], refs[-1]
+    arrays, message, left, sems = refs[: 2 * CHUNKS], refs[2 * CHUNKS], refs[2 * CHUNKS + 1 : -1], refs[-1]
+    copies = [
+        pltpu.make_async_copy(array, place, sems.at[c]) for c, (array, place) in enumerate(zip(arrays[CHUNKS:], left))
+    ]
+    for copy in copies:
+        copy.start()
 
     def send(peer, carry):
         for k in range(CAP):
@@ -720,7 +725,9 @@
             message[tile(peer * CAP + k, vectors), :] = value.astype(bf16)
         return carry
 
-    lax.fori_loop(0, groups, send, 0)
+    lax.fori_loop(0, groups, send, 0, unroll=8)
+    for copy in copies:
+        copy.wait()
 
 
 def pack_rounded(asked, arrays, vectors):
@@ -729,22 +736,25 @@
     groups = lax.axis_size("curve")
     return pl.pallas_call(
         functools.partial(pack_rounded_kernel, each, vectors, groups),
-        out_shape=shaped((groups * CAP * vectors, node), bf16),
+        out_shape=[shaped((groups * CAP * vectors, node), bf16)] + [pltpu.HBM(arrays[0].shape, f32)] * CHUNKS,
         in_specs=[smem()] + [vmem()] * (2 * CHUNKS),
-        out_specs=vmem(),
+        out_specs=[vmem()] + [anywhere()] * CHUNKS,
+        scratch_shapes=[pltpu.SemaphoreType.DMA((CHUNKS,))],
         compiler_params=params(16),
         name="pack_rounded",
     )(asked, *arrays)
 
 
-def finish_kernel(shares, scale, state_in, drive_in, image_in, out, one, two, mix, state, drive, image, sems):
+def finish_kernel(shares, scale, state_in, drive_in, image_in, out, one, two, mix, state, drive, image, ready, sems):
+    places = ((state_in, state), (drive_in, drive), (image_in, image), (ready, out))
     copies = [
         [pltpu.make_async_copy(source.at[v], place.at[v], sems.at[k, v]) for v in range(out.shape[0])]
-        for k, (source, place) in enumerate(((state_in, state), (drive_in, drive), (image_in, image)))
+        for k, (source, place) in enumerate(places)
     ]
-    for column in copies:
-        for copy in column:
-            copy.start()
+    leaving = copies.pop()
+    for v in range(out.shape[0]):
+        for column in copies:
+            column[v].start()
     shape = scale.shape
     vectors = shape[0]
     line = jnp.sum(shares[...], axis=0, keepdims=True)
@@ -775,7 +785,10 @@
         weight_one, weight_two, share = [jnp.broadcast_to(ref[at, :], size) for ref in (one, two, mix)]
         for column in copies:
             column[v].wait()
-        out[v] = state[v] + (weight_one * drive[v] + weight_two * (image[v] - share * drive[v]))
+        ready[v] = state[v] + (weight_one * drive[v] + weight_two * (image[v] - share * drive[v]))
+        leaving[v].start()
+    for copy in leaving:
+        copy.wait()
 
 
 def finish(shares, scale, state, drive, image):
@@ -783,10 +796,10 @@
         finish_kernel,
         out_shape=shaped(state.shape, f32),
         in_specs=[vmem()] * 2 + [anywhere()] * 3,
-        out_specs=vmem(),
+        out_specs=anywhere(),
         scratch_shapes=[pltpu.VMEM(scale.shape, f32)] * 3
-        + [pltpu.VMEM(state.shape, f32)] * 3
-        + [pltpu.SemaphoreType.DMA((3, state.shape[0]))],
+        + [pltpu.VMEM(state.shape, f32)] * 4
+        + [pltpu.SemaphoreType.DMA((4, state.shape[0]))],
         compiler_params=params(16),
         name="finish",
     )(shares, scale, state, in_hbm(drive), in_hbm(image))
@@ -808,11 +821,11 @@
     across = []
     for code in codes:
         across.append(swap(code, 2))
-    mine = [
-        decode(code, other, vectors, each, None if drive is None else drive[c])
-        for c, (code, other) in enumerate(zip(codes, across))
-    ]
-    return mine + [swap(array, 1) for array in mine]
+    mine, others = [], []
+    for c, (code, other) in enumerate(zip(codes, across)):
+        mine.append(decode(code, other, vectors, each, drive and drive[c], mine[-1] if c else None))
+        others.append(swap(mine[c], 1))
+    return mine + others
 
 
 def body(state, blocks, diag_blocks, block_cols):
@@ -822,11 +835,10 @@
     vectors = width * lax.axis_size("band")
     blocks = in_hbm(blocks)
     diag_blocks = in_hbm(diag_blocks)
-    rounded = state.astype(bf16)
     state = in_hbm(state)
+    rounded, pick, target, wanted, origin = plan(block_cols.reshape(1, rows), state)
     across = swap(rounded, 2)
     beside = swap(rounded, 1)
-    pick, target, wanted, origin = plan(block_cols.reshape(1, rows))
     asked = exchange(wanted)
     corner = swap(across, 1)
     parts = [rounded, beside, across, corner]
@@ -840,11 +852,13 @@
     halo = exchange(pack(asked, origin, drive, vectors))
     keep, give, scale = operate_second(pick, target, asked, drive, halo, arrived, blocks, diag_blocks)
     image = band_sum(keep, give, vectors, drive)
-    halo = exchange(pack_rounded(asked, image, vectors))
+    message, *left = pack_rounded(asked, image, vectors)
+    halo = exchange(message)
+    image = image[:CHUNKS] + left
     form, left, drive_own, image_own = operate_third(
         pick, wanted, origin, drive, image, own, blocks, diag_blocks, width, vectors
     )
-    share = tail(form, left, halo, image[:CHUNKS], devices)
+    share = tail(form, left, halo, image[CHUNKS - 1], devices)
     shares = lax.all_to_all(share, ("curve", "band"), split_axis=0, concat_axis=0, tiled=True)
     return finish(shares, scale, state, drive_own, image_own)
 

time: 132 us -> 132 us (level)
  Pallas kernels: 38.5 us -> 40 us
  local copies, waits for them, and re-layouts: 1.5 us -> 0 us
    unnamed x6 -> x0, local copies, waits for them, and re-layouts: 1.5 us -> none
  transfers between devices with their start and end apart: 19 -> 19, of which waited for: 10 -> 12; matrix products, arithmetic and copies ran while one was open for 0% -> 0% of each run, Pallas kernels for 18% -> 17%
where the time goes in v6:
time: 132 us; the launch traced here: 131 us
  Pallas kernels  40 us (30%)
  waiting for transfers between devices  37.7 us (29%)
  starting transfers between devices  27.4 us (21%)
  blocking collectives  26.2 us (20%)
    ppermute x15, waiting for transfers between devices, swap(): return lax.ppermute(array, 'band', [(k, k ^ bit) for k in range(size)])  33.8 us
    all_to_all x4, starting transfers between devices, exchange(): lax.all_to_all(array, 'curve', split_axis=0, concat_axis=0, tiled=True)  17.9 us
    all_to_all x1, blocking collectives, exchange(): lax.all_to_all(array, 'curve', split_axis=0, concat_axis=0, tiled=True)  13.3 us
    all_to_all x1, blocking collectives, body(): lax.all_to_all(share, ('curve', 'band'), split_axis=0, concat_axis=0, til...  12.9 us
    ppermute x15, starting transfers between devices, swap(): return lax.ppermute(array, 'band', [(k, k ^ bit) for k in range(size)])  9.5 us
    pallas_call x1, Pallas kernels, operate_local(): pl.pallas_call(functools.partial(local_kernel, rows, vectors), out_shape=...  6.89 us
    pallas_call x1, Pallas kernels, operate_third(): pl.pallas_call(functools.partial(third_kernel, rows, vectors, groups, wid...  6.8 us
    pallas_call x1, Pallas kernels, operate_second(): pl.pallas_call(functools.partial(second_kernel, rows, vectors, groups), o...  6.52 us
  transfers between devices with their start and end apart: 19, of which 12 were waited for; matrix products, arithmetic and copies ran while one was open for 0% of the time, Pallas kernels for 17%

profile of v6, /device:TPU:0, one launch (start us, length us, event | category | flops | bytes accessed | tf_op | source)
XLA Modules:
  0.0 131.5 jit_solution(2578340214299168775)
XLA Ops:
  0.0 1.9 %plan.1 = (bf16[4,256,128]{2,1,0:T(8,128)(2,1)S(1)}, s32[1,256]{1,0:T(1,128)S(1)}, s32[1,256]{1,0:T(1,128)S(1)}, s32[8,128]{1,0:T(8,128)}, s32[8,128]{1,0:T(8,128)S(1)}) custom-call(s32[1,256]{1,0:T(1,128)} %bitcast.26, f32[4,256,128]{2,1,0:T(8,128)} %state_in.1), custom_call_target="tpu_custom_call" | custom-call | tf_op jit(solution)/shard_map/plan/pallas_call | solution.py:130
  1.9 3.0 %collective-permute-start.1 = (bf16[4,256,128]{2,1,0:T(8,128)(2,1)S(1)}, bf16[4,256,128]{2,1,0:T(8,128)(2,1)S(1)}, u32[]{:S(2)}, u32[]{:S(2)}) collective-permute-start(bf16[4,256,128]{2,1,0:T(8,128)(2,1)S(1)} %get-tuple-element.33.refs_0_), channel_id=1, source_target_pairs={{0,2},{1,3},{2,0},{3,1},{4,6},{5,7},{6,4},{7,5},{8,10},{9,11},{10,... | collective-permute-start | bytes 786440 | tf_op jit(solution)/shard_map/ppermute | solution.py:810
  4.9 6.3 %collective-permute-done.1.refs_2_ = bf16[4,256,128]{2,1,0:T(8,128)(2,1)S(1)} collective-permute-done((bf16[4,256,128]{2,1,0:T(8,128)(2,1)S(1)}, bf16[4,256,128]{2,1,0:T(8,128)(2,1)S(1)}, u32[]{:S(2)}, u32[]{:S(2)}) %collective-permute-start.1) | collective-permute-done | bytes 262176 | tf_op jit(solution)/shard_map/ppermute | solution.py:810
  11.2 6.1 %all-to-all-start = ((s32[8,1,128]{2,1,0:T(1,128)}), s32[8,1,128]{2,1,0:T(1,128)S(1)}, u32[]{:S(2)}, u32[]{:S(2)}) async-start(s32[8,1,128]{2,1,0:T(1,128)} %bitcast.2), calls=%async_computation | async-start | bytes 8192 | tf_op jit(solution)/shard_map/all_to_all | solution.py:814
  17.3 3.4 %spread.1 = (bf16[4112,128]{1,0:T(8,128)(2,1)}, bf16[16,128,128]{2,1,0:T(8,128)(2,1)}, bf16[512,128]{1,0:T(8,128)(2,1)S(1)}) custom-call(s32[8,128]{1,0:T(8,128)S(1)} %get-tuple-element.31.origin, bf16[256,1,128,128]{3,2,1,0:T(8,128)(2,1)} %refs_9_.1, bf16[4,256,128]{2,1,0:T(8,128)(2,1)S(1)} %get-tuple-element.33.refs_0_, ...), custom_call_target="tpu_custom_call" | custom-call | tf_op jit(solution)/shard_map/spread/pallas_call | solution.py:185
  20.7 3.1 %all-to-all-done = s32[8,1,128]{2,1,0:T(1,128)S(1)} async-done(((s32[8,1,128]{2,1,0:T(1,128)}), s32[8,1,128]{2,1,0:T(1,128)S(1)}, u32[]{:S(2)}, u32[]{:S(2)}) %all-to-all-start) | async-done | bytes 4128 | tf_op jit(solution)/shard_map/all_to_all | solution.py:814
  23.8 1.9 %reply.1 = bf16[768,128]{1,0:T(8,128)(2,1)} custom-call(s32[8,128]{1,0:T(8,128)S(1)} %bitcast.19, bf16[4112,128]{1,0:T(8,128)(2,1)} %get-tuple-element.34.field, bf16[512,128]{1,0:T(8,128)(2,1)S(1)} %get-tuple-element.35.split), custom_call_target="tpu_custom_call" | custom-call | tf_op jit(solution)/shard_map/reply/pallas_call | solution.py:214
  25.7 3.4 %all-to-all-start.1 = ((bf16[8,96,128]{2,1,0:T(8,128)(2,1)}), bf16[8,96,128]{2,1,0:T(8,128)(2,1)S(1)}, u32[]{:S(2)}, u32[]{:S(2)}) async-start(bf16[8,96,128]{2,1,0:T(8,128)(2,1)} %bitcast.4), calls=%async_computation.1 | async-start | bytes 393216 | tf_op jit(solution)/shard_map/all_to_all | solution.py:814
  29.1 6.9 %operate_local.1.local = f32[4112,128]{1,0:T(8,128)S(1)} custom-call(s32[1,256]{1,0:T(1,128)S(1)} %get-tuple-element.29.pick, s32[1,256]{1,0:T(1,128)S(1)} %get-tuple-element.32.target, bf16[4112,128]{1,0:T(8,128)(2,1)} %get-tuple-element.34.field, f32[4,256,128]{2,1,0:T(8,128)} %state_in.1, bf16[256,1,128,128]{3,2,1,0:T(8,128)(2,1)} %refs_9_.1, ...), custom_call_target="tpu_custom_call" | custom-call | tf_op jit(solution)/shard_map/operate_local/pallas_call | solution.py:314
  36.8 2.6 %settle.1 = (f32[1024,128]{1,0:T(8,128)S(1)}, f32[1024,128]{1,0:T(8,128)S(1)}, f32[1024,128]{1,0:T(8,128)}, f32[1024,128]{1,0:T(8,128)}) custom-call(s32[8,128]{1,0:T(8,128)} %get-tuple-element.30.wanted, s32[8,128]{1,0:T(8,128)S(1)} %get-tuple-element.31.origin, s32[8,128]{1,0:T(8,128)S(1)} %bitcast.20, f32[4112,128]{1,0:T(8,128)S(1)} %operate_local.1.local, ...), custom_call_target="tpu_custom_call" | custom-call | tf_op jit(solution)/shard_map/settle/pallas_call | solution.py:355
  39.9 5.1 %all-to-all-start.3 = ((bf16[16,128,128]{2,1,0:T(8,128)(2,1)}), bf16[16,128,128]{2,1,0:T(8,128)(2,1)S(1)}, u32[]{:S(2)}, u32[]{:S(2)}) async-start(bf16[16,128,128]{2,1,0:T(8,128)(2,1)} %get-tuple-element.36.own.refs_8_), calls=%async_computation.3 | async-start | bytes 1048576 | tf_op jit(solution)/shard_map/all_to_all | solution.py:814
  45.6 1.6 %collective-permute-start.4 = (s16[1040,128]{1,0:T(8,128)(2,1)S(1)}, s16[1040,128]{1,0:T(8,128)(2,1)S(1)}, u32[]{:S(2)}, u32[]{:S(2)}) collective-permute-start(s16[1040,128]{1,0:T(8,128)(2,1)S(1)} %encode.4.refs_0_), channel_id=1, source_target_pairs={{0,2},{1,3},{2,0},{3,1},{4,6},{5,7},{6,4},{7,5},{8,10},{9,11},{10,... | collective-permute-start | bytes 798728 | tf_op jit(solution)/shard_map/ppermute | solution.py:810
  48.3 6.6 %collective-permute-done.4.refs_1_ = s16[1040,128]{1,0:T(8,128)(2,1)S(1)} collective-permute-done((s16[1040,128]{1,0:T(8,128)(2,1)S(1)}, s16[1040,128]{1,0:T(8,128)(2,1)S(1)}, u32[]{:S(2)}, u32[]{:S(2)}) %collective-permute-start.4) | collective-permute-done | bytes 266272 | tf_op jit(solution)/shard_map/ppermute | solution.py:810
  55.3 4.0 %collective-permute-done.6.refs_1_ = s16[1040,128]{1,0:T(8,128)(2,1)S(1)} collective-permute-done((s16[1040,128]{1,0:T(8,128)(2,1)S(1)}, s16[1040,128]{1,0:T(8,128)(2,1)S(1)}, u32[]{:S(2)}, u32[]{:S(2)}) %collective-permute-start.6) | collective-permute-done | bytes 266272 | tf_op jit(solution)/shard_map/ppermute | solution.py:810
  64.0 13.3 %all_to_all.60 = s16[8,80,128]{2,1,0:T(8,128)(2,1)S(1)} all-to-all(s16[8,80,128]{2,1,0:T(8,128)(2,1)S(1)} %bitcast.16), channel_id=1, replica_groups=mesh['curve'=8,'band'=4] {'curve'}, dimensions={0} | all-to-all | bytes 327680 | tf_op jit(solution)/shard_map/all_to_all | solution.py:814
  77.3 6.5 %operate_second.1 = (f32[1024,128]{1,0:T(8,128)S(1)}, f32[1024,128]{1,0:T(8,128)S(1)}, f32[1024,128]{1,0:T(8,128)S(1)}, f32[1024,128]{1,0:T(8,128)S(1)}, f32[16,128]{1,0:T(8,128)S(1)}) custom-call(s32[1,256]{1,0:T(1,128)S(1)} %get-tuple-element.29.pick, s32[1,256]{1,0:T(1,128)S(1)} %get-tuple-element.32.target, s32[8,128]{1,0:T(8,128)S(1)} %bitcast.22, ...), custom_call_target="tpu_custom_call" | custom-call | tf_op jit(solution)/shard_map/operate_second/pallas_call | solution.py:426
  86.3 1.6 %collective-permute-start.10 = (s16[1040,128]{1,0:T(8,128)(2,1)S(1)}, s16[1040,128]{1,0:T(8,128)(2,1)S(1)}, u32[]{:S(2)}, u32[]{:S(2)}) collective-permute-start(s16[1040,128]{1,0:T(8,128)(2,1)S(1)} %encode.6.refs_0_), channel_id=1, source_target_pairs={{0,2},{1,3},{2,0},{3,1},{4,6},{5,7},{6,4},{7,5},{8,10},{9,11},{10,... | collective-permute-start | bytes 798728 | tf_op jit(solution)/shard_map/ppermute | solution.py:810
  89.0 6.6 %collective-permute-done.10.refs_1_ = s16[1040,128]{1,0:T(8,128)(2,1)S(1)} collective-permute-done((s16[1040,128]{1,0:T(8,128)(2,1)S(1)}, s16[1040,128]{1,0:T(8,128)(2,1)S(1)}, u32[]{:S(2)}, u32[]{:S(2)}) %collective-permute-start.10) | collective-permute-done | bytes 266272 | tf_op jit(solution)/shard_map/ppermute | solution.py:810
  96.1 4.4 %collective-permute-done.12.refs_1_ = s16[1040,128]{1,0:T(8,128)(2,1)S(1)} collective-permute-done((s16[1040,128]{1,0:T(8,128)(2,1)S(1)}, s16[1040,128]{1,0:T(8,128)(2,1)S(1)}, u32[]{:S(2)}, u32[]{:S(2)}) %collective-permute-start.12) | collective-permute-done | bytes 266272 | tf_op jit(solution)/shard_map/ppermute | solution.py:810
  103.8 2.2 %pack_rounded.1 = (bf16[256,128]{1,0:T(8,128)(2,1)}, f32[1056,128]{1,0:T(8,128)}, f32[1056,128]{1,0:T(8,128)}) custom-call(s32[8,128]{1,0:T(8,128)S(1)} %bitcast.23, f32[1056,128]{1,0:T(8,128)S(1)} %decode.6.refs_3_.refs_0_.refs_4_, f32[1056,128]{1,0:T(8,128)S(1)} %decode.7.refs_1_.refs_5_.image, f32[1056,128]{1,0:T(8,128)S(1)} %collective-permute-done.13.refs_2_, ...), custom_call_target="tpu_custom_call" | custom-call | tf_op jit(solution)/shard_map/pack_rounded/pallas_call | solution.py:737
  106.0 3.4 %all-to-all-start.4 = ((bf16[8,32,128]{2,1,0:T(8,128)(2,1)}), bf16[8,32,128]{2,1,0:T(8,128)(2,1)S(1)}, u32[]{:S(2)}, u32[]{:S(2)}) async-start(bf16[8,32,128]{2,1,0:T(8,128)(2,1)} %bitcast.8), calls=%async_computation.4 | async-start | bytes 131072 | tf_op jit(solution)/shard_map/all_to_all | solution.py:814
  109.4 6.8 %operate_third.1 = (f32[16,128]{1,0:T(8,128)S(1)}, f32[256,128]{1,0:T(8,128)S(1)}, f32[4,256,128]{2,1,0:T(8,128)}, f32[4,256,128]{2,1,0:T(8,128)}) custom-call(s32[1,256]{1,0:T(1,128)S(1)} %get-tuple-element.29.pick, s32[8,128]{1,0:T(8,128)} %get-tuple-element.30.wanted, s32[8,128]{1,0:T(8,128)S(1)} %get-tuple-element.31.origin, ...), custom_call_target="tpu_custom_call" | custom-call | tf_op jit(solution)/shard_map/operate_third/pallas_call | solution.py:507
  116.3 12.9 %all_to_all.61 = f32[32,1,128]{2,1,0:T(1,128)S(1)} all-to-all(f32[32,1,128]{2,1,0:T(1,128)S(1)} %bitcast.25), channel_id=1, replica_groups=mesh['curve'=8,'band'=4] {'curve','band'}, dimensions={0} | all-to-all | bytes 32768 | tf_op jit(solution)/shard_map/all_to_all | solution.py:862
  129.2 2.3 %finish.1 = f32[4,256,128]{2,1,0:T(8,128)} custom-call(f32[32,128]{1,0:T(8,128)S(1)} %bitcast.24, f32[16,128]{1,0:T(8,128)S(1)} %get-tuple-element.50.scale, f32[4,256,128]{2,1,0:T(8,128)} %state_in.1, f32[4,256,128]{2,1,0:T(8,128)} %get-tuple-element.51.drive_in, f32[4,256,128]{2,1,0:T(8,128)} %get-tuple-element.52.image_in), custom_call_target="tpu_custom_call" | custom-call | tf_op jit(solution)/shard_map/finish/pallas_call | solution.py:795
  (35 shorter events, 15.5 us)
Async XLA Ops:
  1.9 9.3 %collective-permute-start.1 = (bf16[4,256,128]{2,1,0:T(8,128)(2,1)S(1)}, bf16[4,256,128]{2,1,0:T(8,128)(2,1)S(1)}, u32[]{:S(2)}, u32[]{:S(2)}) collective-permute-start(bf16[4,256,128]{2,1,0:T(8,128)(2,1)S(1)} %get-tuple-element.33.refs_0_), channel_id=1, source_target_pairs={{0,2},{1,3},{2,0},{3,1},{4,6},{5,7},{6,4},{7,5},{8,10},{9,11},{10,... | collective-permute-start | bytes 786440 | tf_op jit(solution)/shard_map/ppermute | solution.py:810
  4.9 12.4 %collective-permute-start = (bf16[4,256,128]{2,1,0:T(8,128)(2,1)S(1)}, bf16[4,256,128]{2,1,0:T(8,128)(2,1)S(1)}, u32[]{:S(2)}, u32[]{:S(2)}) collective-permute-start(bf16[4,256,128]{2,1,0:T(8,128)(2,1)S(1)} %get-tuple-element.33.refs_0_), channel_id=1, source_target_pairs={{0,1},{1,0},{2,3},{3,2},{4,5},{5,4},{6,7},{7,6},{8,9},{9,8},{10,11... | collective-permute-start | bytes 786440 | tf_op jit(solution)/shard_map/ppermute | solution.py:810
  11.2 6.1 %collective-permute-start.2 = (bf16[4,256,128]{2,1,0:T(8,128)(2,1)S(1)}, bf16[4,256,128]{2,1,0:T(8,128)(2,1)S(1)}, u32[]{:S(2)}, u32[]{:S(2)}) collective-permute-start(bf16[4,256,128]{2,1,0:T(8,128)(2,1)S(1)} %collective-permute-done.1.refs_2_), channel_id=1, source_target_pairs={{0,1},{1,0},{2,3},{3,2},{4,5},{5,4},{6,7},{7,6},{8,9},{9,8},{10,11... | collective-permute-start | bytes 786440 | tf_op jit(solution)/shard_map/ppermute | solution.py:810
  11.2 12.6 %all-to-all-start = ((s32[8,1,128]{2,1,0:T(1,128)}), s32[8,1,128]{2,1,0:T(1,128)S(1)}, u32[]{:S(2)}, u32[]{:S(2)}) async-start(s32[8,1,128]{2,1,0:T(1,128)} %bitcast.2), calls=%async_computation | async-start | bytes 8192 | tf_op jit(solution)/shard_map/all_to_all | solution.py:814
  25.7 11.1 %all-to-all-start.1 = ((bf16[8,96,128]{2,1,0:T(8,128)(2,1)}), bf16[8,96,128]{2,1,0:T(8,128)(2,1)S(1)}, u32[]{:S(2)}, u32[]{:S(2)}) async-start(bf16[8,96,128]{2,1,0:T(8,128)(2,1)} %bitcast.4), calls=%async_computation.1 | async-start | bytes 393216 | tf_op jit(solution)/shard_map/all_to_all | solution.py:814
  39.4 5.6 %collective-permute-start.3 = (f32[1024,128]{1,0:T(8,128)}, f32[1024,128]{1,0:T(8,128)S(1)}, u32[]{:S(2)}, u32[]{:S(2)}) collective-permute-start(f32[1024,128]{1,0:T(8,128)} %get-tuple-element.38), channel_id=1, source_target_pairs={{0,1},{1,0},{2,3},{3,2},{4,5},{5,4},{6,7},{7,6},{8,9},{9,8},{10,11... | collective-permute-start | bytes 1572872 | tf_op jit(solution)/shard_map/ppermute | solution.py:810
  39.4 7.7 %collective-permute-start.5 = (f32[1024,128]{1,0:T(8,128)}, f32[1024,128]{1,0:T(8,128)S(1)}, u32[]{:S(2)}, u32[]{:S(2)}) collective-permute-start(f32[1024,128]{1,0:T(8,128)} %get-tuple-element.40), channel_id=1, source_target_pairs={{0,1},{1,0},{2,3},{3,2},{4,5},{5,4},{6,7},{7,6},{8,9},{9,8},{10,11... | collective-permute-start | bytes 1572872 | tf_op jit(solution)/shard_map/ppermute | solution.py:810
  39.9 24.1 %all-to-all-start.3 = ((bf16[16,128,128]{2,1,0:T(8,128)(2,1)}), bf16[16,128,128]{2,1,0:T(8,128)(2,1)S(1)}, u32[]{:S(2)}, u32[]{:S(2)}) async-start(bf16[16,128,128]{2,1,0:T(8,128)(2,1)} %get-tuple-element.36.own.refs_8_), calls=%async_computation.3 | async-start | bytes 1048576 | tf_op jit(solution)/shard_map/all_to_all | solution.py:814
  45.6 9.3 %collective-permute-start.4 = (s16[1040,128]{1,0:T(8,128)(2,1)S(1)}, s16[1040,128]{1,0:T(8,128)(2,1)S(1)}, u32[]{:S(2)}, u32[]{:S(2)}) collective-permute-start(s16[1040,128]{1,0:T(8,128)(2,1)S(1)} %encode.4.refs_0_), channel_id=1, source_target_pairs={{0,2},{1,3},{2,0},{3,1},{4,6},{5,7},{6,4},{7,5},{8,10},{9,11},{10,... | collective-permute-start | bytes 798728 | tf_op jit(solution)/shard_map/ppermute | solution.py:810
  47.7 11.7 %collective-permute-start.6 = (s16[1040,128]{1,0:T(8,128)(2,1)S(1)}, s16[1040,128]{1,0:T(8,128)(2,1)S(1)}, u32[]{:S(2)}, u32[]{:S(2)}) collective-permute-start(s16[1040,128]{1,0:T(8,128)(2,1)S(1)} %encode.5.refs_0_), channel_id=1, source_target_pairs={{0,2},{1,3},{2,0},{3,1},{4,6},{5,7},{6,4},{7,5},{8,10},{9,11},{10,... | collective-permute-start | bytes 798728 | tf_op jit(solution)/shard_map/ppermute | solution.py:810
  59.8 2.0 %collective-permute-start.8 = (f32[1040,128]{1,0:T(8,128)S(1)}, f32[1040,128]{1,0:T(8,128)S(1)}, u32[]{:S(2)}, u32[]{:S(2)}) collective-permute-start(f32[1040,128]{1,0:T(8,128)S(1)} %decode.5.refs_1_.refs_2_), channel_id=1, source_target_pairs={{0,1},{1,0},{2,3},{3,2},{4,5},{5,4},{6,7},{7,6},{8,9},{9,8},{10,11... | collective-permute-start | bytes 1597448 | tf_op jit(solution)/shard_map/ppermute | solution.py:810
  59.9 2.7 %collective-permute-start.7 = (f32[1040,128]{1,0:T(8,128)S(1)}, f32[1040,128]{1,0:T(8,128)S(1)}, u32[]{:S(2)}, u32[]{:S(2)}) collective-permute-start(f32[1040,128]{1,0:T(8,128)S(1)} %decode.4.refs_2_.refs_0_), channel_id=1, source_target_pairs={{0,1},{1,0},{2,3},{3,2},{4,5},{5,4},{6,7},{7,6},{8,9},{9,8},{10,11... | collective-permute-start | bytes 1597448 | tf_op jit(solution)/shard_map/ppermute | solution.py:810
  83.8 2.0 %collective-permute-start.9 = (f32[1024,128]{1,0:T(8,128)S(1)}, f32[1024,128]{1,0:T(8,128)S(1)}, u32[]{:S(2)}, u32[]{:S(2)}) collective-permute-start(f32[1024,128]{1,0:T(8,128)S(1)} %get-tuple-element.42), channel_id=1, source_target_pairs={{0,1},{1,0},{2,3},{3,2},{4,5},{5,4},{6,7},{7,6},{8,9},{9,8},{10,11... | collective-permute-start | bytes 1572872 | tf_op jit(solution)/shard_map/ppermute | solution.py:810
  83.9 4.0 %collective-permute-start.11 = (f32[1024,128]{1,0:T(8,128)S(1)}, f32[1024,128]{1,0:T(8,128)S(1)}, u32[]{:S(2)}, u32[]{:S(2)}) collective-permute-start(f32[1024,128]{1,0:T(8,128)S(1)} %get-tuple-element.44), channel_id=1, source_target_pairs={{0,1},{1,0},{2,3},{3,2},{4,5},{5,4},{6,7},{7,6},{8,9},{9,8},{10,11... | collective-permute-start | bytes 1572872 | tf_op jit(solution)/shard_map/ppermute | solution.py:810
  86.3 9.3 %collective-permute-start.10 = (s16[1040,128]{1,0:T(8,128)(2,1)S(1)}, s16[1040,128]{1,0:T(8,128)(2,1)S(1)}, u32[]{:S(2)}, u32[]{:S(2)}) collective-permute-start(s16[1040,128]{1,0:T(8,128)(2,1)S(1)} %encode.6.refs_0_), channel_id=1, source_target_pairs={{0,2},{1,3},{2,0},{3,1},{4,6},{5,7},{6,4},{7,5},{8,10},{9,11},{10,... | collective-permute-start | bytes 798728 | tf_op jit(solution)/shard_map/ppermute | solution.py:810
  88.4 12.1 %collective-permute-start.12 = (s16[1040,128]{1,0:T(8,128)(2,1)S(1)}, s16[1040,128]{1,0:T(8,128)(2,1)S(1)}, u32[]{:S(2)}, u32[]{:S(2)}) collective-permute-start(s16[1040,128]{1,0:T(8,128)(2,1)S(1)} %encode.7.refs_0_), channel_id=1, source_target_pairs={{0,2},{1,3},{2,0},{3,1},{4,6},{5,7},{6,4},{7,5},{8,10},{9,11},{10,... | collective-permute-start | bytes 798728 | tf_op jit(solution)/shard_map/ppermute | solution.py:810
  101.0 2.0 %collective-permute-start.14 = (f32[1056,128]{1,0:T(8,128)S(1)}, f32[1056,128]{1,0:T(8,128)S(1)}, u32[]{:S(2)}, u32[]{:S(2)}) collective-permute-start(f32[1056,128]{1,0:T(8,128)S(1)} %decode.7.refs_1_.refs_5_.image), channel_id=1, source_target_pairs={{0,1},{1,0},{2,3},{3,2},{4,5},{5,4},{6,7},{7,6},{8,9},{9,8},{10,11... | collective-permute-start | bytes 1622024 | tf_op jit(solution)/shard_map/ppermute | solution.py:810
  101.1 2.7 %collective-permute-start.13 = (f32[1056,128]{1,0:T(8,128)S(1)}, f32[1056,128]{1,0:T(8,128)S(1)}, u32[]{:S(2)}, u32[]{:S(2)}) collective-permute-start(f32[1056,128]{1,0:T(8,128)S(1)} %decode.6.refs_3_.refs_0_.refs_4_), channel_id=1, source_target_pairs={{0,1},{1,0},{2,3},{3,2},{4,5},{5,4},{6,7},{7,6},{8,9},{9,8},{10,11... | collective-permute-start | bytes 1622024 | tf_op jit(solution)/shard_map/ppermute | solution.py:810
  106.0 10.2 %all-to-all-start.4 = ((bf16[8,32,128]{2,1,0:T(8,128)(2,1)}), bf16[8,32,128]{2,1,0:T(8,128)(2,1)S(1)}, u32[]{:S(2)}, u32[]{:S(2)}) async-start(bf16[8,32,128]{2,1,0:T(8,128)(2,1)} %bitcast.8), calls=%async_computation.4 | async-start | bytes 131072 | tf_op jit(solution)/shard_map/all_to_all | solution.py:814

commit v7 on v6

--- a/solution.py
+++ b/solution.py
@@ -185,14 +185,14 @@
     return pl.pallas_call(
         functools.partial(spread_kernel, rows, vectors, groups, width),
         out_shape=[
-            pltpu.HBM(((rows + 1) * vectors, node), bf16),
+            shaped(((rows + 1) * vectors, node), bf16),
             shaped((slots, node, node), bf16),
             shaped((slots * 2 * vectors, node), bf16),
         ],
         in_specs=[smem(), anywhere()] + [vmem()] * len(parts),
         out_specs=[vmem()] * 3,
         scratch_shapes=[pltpu.VMEM((rows * vectors, node), f32), pltpu.SemaphoreType.DMA((slots,))],
-        compiler_params=params(16),
+        compiler_params=params(10),
         name="spread",
     )(origin, blocks, *parts)
 
@@ -216,9 +216,9 @@
         out_shape=shaped((groups * 3 * CAP * vectors, field.shape[1]), bf16),
         in_specs=[smem()] + [vmem()] * 2,
         out_specs=vmem(),
-        compiler_params=params(16),
+        compiler_params=params(10),
         name="reply",
-    )(asked, in_hbm(field), split)
+    )(asked, field, split)
 
 
 class Stream:
@@ -317,9 +317,9 @@
         in_specs=[smem()] * 2 + [vmem()] * 2 + [anywhere()] * 2,
         out_specs=vmem(),
         scratch_shapes=stream_scratch(blocks, diag),
-        compiler_params=params(20),
+        compiler_params=params(17),
         name="operate_local",
-    )(pick, target, in_hbm(field), state, blocks, diag)
+    )(pick, target, field, state, blocks, diag)
 
 
 def settle_kernel(rows, vectors, groups, wanted, origin, asked, local, halo, own, *refs):
@@ -358,7 +358,7 @@
         in_specs=[smem()] * 3 + [vmem()] * 3,
         out_specs=[vmem()] * (2 * CHUNKS),
         scratch_shapes=[pltpu.VMEM(local.shape, f32)],
-        compiler_params=params(20),
+        compiler_params=params(17),
         name="settle",
     )(wanted, origin, asked, local, halo, own)
     return outs[:CHUNKS], outs[CHUNKS:]
@@ -433,7 +433,7 @@
             pltpu.VMEM(((rows + 1) * vectors, node), f32),
         ]
         + stream_scratch(blocks, diag),
-        compiler_params=params(22),
+        compiler_params=params(18),
         name="operate_second",
     )(pick, target, asked, *arrays, halo, arrived, blocks, diag)
     return outs[:CHUNKS], outs[CHUNKS : 2 * CHUNKS], outs[-1]
@@ -510,7 +510,7 @@
         in_specs=[smem()] * 3 + [vmem()] * (4 * CHUNKS + 1) + [anywhere()] * 2,
         out_specs=[vmem()] * 4,
         scratch_shapes=[pltpu.VMEM(((rows + 1) * vectors, node), bf16)] + stream_scratch(blocks, diag),
-        compiler_params=params(22),
+        compiler_params=params(18),
         name="operate_third",
     )(pick, wanted, origin, *drive, *image[:CHUNKS], *map(in_hbm, image[CHUNKS:]), own, blocks, diag)
 
@@ -542,7 +542,7 @@
         out_shape=shaped((devices, node), f32),
         in_specs=[vmem()] * 4,
         out_specs=vmem(),
-        compiler_params=params(16),
+        compiler_params=params(10),
         name="tail",
     )(form, left, halo, image)
 
@@ -582,7 +582,7 @@
         in_specs=[vmem()] * 2,
         out_specs=vmem(),
         scratch_shapes=[pltpu.VMEM((size, node), f32)],
-        compiler_params=params(12),
+        compiler_params=params(6),
         name="encode",
     )(keep, came)
 
@@ -635,7 +635,7 @@
         out_shape=shaped(((each + extra) * vectors, node), f32),
         in_specs=[vmem()] * len(inputs),
         out_specs=vmem(),
-        compiler_params=params(12),
+        compiler_params=params(6),
         name="decode",
     )(*inputs)
 
@@ -706,7 +706,7 @@
         out_shape=shaped((groups * (2 * CAP + 1) * vectors, node), jnp.int16),
         in_specs=[smem()] * 2 + [vmem()] * (2 * CHUNKS),
         out_specs=vmem(),
-        compiler_params=params(16),
+        compiler_params=params(10),
         name="pack",
     )(asked, origin, *arrays)
 
@@ -740,7 +740,7 @@
         in_specs=[smem()] + [vmem()] * (2 * CHUNKS),
         out_specs=[vmem()] + [anywhere()] * CHUNKS,
         scratch_shapes=[pltpu.SemaphoreType.DMA((CHUNKS,))],
-        compiler_params=params(16),
+        compiler_params=params(10),
         name="pack_rounded",
     )(asked, *arrays)
 
@@ -800,7 +800,7 @@
         scratch_shapes=[pltpu.VMEM(scale.shape, f32)] * 3
         + [pltpu.VMEM(state.shape, f32)] * 4
         + [pltpu.SemaphoreType.DMA((4, state.shape[0]))],
-        compiler_params=params(16),
+        compiler_params=params(10),
         name="finish",
     )(shares, scale, state, in_hbm(drive), in_hbm(image))
 

time: 132 us -> 133 us (level)
  local copies, waits for them, and re-layouts: 0 us -> 1.84 us
    unnamed x0 -> x4, local copies, waits for them, and re-layouts: none -> 1.84 us
  transfers between devices with their start and end apart: 19 -> 19, of which waited for: 12 -> 12; matrix products, arithmetic and copies ran while one was open for 0% -> 0% of each run, Pallas kernels for 17% -> 16%
where the time goes in v7:
time: 133 us; the launch traced here: 132 us
  Pallas kernels  38.8 us (29%)
  waiting for transfers between devices  38.3 us (29%)
  starting transfers between devices  27.1 us (20%)
  blocking collectives  26.2 us (20%)
  local copies, waits for them, and re-layouts  1.84 us (1%)
    ppermute x15, waiting for transfers between devices, swap(): return lax.ppermute(array, 'band', [(k, k ^ bit) for k in range(size)])  33.8 us
    all_to_all x4, starting transfers between devices, exchange(): lax.all_to_all(array, 'curve', split_axis=0, concat_axis=0, tiled=True)  17.6 us
    all_to_all x1, blocking collectives, exchange(): lax.all_to_all(array, 'curve', split_axis=0, concat_axis=0, tiled=True)  13.3 us
    all_to_all x1, blocking collectives, body(): lax.all_to_all(share, ('curve', 'band'), split_axis=0, concat_axis=0, til...  12.9 us
    ppermute x15, starting transfers between devices, swap(): return lax.ppermute(array, 'band', [(k, k ^ bit) for k in range(size)])  9.5 us
    pallas_call x1, Pallas kernels, operate_third(): pl.pallas_call(functools.partial(third_kernel, rows, vectors, groups, wid...  6.81 us
    pallas_call x1, Pallas kernels, operate_local(): pl.pallas_call(functools.partial(local_kernel, rows, vectors), out_shape=...  6.55 us
    pallas_call x1, Pallas kernels, operate_second(): pl.pallas_call(functools.partial(second_kernel, rows, vectors, groups), o...  6.52 us
  transfers between devices with their start and end apart: 19, of which 12 were waited for; matrix products, arithmetic and copies ran while one was open for 0% of the time, Pallas kernels for 16%

profile of v7, /device:TPU:0, one launch (start us, length us, event | category | flops | bytes accessed | tf_op | source)
XLA Modules:
  0.0 132.4 jit_solution(16108387778697598465)
XLA Ops:
  0.0 1.9 %plan.1 = (bf16[4,256,128]{2,1,0:T(8,128)(2,1)S(1)}, s32[1,256]{1,0:T(1,128)S(1)}, s32[1,256]{1,0:T(1,128)S(1)}, s32[8,128]{1,0:T(8,128)}, s32[8,128]{1,0:T(8,128)S(1)}) custom-call(s32[1,256]{1,0:T(1,128)} %bitcast.26, f32[4,256,128]{2,1,0:T(8,128)} %state_in.1), custom_call_target="tpu_custom_call" | custom-call | tf_op jit(solution)/shard_map/plan/pallas_call | solution.py:130
  1.9 3.0 %collective-permute-start.1 = (bf16[4,256,128]{2,1,0:T(8,128)(2,1)S(1)}, bf16[4,256,128]{2,1,0:T(8,128)(2,1)S(1)}, u32[]{:S(2)}, u32[]{:S(2)}) collective-permute-start(bf16[4,256,128]{2,1,0:T(8,128)(2,1)S(1)} %get-tuple-element.33.refs_0_), channel_id=1, source_target_pairs={{0,2},{1,3},{2,0},{3,1},{4,6},{5,7},{6,4},{7,5},{8,10},{9,11},{10,... | collective-permute-start | bytes 786440 | tf_op jit(solution)/shard_map/ppermute | solution.py:810
  4.9 6.3 %collective-permute-done.1.refs_2_ = bf16[4,256,128]{2,1,0:T(8,128)(2,1)S(1)} collective-permute-done((bf16[4,256,128]{2,1,0:T(8,128)(2,1)S(1)}, bf16[4,256,128]{2,1,0:T(8,128)(2,1)S(1)}, u32[]{:S(2)}, u32[]{:S(2)}) %collective-permute-start.1) | collective-permute-done | bytes 262176 | tf_op jit(solution)/shard_map/ppermute | solution.py:810
  11.2 6.1 %all-to-all-start = ((s32[8,1,128]{2,1,0:T(1,128)}), s32[8,1,128]{2,1,0:T(1,128)S(1)}, u32[]{:S(2)}, u32[]{:S(2)}) async-start(s32[8,1,128]{2,1,0:T(1,128)} %bitcast.2), calls=%async_computation | async-start | bytes 8192 | tf_op jit(solution)/shard_map/all_to_all | solution.py:814
  17.3 3.1 %spread.1 = (bf16[4112,128]{1,0:T(8,128)(2,1)S(1)}, bf16[16,128,128]{2,1,0:T(8,128)(2,1)}, bf16[512,128]{1,0:T(8,128)(2,1)S(1)}) custom-call(s32[8,128]{1,0:T(8,128)S(1)} %get-tuple-element.31.origin, bf16[256,1,128,128]{3,2,1,0:T(8,128)(2,1)} %refs_9_.1, bf16[4,256,128]{2,1,0:T(8,128)(2,1)S(1)} %get-tuple-element.33.refs_0_, ...), custom_call_target="tpu_custom_call" | custom-call | tf_op jit(solution)/shard_map/spread/pallas_call | solution.py:185
  20.4 3.4 %all-to-all-done = s32[8,1,128]{2,1,0:T(1,128)S(1)} async-done(((s32[8,1,128]{2,1,0:T(1,128)}), s32[8,1,128]{2,1,0:T(1,128)S(1)}, u32[]{:S(2)}, u32[]{:S(2)}) %all-to-all-start) | async-done | bytes 4128 | tf_op jit(solution)/shard_map/all_to_all | solution.py:814
  25.1 3.4 %all-to-all-start.1 = ((bf16[8,96,128]{2,1,0:T(8,128)(2,1)}), bf16[8,96,128]{2,1,0:T(8,128)(2,1)S(1)}, u32[]{:S(2)}, u32[]{:S(2)}) async-start(bf16[8,96,128]{2,1,0:T(8,128)(2,1)} %bitcast.4), calls=%async_computation.1 | async-start | bytes 393216 | tf_op jit(solution)/shard_map/all_to_all | solution.py:814
  28.5 6.6 %operate_local.1.local = f32[4112,128]{1,0:T(8,128)S(1)} custom-call(s32[1,256]{1,0:T(1,128)S(1)} %get-tuple-element.29.pick, s32[1,256]{1,0:T(1,128)S(1)} %get-tuple-element.32.target, bf16[4112,128]{1,0:T(8,128)(2,1)S(1)} %get-tuple-element.34.field, f32[4,256,128]{2,1,0:T(8,128)} %state_in.1, bf16[256,1,128,128]{3,2,1,0:T(8,128)(2,1)} %refs_9_.1, ...), custom_call_target="tpu_custom_call" | custom-call | tf_op jit(solution)/shard_map/operate_local/pallas_call | solution.py:314
  36.2 2.6 %settle.1 = (f32[1024,128]{1,0:T(8,128)S(1)}, f32[1024,128]{1,0:T(8,128)S(1)}, f32[1024,128]{1,0:T(8,128)}, f32[1024,128]{1,0:T(8,128)}) custom-call(s32[8,128]{1,0:T(8,128)} %get-tuple-element.30.wanted, s32[8,128]{1,0:T(8,128)S(1)} %get-tuple-element.31.origin, s32[8,128]{1,0:T(8,128)S(1)} %bitcast.20, f32[4112,128]{1,0:T(8,128)S(1)} %operate_local.1.local, ...), custom_call_target="tpu_custom_call" | custom-call | tf_op jit(solution)/shard_map/settle/pallas_call | solution.py:355
  39.3 4.8 %all-to-all-start.3 = ((bf16[16,128,128]{2,1,0:T(8,128)(2,1)}), bf16[16,128,128]{2,1,0:T(8,128)(2,1)S(1)}, u32[]{:S(2)}, u32[]{:S(2)}) async-start(bf16[16,128,128]{2,1,0:T(8,128)(2,1)} %get-tuple-element.36.own.refs_8_), calls=%async_computation.3 | async-start | bytes 1048576 | tf_op jit(solution)/shard_map/all_to_all | solution.py:814
  46.5 1.6 %collective-permute-start.4 = (s16[1040,128]{1,0:T(8,128)(2,1)S(1)}, s16[1040,128]{1,0:T(8,128)(2,1)S(1)}, u32[]{:S(2)}, u32[]{:S(2)}) collective-permute-start(s16[1040,128]{1,0:T(8,128)(2,1)S(1)} %encode.4.refs_0_), channel_id=1, source_target_pairs={{0,2},{1,3},{2,0},{3,1},{4,6},{5,7},{6,4},{7,5},{8,10},{9,11},{10,... | collective-permute-start | bytes 798728 | tf_op jit(solution)/shard_map/ppermute | solution.py:810
  49.2 6.6 %collective-permute-done.4.refs_1_ = s16[1040,128]{1,0:T(8,128)(2,1)S(1)} collective-permute-done((s16[1040,128]{1,0:T(8,128)(2,1)S(1)}, s16[1040,128]{1,0:T(8,128)(2,1)S(1)}, u32[]{:S(2)}, u32[]{:S(2)}) %collective-permute-start.4) | collective-permute-done | bytes 266272 | tf_op jit(solution)/shard_map/ppermute | solution.py:810
  56.3 4.0 %collective-permute-done.6.refs_1_ = s16[1040,128]{1,0:T(8,128)(2,1)S(1)} collective-permute-done((s16[1040,128]{1,0:T(8,128)(2,1)S(1)}, s16[1040,128]{1,0:T(8,128)(2,1)S(1)}, u32[]{:S(2)}, u32[]{:S(2)}) %collective-permute-start.6) | collective-permute-done | bytes 266272 | tf_op jit(solution)/shard_map/ppermute | solution.py:810
  63.5 1.4 %pack.1 = s16[640,128]{1,0:T(8,128)(2,1)S(1)} custom-call(s32[8,128]{1,0:T(8,128)S(1)} %bitcast.21, s32[8,128]{1,0:T(8,128)S(1)} %get-tuple-element.31.origin, f32[1040,128]{1,0:T(8,128)S(1)} %decode.4.refs_2_.refs_0_, f32[1040,128]{1,0:T(8,128)S(1)} %decode.5.refs_1_.refs_2_, f32[1040,128]{1,0:T(8,128)S(1)} %collective-permute-done.7.refs_2_, ...), custom_call_target="tpu_custom_call" | custom-call | tf_op jit(solution)/shard_map/pack/pallas_call | solution.py:704
  64.9 13.3 %all_to_all.60 = s16[8,80,128]{2,1,0:T(8,128)(2,1)S(1)} all-to-all(s16[8,80,128]{2,1,0:T(8,128)(2,1)S(1)} %bitcast.16), channel_id=1, replica_groups=mesh['curve'=8,'band'=4] {'curve'}, dimensions={0} | all-to-all | bytes 327680 | tf_op jit(solution)/shard_map/all_to_all | solution.py:814
  78.2 6.5 %operate_second.1 = (f32[1024,128]{1,0:T(8,128)S(1)}, f32[1024,128]{1,0:T(8,128)S(1)}, f32[1024,128]{1,0:T(8,128)S(1)}, f32[1024,128]{1,0:T(8,128)S(1)}, f32[16,128]{1,0:T(8,128)S(1)}) custom-call(s32[1,256]{1,0:T(1,128)S(1)} %get-tuple-element.29.pick, s32[1,256]{1,0:T(1,128)S(1)} %get-tuple-element.32.target, s32[8,128]{1,0:T(8,128)S(1)} %bitcast.22, ...), custom_call_target="tpu_custom_call" | custom-call | tf_op jit(solution)/shard_map/operate_second/pallas_call | solution.py:426
  87.2 1.6 %collective-permute-start.10 = (s16[1040,128]{1,0:T(8,128)(2,1)S(1)}, s16[1040,128]{1,0:T(8,128)(2,1)S(1)}, u32[]{:S(2)}, u32[]{:S(2)}) collective-permute-start(s16[1040,128]{1,0:T(8,128)(2,1)S(1)} %encode.6.refs_0_), channel_id=1, source_target_pairs={{0,2},{1,3},{2,0},{3,1},{4,6},{5,7},{6,4},{7,5},{8,10},{9,11},{10,... | collective-permute-start | bytes 798728 | tf_op jit(solution)/shard_map/ppermute | solution.py:810
  89.9 6.6 %collective-permute-done.10.refs_1_ = s16[1040,128]{1,0:T(8,128)(2,1)S(1)} collective-permute-done((s16[1040,128]{1,0:T(8,128)(2,1)S(1)}, s16[1040,128]{1,0:T(8,128)(2,1)S(1)}, u32[]{:S(2)}, u32[]{:S(2)}) %collective-permute-start.10) | collective-permute-done | bytes 266272 | tf_op jit(solution)/shard_map/ppermute | solution.py:810
  97.0 4.4 %collective-permute-done.12.refs_1_ = s16[1040,128]{1,0:T(8,128)(2,1)S(1)} collective-permute-done((s16[1040,128]{1,0:T(8,128)(2,1)S(1)}, s16[1040,128]{1,0:T(8,128)(2,1)S(1)}, u32[]{:S(2)}, u32[]{:S(2)}) %collective-permute-start.12) | collective-permute-done | bytes 266272 | tf_op jit(solution)/shard_map/ppermute | solution.py:810
  104.7 2.2 %pack_rounded.1 = (bf16[256,128]{1,0:T(8,128)(2,1)}, f32[1056,128]{1,0:T(8,128)}, f32[1056,128]{1,0:T(8,128)}) custom-call(s32[8,128]{1,0:T(8,128)S(1)} %bitcast.23, f32[1056,128]{1,0:T(8,128)S(1)} %decode.6.refs_3_.refs_0_.refs_4_, f32[1056,128]{1,0:T(8,128)S(1)} %decode.7.refs_1_.refs_5_.image, f32[1056,128]{1,0:T(8,128)S(1)} %collective-permute-done.13.refs_2_, ...), custom_call_target="tpu_custom_call" | custom-call | tf_op jit(solution)/shard_map/pack_rounded/pallas_call | solution.py:737
  106.9 3.4 %all-to-all-start.4 = ((bf16[8,32,128]{2,1,0:T(8,128)(2,1)}), bf16[8,32,128]{2,1,0:T(8,128)(2,1)S(1)}, u32[]{:S(2)}, u32[]{:S(2)}) async-start(bf16[8,32,128]{2,1,0:T(8,128)(2,1)} %bitcast.8), calls=%async_computation.4 | async-start | bytes 131072 | tf_op jit(solution)/shard_map/all_to_all | solution.py:814
  110.3 6.8 %operate_third.1 = (f32[16,128]{1,0:T(8,128)S(1)}, f32[256,128]{1,0:T(8,128)S(1)}, f32[4,256,128]{2,1,0:T(8,128)}, f32[4,256,128]{2,1,0:T(8,128)}) custom-call(s32[1,256]{1,0:T(1,128)S(1)} %get-tuple-element.29.pick, s32[8,128]{1,0:T(8,128)} %get-tuple-element.30.wanted, s32[8,128]{1,0:T(8,128)S(1)} %get-tuple-element.31.origin, ...), custom_call_target="tpu_custom_call" | custom-call | tf_op jit(solution)/shard_map/operate_third/pallas_call | solution.py:507
  117.2 12.9 %all_to_all.61 = f32[32,1,128]{2,1,0:T(1,128)S(1)} all-to-all(f32[32,1,128]{2,1,0:T(1,128)S(1)} %bitcast.25), channel_id=1, replica_groups=mesh['curve'=8,'band'=4] {'curve','band'}, dimensions={0} | all-to-all | bytes 32768 | tf_op jit(solution)/shard_map/all_to_all | solution.py:862
  130.1 2.3 %finish.1 = f32[4,256,128]{2,1,0:T(8,128)} custom-call(f32[32,128]{1,0:T(8,128)S(1)} %bitcast.24, f32[16,128]{1,0:T(8,128)S(1)} %get-tuple-element.50.scale, f32[4,256,128]{2,1,0:T(8,128)} %state_in.1, f32[4,256,128]{2,1,0:T(8,128)} %get-tuple-element.51.drive_in, f32[4,256,128]{2,1,0:T(8,128)} %get-tuple-element.52.image_in), custom_call_target="tpu_custom_call" | custom-call | tf_op jit(solution)/shard_map/finish/pallas_call | solution.py:795
  (39 shorter events, 17.6 us)
Async XLA Ops:
  1.9 9.3 %collective-permute-start.1 = (bf16[4,256,128]{2,1,0:T(8,128)(2,1)S(1)}, bf16[4,256,128]{2,1,0:T(8,128)(2,1)S(1)}, u32[]{:S(2)}, u32[]{:S(2)}) collective-permute-start(bf16[4,256,128]{2,1,0:T(8,128)(2,1)S(1)} %get-tuple-element.33.refs_0_), channel_id=1, source_target_pairs={{0,2},{1,3},{2,0},{3,1},{4,6},{5,7},{6,4},{7,5},{8,10},{9,11},{10,... | collective-permute-start | bytes 786440 | tf_op jit(solution)/shard_map/ppermute | solution.py:810
  4.9 12.4 %collective-permute-start = (bf16[4,256,128]{2,1,0:T(8,128)(2,1)S(1)}, bf16[4,256,128]{2,1,0:T(8,128)(2,1)S(1)}, u32[]{:S(2)}, u32[]{:S(2)}) collective-permute-start(bf16[4,256,128]{2,1,0:T(8,128)(2,1)S(1)} %get-tuple-element.33.refs_0_), channel_id=1, source_target_pairs={{0,1},{1,0},{2,3},{3,2},{4,5},{5,4},{6,7},{7,6},{8,9},{9,8},{10,11... | collective-permute-start | bytes 786440 | tf_op jit(solution)/shard_map/ppermute | solution.py:810
  11.2 6.1 %collective-permute-start.2 = (bf16[4,256,128]{2,1,0:T(8,128)(2,1)S(1)}, bf16[4,256,128]{2,1,0:T(8,128)(2,1)S(1)}, u32[]{:S(2)}, u32[]{:S(2)}) collective-permute-start(bf16[4,256,128]{2,1,0:T(8,128)(2,1)S(1)} %collective-permute-done.1.refs_2_), channel_id=1, source_target_pairs={{0,1},{1,0},{2,3},{3,2},{4,5},{5,4},{6,7},{7,6},{8,9},{9,8},{10,11... | collective-permute-start | bytes 786440 | tf_op jit(solution)/shard_map/ppermute | solution.py:810
  11.2 12.6 %all-to-all-start = ((s32[8,1,128]{2,1,0:T(1,128)}), s32[8,1,128]{2,1,0:T(1,128)S(1)}, u32[]{:S(2)}, u32[]{:S(2)}) async-start(s32[8,1,128]{2,1,0:T(1,128)} %bitcast.2), calls=%async_computation | async-start | bytes 8192 | tf_op jit(solution)/shard_map/all_to_all | solution.py:814
  25.1 11.1 %all-to-all-start.1 = ((bf16[8,96,128]{2,1,0:T(8,128)(2,1)}), bf16[8,96,128]{2,1,0:T(8,128)(2,1)S(1)}, u32[]{:S(2)}, u32[]{:S(2)}) async-start(bf16[8,96,128]{2,1,0:T(8,128)(2,1)} %bitcast.4), calls=%async_computation.1 | async-start | bytes 393216 | tf_op jit(solution)/shard_map/all_to_all | solution.py:814
  38.8 5.3 %collective-permute-start.3 = (f32[1024,128]{1,0:T(8,128)}, f32[1024,128]{1,0:T(8,128)S(1)}, u32[]{:S(2)}, u32[]{:S(2)}) collective-permute-start(f32[1024,128]{1,0:T(8,128)} %get-tuple-element.38), channel_id=1, source_target_pairs={{0,1},{1,0},{2,3},{3,2},{4,5},{5,4},{6,7},{7,6},{8,9},{9,8},{10,11... | collective-permute-start | bytes 1572872 | tf_op jit(solution)/shard_map/ppermute | solution.py:810
  38.8 9.3 %collective-permute-start.5 = (f32[1024,128]{1,0:T(8,128)}, f32[1024,128]{1,0:T(8,128)S(1)}, u32[]{:S(2)}, u32[]{:S(2)}) collective-permute-start(f32[1024,128]{1,0:T(8,128)} %get-tuple-element.40), channel_id=1, source_target_pairs={{0,1},{1,0},{2,3},{3,2},{4,5},{5,4},{6,7},{7,6},{8,9},{9,8},{10,11... | collective-permute-start | bytes 1572872 | tf_op jit(solution)/shard_map/ppermute | solution.py:810
  39.3 25.6 %all-to-all-start.3 = ((bf16[16,128,128]{2,1,0:T(8,128)(2,1)}), bf16[16,128,128]{2,1,0:T(8,128)(2,1)S(1)}, u32[]{:S(2)}, u32[]{:S(2)}) async-start(bf16[16,128,128]{2,1,0:T(8,128)(2,1)} %get-tuple-element.36.own.refs_8_), calls=%async_computation.3 | async-start | bytes 1048576 | tf_op jit(solution)/shard_map/all_to_all | solution.py:814
  44.1 0.8 copy-start
  44.9 1.0 copy-start.1
  46.5 9.3 %collective-permute-start.4 = (s16[1040,128]{1,0:T(8,128)(2,1)S(1)}, s16[1040,128]{1,0:T(8,128)(2,1)S(1)}, u32[]{:S(2)}, u32[]{:S(2)}) collective-permute-start(s16[1040,128]{1,0:T(8,128)(2,1)S(1)} %encode.4.refs_0_), channel_id=1, source_target_pairs={{0,2},{1,3},{2,0},{3,1},{4,6},{5,7},{6,4},{7,5},{8,10},{9,11},{10,... | collective-permute-start | bytes 798728 | tf_op jit(solution)/shard_map/ppermute | solution.py:810
  48.6 11.7 %collective-permute-start.6 = (s16[1040,128]{1,0:T(8,128)(2,1)S(1)}, s16[1040,128]{1,0:T(8,128)(2,1)S(1)}, u32[]{:S(2)}, u32[]{:S(2)}) collective-permute-start(s16[1040,128]{1,0:T(8,128)(2,1)S(1)} %encode.5.refs_0_), channel_id=1, source_target_pairs={{0,2},{1,3},{2,0},{3,1},{4,6},{5,7},{6,4},{7,5},{8,10},{9,11},{10,... | collective-permute-start | bytes 798728 | tf_op jit(solution)/shard_map/ppermute | solution.py:810
  60.7 2.0 %collective-permute-start.8 = (f32[1040,128]{1,0:T(8,128)S(1)}, f32[1040,128]{1,0:T(8,128)S(1)}, u32[]{:S(2)}, u32[]{:S(2)}) collective-permute-start(f32[1040,128]{1,0:T(8,128)S(1)} %decode.5.refs_1_.refs_2_), channel_id=1, source_target_pairs={{0,1},{1,0},{2,3},{3,2},{4,5},{5,4},{6,7},{7,6},{8,9},{9,8},{10,11... | collective-permute-start | bytes 1597448 | tf_op jit(solution)/shard_map/ppermute | solution.py:810
  60.8 2.7 %collective-permute-start.7 = (f32[1040,128]{1,0:T(8,128)S(1)}, f32[1040,128]{1,0:T(8,128)S(1)}, u32[]{:S(2)}, u32[]{:S(2)}) collective-permute-start(f32[1040,128]{1,0:T(8,128)S(1)} %decode.4.refs_2_.refs_0_), channel_id=1, source_target_pairs={{0,1},{1,0},{2,3},{3,2},{4,5},{5,4},{6,7},{7,6},{8,9},{9,8},{10,11... | collective-permute-start | bytes 1597448 | tf_op jit(solution)/shard_map/ppermute | solution.py:810
  84.7 2.0 %collective-permute-start.9 = (f32[1024,128]{1,0:T(8,128)S(1)}, f32[1024,128]{1,0:T(8,128)S(1)}, u32[]{:S(2)}, u32[]{:S(2)}) collective-permute-start(f32[1024,128]{1,0:T(8,128)S(1)} %get-tuple-element.42), channel_id=1, source_target_pairs={{0,1},{1,0},{2,3},{3,2},{4,5},{5,4},{6,7},{7,6},{8,9},{9,8},{10,11... | collective-permute-start | bytes 1572872 | tf_op jit(solution)/shard_map/ppermute | solution.py:810
  84.8 4.0 %collective-permute-start.11 = (f32[1024,128]{1,0:T(8,128)S(1)}, f32[1024,128]{1,0:T(8,128)S(1)}, u32[]{:S(2)}, u32[]{:S(2)}) collective-permute-start(f32[1024,128]{1,0:T(8,128)S(1)} %get-tuple-element.44), channel_id=1, source_target_pairs={{0,1},{1,0},{2,3},{3,2},{4,5},{5,4},{6,7},{7,6},{8,9},{9,8},{10,11... | collective-permute-start | bytes 1572872 | tf_op jit(solution)/shard_map/ppermute | solution.py:810
  87.2 9.3 %collective-permute-start.10 = (s16[1040,128]{1,0:T(8,128)(2,1)S(1)}, s16[1040,128]{1,0:T(8,128)(2,1)S(1)}, u32[]{:S(2)}, u32[]{:S(2)}) collective-permute-start(s16[1040,128]{1,0:T(8,128)(2,1)S(1)} %encode.6.refs_0_), channel_id=1, source_target_pairs={{0,2},{1,3},{2,0},{3,1},{4,6},{5,7},{6,4},{7,5},{8,10},{9,11},{10,... | collective-permute-start | bytes 798728 | tf_op jit(solution)/shard_map/ppermute | solution.py:810
  89.3 12.1 %collective-permute-start.12 = (s16[1040,128]{1,0:T(8,128)(2,1)S(1)}, s16[1040,128]{1,0:T(8,128)(2,1)S(1)}, u32[]{:S(2)}, u32[]{:S(2)}) collective-permute-start(s16[1040,128]{1,0:T(8,128)(2,1)S(1)} %encode.7.refs_0_), channel_id=1, source_target_pairs={{0,2},{1,3},{2,0},{3,1},{4,6},{5,7},{6,4},{7,5},{8,10},{9,11},{10,... | collective-permute-start | bytes 798728 | tf_op jit(solution)/shard_map/ppermute | solution.py:810
  101.9 2.0 %collective-permute-start.14 = (f32[1056,128]{1,0:T(8,128)S(1)}, f32[1056,128]{1,0:T(8,128)S(1)}, u32[]{:S(2)}, u32[]{:S(2)}) collective-permute-start(f32[1056,128]{1,0:T(8,128)S(1)} %decode.7.refs_1_.refs_5_.image), channel_id=1, source_target_pairs={{0,1},{1,0},{2,3},{3,2},{4,5},{5,4},{6,7},{7,6},{8,9},{9,8},{10,11... | collective-permute-start | bytes 1622024 | tf_op jit(solution)/shard_map/ppermute | solution.py:810
  102.0 2.7 %collective-permute-start.13 = (f32[1056,128]{1,0:T(8,128)S(1)}, f32[1056,128]{1,0:T(8,128)S(1)}, u32[]{:S(2)}, u32[]{:S(2)}) collective-permute-start(f32[1056,128]{1,0:T(8,128)S(1)} %decode.6.refs_3_.refs_0_.refs_4_), channel_id=1, source_target_pairs={{0,1},{1,0},{2,3},{3,2},{4,5},{5,4},{6,7},{7,6},{8,9},{9,8},{10,11... | collective-permute-start | bytes 1622024 | tf_op jit(solution)/shard_map/ppermute | solution.py:810
  106.9 10.2 %all-to-all-start.4 = ((bf16[8,32,128]{2,1,0:T(8,128)(2,1)}), bf16[8,32,128]{2,1,0:T(8,128)(2,1)S(1)}, u32[]{:S(2)}, u32[]{:S(2)}) async-start(bf16[8,32,128]{2,1,0:T(8,128)(2,1)} %bitcast.8), calls=%async_computation.4 | async-start | bytes 131072 | tf_op jit(solution)/shard_map/all_to_all | solution.py:814

commit v8 on v7

--- a/solution.py
+++ b/solution.py
@@ -352,9 +352,11 @@
     node = local.shape[1]
     vectors = local.shape[0] // (rows + 1)
     groups = lax.axis_size("curve")
+    shapes = chunk_shapes(rows, vectors, node)
+    shapes[CHUNKS - 1] = pltpu.HBM(shapes[0].shape, f32)
     outs = pl.pallas_call(
         functools.partial(settle_kernel, rows, vectors, groups),
-        out_shape=chunk_shapes(rows, vectors, node),
+        out_shape=shapes,
         in_specs=[smem()] * 3 + [vmem()] * 3,
         out_specs=[vmem()] * (2 * CHUNKS),
         scratch_shapes=[pltpu.VMEM(local.shape, f32)],
@@ -441,10 +443,11 @@
 
 def third_kernel(rows, vectors, groups, width, pick, wanted, origin, *refs):
     count = 2 * CHUNKS
-    drive, image, (own, blocks, diag), refs = refs[:count], refs[count : 2 * count], refs[2 * count : 2 * count + 3], refs[2 * count + 3 :]
-    form, left, drive_own, image_own, field = refs[:5]
-    stream = Stream(blocks, diag, *refs[5:])
+    image, (own, blocks, diag), refs = refs[:count], refs[count : count + 3], refs[count + 3 :]
+    form, left, image_out, field, image_own, sem = refs[:6]
+    stream = Stream(blocks, diag, *refs[6:])
     stream.start()
+    leaving = pltpu.make_async_copy(image_own, image_out, sem)
     half = rows // 2
     each = half // CHUNKS
     shape = form.shape
@@ -463,8 +466,8 @@
             for v in range(width):
                 inside = pl.ds(pl.multiple_of(start + c * each, each), each)
                 source = pl.ds(band * width + v, each, stride=vectors)
-                drive_own[v, inside, :] = drive[side * CHUNKS + c][source, :]
                 image_own[v, inside, :] = array[source, :]
+    leaving.start()
     field[rows * vectors :, :] = jnp.zeros((vectors, shape[1]), bf16)
 
     def at(row):
@@ -498,21 +501,53 @@
         return carry
 
     lax.fori_loop(0, groups, remote, 0, unroll=8)
-
-
-def operate_third(pick, wanted, origin, drive, image, own, blocks, diag, width, vectors):
+    leaving.wait()
+
+
+def operate_third(pick, wanted, origin, image, own, blocks, diag, width, vectors):
     rows, node = blocks.shape[0], blocks.shape[-1]
     groups = lax.axis_size("curve")
     mine = pltpu.HBM((width, rows, node), f32)
     return pl.pallas_call(
         functools.partial(third_kernel, rows, vectors, groups, width),
-        out_shape=[shaped((vectors, node), f32), shaped((groups * CAP * vectors, node), f32), mine, mine],
-        in_specs=[smem()] * 3 + [vmem()] * (4 * CHUNKS + 1) + [anywhere()] * 2,
-        out_specs=[vmem()] * 4,
-        scratch_shapes=[pltpu.VMEM(((rows + 1) * vectors, node), bf16)] + stream_scratch(blocks, diag),
+        out_shape=[shaped((vectors, node), f32), shaped((groups * CAP * vectors, node), f32), mine],
+        in_specs=[smem()] * 3 + [vmem()] * (2 * CHUNKS + 1) + [anywhere()] * 2,
+        out_specs=[vmem()] * 2 + [anywhere()],
+        scratch_shapes=[
+            pltpu.VMEM(((rows + 1) * vectors, node), bf16),
+            pltpu.VMEM((width, rows, node), f32),
+            pltpu.SemaphoreType.DMA(()),
+        ]
+        + stream_scratch(blocks, diag),
         compiler_params=params(18),
         name="operate_third",
-    )(pick, wanted, origin, *drive, *image[:CHUNKS], *map(in_hbm, image[CHUNKS:]), own, blocks, diag)
+    )(pick, wanted, origin, *image[:CHUNKS], *map(in_hbm, image[CHUNKS:]), own, blocks, diag)
+
+
+def select_kernel(each, vectors, *refs):
+    arrays, out = refs[:-1], refs[-1]
+    width = out.shape[0]
+    band = lax.axis_index("band")
+    core = core_of(band)
+    for side in range(2):
+        start = jnp.where(core == side, 0, each * CHUNKS)
+        for c in range(CHUNKS):
+            inside = pl.ds(pl.multiple_of(start + c * each, each), each)
+            for v in range(width):
+                source = pl.ds(band * width + v, each, stride=vectors)
+                out[v, inside, :] = arrays[side * CHUNKS + c][source, :]
+
+
+def select_own(arrays, width, rows, vectors):
+    node = arrays[0].shape[1]
+    return pl.pallas_call(
+        functools.partial(select_kernel, rows // 2 // CHUNKS, vectors),
+        out_shape=pltpu.HBM((width, rows, node), f32),
+        in_specs=[vmem()] * (2 * CHUNKS),
+        out_specs=vmem(),
+        compiler_params=params(10),
+        name="select_own",
+    )(*arrays)
 
 
 def tail_kernel(each, vectors, form, left, halo, image, share):
@@ -851,12 +886,13 @@
     arrived = exchange(own)
     halo = exchange(pack(asked, origin, drive, vectors))
     keep, give, scale = operate_second(pick, target, asked, drive, halo, arrived, blocks, diag_blocks)
+    drive_own = select_own(drive, width, rows, vectors)
     image = band_sum(keep, give, vectors, drive)
     message, *left = pack_rounded(asked, image, vectors)
     halo = exchange(message)
     image = image[:CHUNKS] + left
-    form, left, drive_own, image_own = operate_third(
-        pick, wanted, origin, drive, image, own, blocks, diag_blocks, width, vectors
+    form, left, image_own = operate_third(
+        pick, wanted, origin, image, own, blocks, diag_blocks, width, vectors
     )
     share = tail(form, left, halo, image[CHUNKS - 1], devices)
     shares = lax.all_to_all(share, ("curve", "band"), split_axis=0, concat_axis=0, tiled=True)

time: 133 us -> 132 us (level)
  blocking collectives: 26.2 us -> 13.3 us
  waiting for transfers between devices: 38.3 us -> 44.4 us
  starting transfers between devices: 27.1 us -> 31.6 us
    all_to_all x1 -> x0, blocking collectives: 12.9 us -> none  [body(): lax.all_to_all(share, ('curve', 'band'), split_axis=0, concat_axis=0, til...]
    all_to_all x0 -> x1, waiting for transfers between devices: none -> 6.14 us  [body(): lax.all_to_all(share, ('curve', 'band'), split_axis=0, concat_axis=0, til...]
    all_to_all x0 -> x1, starting transfers between devices: none -> 5.3 us  [body(): lax.all_to_all(share, ('curve', 'band'), split_axis=0, concat_axis=0, til...]
  transfers between devices with their start and end apart: 19 -> 20, of which waited for: 12 -> 12; matrix products, arithmetic and copies ran while one was open for 0% -> 0% of each run, Pallas kernels for 16% -> 17%
where the time goes in v8:
time: 132 us; the launch traced here: 131 us
  waiting for transfers between devices  44.4 us (34%)
  Pallas kernels  39.8 us (30%)
  starting transfers between devices  31.6 us (24%)
  blocking collectives  13.3 us (10%)
  local copies, waits for them, and re-layouts  1.84 us (1%)
    ppermute x15, waiting for transfers between devices, swap(): return lax.ppermute(array, 'band', [(k, k ^ bit) for k in range(size)])  33.1 us
    all_to_all x4, starting transfers between devices, exchange(): lax.all_to_all(array, 'curve', split_axis=0, concat_axis=0, tiled=True)  17.6 us
    all_to_all x1, blocking collectives, exchange(): lax.all_to_all(array, 'curve', split_axis=0, concat_axis=0, tiled=True)  13.3 us
    ppermute x15, starting transfers between devices, swap(): return lax.ppermute(array, 'band', [(k, k ^ bit) for k in range(size)])  8.65 us
    pallas_call x1, Pallas kernels, operate_local(): pl.pallas_call(functools.partial(local_kernel, rows, vectors), out_shape=...  6.55 us
    pallas_call x1, Pallas kernels, operate_second(): pl.pallas_call(functools.partial(second_kernel, rows, vectors, groups), o...  6.52 us
    pallas_call x1, Pallas kernels, operate_third(): pl.pallas_call(functools.partial(third_kernel, rows, vectors, groups, wid...  6.19 us
    all_to_all x1, waiting for transfers between devices, body(): lax.all_to_all(share, ('curve', 'band'), split_axis=0, concat_axis=0, til...  6.14 us
  transfers between devices with their start and end apart: 20, of which 12 were waited for; matrix products, arithmetic and copies ran while one was open for 0% of the time, Pallas kernels for 17%

profile of v8, /device:TPU:0, one launch (start us, length us, event | category | flops | bytes accessed | tf_op | source)
XLA Modules:
  0.0 131.1 jit_solution(1143919746528664686)
XLA Ops:
  0.0 1.9 %plan.1 = (bf16[4,256,128]{2,1,0:T(8,128)(2,1)S(1)}, s32[1,256]{1,0:T(1,128)S(1)}, s32[1,256]{1,0:T(1,128)S(1)}, s32[8,128]{1,0:T(8,128)}, s32[8,128]{1,0:T(8,128)S(1)}) custom-call(s32[1,256]{1,0:T(1,128)} %bitcast.25, f32[4,256,128]{2,1,0:T(8,128)} %state_in.1), custom_call_target="tpu_custom_call" | custom-call | tf_op jit(solution)/shard_map/plan/pallas_call | solution.py:130
  1.9 3.0 %collective-permute-start.1 = (bf16[4,256,128]{2,1,0:T(8,128)(2,1)S(1)}, bf16[4,256,128]{2,1,0:T(8,128)(2,1)S(1)}, u32[]{:S(2)}, u32[]{:S(2)}) collective-permute-start(bf16[4,256,128]{2,1,0:T(8,128)(2,1)S(1)} %get-tuple-element.32.refs_0_), channel_id=1, source_target_pairs={{0,2},{1,3},{2,0},{3,1},{4,6},{5,7},{6,4},{7,5},{8,10},{9,11},{10,... | collective-permute-start | bytes 786440 | tf_op jit(solution)/shard_map/ppermute | solution.py:845
  4.9 6.3 %collective-permute-done.1.refs_2_ = bf16[4,256,128]{2,1,0:T(8,128)(2,1)S(1)} collective-permute-done((bf16[4,256,128]{2,1,0:T(8,128)(2,1)S(1)}, bf16[4,256,128]{2,1,0:T(8,128)(2,1)S(1)}, u32[]{:S(2)}, u32[]{:S(2)}) %collective-permute-start.1) | collective-permute-done | bytes 262176 | tf_op jit(solution)/shard_map/ppermute | solution.py:845
  11.2 6.1 %all-to-all-start = ((s32[8,1,128]{2,1,0:T(1,128)}), s32[8,1,128]{2,1,0:T(1,128)S(1)}, u32[]{:S(2)}, u32[]{:S(2)}) async-start(s32[8,1,128]{2,1,0:T(1,128)} %bitcast.2), calls=%async_computation | async-start | bytes 8192 | tf_op jit(solution)/shard_map/all_to_all | solution.py:849
  17.3 3.1 %spread.1 = (bf16[4112,128]{1,0:T(8,128)(2,1)S(1)}, bf16[16,128,128]{2,1,0:T(8,128)(2,1)}, bf16[512,128]{1,0:T(8,128)(2,1)S(1)}) custom-call(s32[8,128]{1,0:T(8,128)S(1)} %get-tuple-element.30.origin, bf16[256,1,128,128]{3,2,1,0:T(8,128)(2,1)} %refs_5_.1, bf16[4,256,128]{2,1,0:T(8,128)(2,1)S(1)} %get-tuple-element.32.refs_0_, ...), custom_call_target="tpu_custom_call" | custom-call | tf_op jit(solution)/shard_map/spread/pallas_call | solution.py:185
  20.4 3.4 %all-to-all-done = s32[8,1,128]{2,1,0:T(1,128)S(1)} async-done(((s32[8,1,128]{2,1,0:T(1,128)}), s32[8,1,128]{2,1,0:T(1,128)S(1)}, u32[]{:S(2)}, u32[]{:S(2)}) %all-to-all-start) | async-done | bytes 4128 | tf_op jit(solution)/shard_map/all_to_all | solution.py:849
  25.1 3.4 %all-to-all-start.1 = ((bf16[8,96,128]{2,1,0:T(8,128)(2,1)}), bf16[8,96,128]{2,1,0:T(8,128)(2,1)S(1)}, u32[]{:S(2)}, u32[]{:S(2)}) async-start(bf16[8,96,128]{2,1,0:T(8,128)(2,1)} %bitcast.4), calls=%async_computation.1 | async-start | bytes 393216 | tf_op jit(solution)/shard_map/all_to_all | solution.py:849
  28.5 6.6 %operate_local.1.local = f32[4112,128]{1,0:T(8,128)S(1)} custom-call(s32[1,256]{1,0:T(1,128)S(1)} %get-tuple-element.28.pick, s32[1,256]{1,0:T(1,128)S(1)} %get-tuple-element.31.target, bf16[4112,128]{1,0:T(8,128)(2,1)S(1)} %get-tuple-element.33.field, f32[4,256,128]{2,1,0:T(8,128)} %state_in.1, bf16[256,1,128,128]{3,2,1,0:T(8,128)(2,1)} %refs_5_.1, ...), custom_call_target="tpu_custom_call" | custom-call | tf_op jit(solution)/shard_map/operate_local/pallas_call | solution.py:314
  36.2 2.6 %settle.1 = (f32[1024,128]{1,0:T(8,128)S(1)}, f32[1024,128]{1,0:T(8,128)}, f32[1024,128]{1,0:T(8,128)}, f32[1024,128]{1,0:T(8,128)}) custom-call(s32[8,128]{1,0:T(8,128)} %get-tuple-element.29.wanted, s32[8,128]{1,0:T(8,128)S(1)} %get-tuple-element.30.origin, s32[8,128]{1,0:T(8,128)S(1)} %bitcast.20, f32[4112,128]{1,0:T(8,128)S(1)} %operate_local.1.local, ...), custom_call_target="tpu_custom_call" | custom-call | tf_op jit(solution)/shard_map/settle/pallas_call | solution.py:357
  39.4 4.8 %all-to-all-start.3 = ((bf16[16,128,128]{2,1,0:T(8,128)(2,1)}), bf16[16,128,128]{2,1,0:T(8,128)(2,1)S(1)}, u32[]{:S(2)}, u32[]{:S(2)}) async-start(bf16[16,128,128]{2,1,0:T(8,128)(2,1)} %get-tuple-element.35.own.refs_4_), calls=%async_computation.3 | async-start | bytes 1048576 | tf_op jit(solution)/shard_map/all_to_all | solution.py:849
  49.2 6.6 %collective-permute-done.4.refs_1_ = s16[1040,128]{1,0:T(8,128)(2,1)S(1)} collective-permute-done((s16[1040,128]{1,0:T(8,128)(2,1)S(1)}, s16[1040,128]{1,0:T(8,128)(2,1)S(1)}, u32[]{:S(2)}, u32[]{:S(2)}) %collective-permute-start.4) | collective-permute-done | bytes 266272 | tf_op jit(solution)/shard_map/ppermute | solution.py:845
  56.4 4.0 %collective-permute-done.6.refs_1_ = s16[1040,128]{1,0:T(8,128)(2,1)S(1)} collective-permute-done((s16[1040,128]{1,0:T(8,128)(2,1)S(1)}, s16[1040,128]{1,0:T(8,128)(2,1)S(1)}, u32[]{:S(2)}, u32[]{:S(2)}) %collective-permute-start.6) | collective-permute-done | bytes 266272 | tf_op jit(solution)/shard_map/ppermute | solution.py:845
  60.9 1.9 %collective-permute-done.8.refs_3_ = f32[1040,128]{1,0:T(8,128)S(1)} collective-permute-done((f32[1040,128]{1,0:T(8,128)S(1)}, f32[1040,128]{1,0:T(8,128)S(1)}, u32[]{:S(2)}, u32[]{:S(2)}) %collective-permute-start.8) | collective-permute-done | bytes 532512 | tf_op jit(solution)/shard_map/ppermute | solution.py:845
  64.2 13.3 %all_to_all.60 = s16[8,80,128]{2,1,0:T(8,128)(2,1)S(1)} all-to-all(s16[8,80,128]{2,1,0:T(8,128)(2,1)S(1)} %bitcast.16), channel_id=1, replica_groups=mesh['curve'=8,'band'=4] {'curve'}, dimensions={0} | all-to-all | bytes 327680 | tf_op jit(solution)/shard_map/all_to_all | solution.py:849
  77.5 6.5 %operate_second.1 = (f32[1024,128]{1,0:T(8,128)S(1)}, f32[1024,128]{1,0:T(8,128)S(1)}, f32[1024,128]{1,0:T(8,128)S(1)}, f32[1024,128]{1,0:T(8,128)S(1)}, f32[16,128]{1,0:T(8,128)S(1)}) custom-call(s32[1,256]{1,0:T(1,128)S(1)} %get-tuple-element.28.pick, s32[1,256]{1,0:T(1,128)S(1)} %get-tuple-element.31.target, s32[8,128]{1,0:T(8,128)S(1)} %bitcast.22, ...), custom_call_target="tpu_custom_call" | custom-call | tf_op jit(solution)/shard_map/operate_second/pallas_call | solution.py:428
  89.3 6.6 %collective-permute-done.10.refs_1_ = s16[1040,128]{1,0:T(8,128)(2,1)S(1)} collective-permute-done((s16[1040,128]{1,0:T(8,128)(2,1)S(1)}, s16[1040,128]{1,0:T(8,128)(2,1)S(1)}, u32[]{:S(2)}, u32[]{:S(2)}) %collective-permute-start.10) | collective-permute-done | bytes 266272 | tf_op jit(solution)/shard_map/ppermute | solution.py:845
  96.4 4.3 %collective-permute-done.12.refs_1_ = s16[1040,128]{1,0:T(8,128)(2,1)S(1)} collective-permute-done((s16[1040,128]{1,0:T(8,128)(2,1)S(1)}, s16[1040,128]{1,0:T(8,128)(2,1)S(1)}, u32[]{:S(2)}, u32[]{:S(2)}) %collective-permute-start.12) | collective-permute-done | bytes 266272 | tf_op jit(solution)/shard_map/ppermute | solution.py:845
  101.3 1.9 %collective-permute-done.14.refs_3_ = f32[1056,128]{1,0:T(8,128)S(1)} collective-permute-done((f32[1056,128]{1,0:T(8,128)S(1)}, f32[1056,128]{1,0:T(8,128)S(1)}, u32[]{:S(2)}, u32[]{:S(2)}) %collective-permute-start.14) | collective-permute-done | bytes 540704 | tf_op jit(solution)/shard_map/ppermute | solution.py:845
  103.2 2.2 %pack_rounded.1 = (bf16[256,128]{1,0:T(8,128)(2,1)}, f32[1056,128]{1,0:T(8,128)}, f32[1056,128]{1,0:T(8,128)}) custom-call(s32[8,128]{1,0:T(8,128)S(1)} %bitcast.23, f32[1056,128]{1,0:T(8,128)S(1)} %decode.6.refs_3_.refs_0_, f32[1056,128]{1,0:T(8,128)S(1)} %decode.7.refs_1_.image, f32[1056,128]{1,0:T(8,128)S(1)} %collective-permute-done.13.refs_2_, ...), custom_call_target="tpu_custom_call" | custom-call | tf_op jit(solution)/shard_map/pack_rounded/pallas_call | solution.py:772
  105.5 3.4 %all-to-all-start.4 = ((bf16[8,32,128]{2,1,0:T(8,128)(2,1)}), bf16[8,32,128]{2,1,0:T(8,128)(2,1)S(1)}, u32[]{:S(2)}, u32[]{:S(2)}) async-start(bf16[8,32,128]{2,1,0:T(8,128)(2,1)} %bitcast.8), calls=%async_computation.4 | async-start | bytes 131072 | tf_op jit(solution)/shard_map/all_to_all | solution.py:849
  108.8 6.2 %operate_third.1 = (f32[16,128]{1,0:T(8,128)S(1)}, f32[256,128]{1,0:T(8,128)S(1)}, f32[4,256,128]{2,1,0:T(8,128)}) custom-call(s32[1,256]{1,0:T(1,128)S(1)} %get-tuple-element.28.pick, s32[8,128]{1,0:T(8,128)} %get-tuple-element.29.wanted, s32[8,128]{1,0:T(8,128)S(1)} %get-tuple-element.30.origin, f32[1056,128]{1,0:T(8,128)S(1)} %decode.6.refs_3_.refs_0_, ...), custom_call_target="tpu_custom_call" | custom-call | tf_op jit(solution)/shard_map/operate_third/pallas_call | solution.py:511
  116.4 5.3 %all-to-all-start.5 = ((f32[32,1,128]{2,1,0:T(1,128)}), f32[32,1,128]{2,1,0:T(1,128)S(1)}, u32[]{:S(2)}, u32[]{:S(2)}) async-start(f32[32,1,128]{2,1,0:T(1,128)} %bitcast.11), calls=%async_computation.5 | async-start | bytes 32768 | tf_op jit(solution)/shard_map/all_to_all | solution.py:898
  122.7 6.1 %all-to-all-done.5 = f32[32,1,128]{2,1,0:T(1,128)S(1)} async-done(((f32[32,1,128]{2,1,0:T(1,128)}), f32[32,1,128]{2,1,0:T(1,128)S(1)}, u32[]{:S(2)}, u32[]{:S(2)}) %all-to-all-start.5) | async-done | bytes 16416 | tf_op jit(solution)/shard_map/all_to_all | solution.py:898
  128.8 2.3 %finish.1 = f32[4,256,128]{2,1,0:T(8,128)} custom-call(f32[32,128]{1,0:T(8,128)S(1)} %bitcast.24, f32[16,128]{1,0:T(8,128)S(1)} %get-tuple-element.49.scale, f32[4,256,128]{2,1,0:T(8,128)} %state_in.1, f32[4,256,128]{2,1,0:T(8,128)} %select_own.1.drive_in, f32[4,256,128]{2,1,0:T(8,128)} %get-tuple-element.50.image_in), custom_call_target="tpu_custom_call" | custom-call | tf_op jit(solution)/shard_map/finish/pallas_call | solution.py:830
  (43 shorter events, 19.1 us)
Async XLA Ops:
  1.9 9.3 %collective-permute-start.1 = (bf16[4,256,128]{2,1,0:T(8,128)(2,1)S(1)}, bf16[4,256,128]{2,1,0:T(8,128)(2,1)S(1)}, u32[]{:S(2)}, u32[]{:S(2)}) collective-permute-start(bf16[4,256,128]{2,1,0:T(8,128)(2,1)S(1)} %get-tuple-element.32.refs_0_), channel_id=1, source_target_pairs={{0,2},{1,3},{2,0},{3,1},{4,6},{5,7},{6,4},{7,5},{8,10},{9,11},{10,... | collective-permute-start | bytes 786440 | tf_op jit(solution)/shard_map/ppermute | solution.py:845
  4.9 12.4 %collective-permute-start = (bf16[4,256,128]{2,1,0:T(8,128)(2,1)S(1)}, bf16[4,256,128]{2,1,0:T(8,128)(2,1)S(1)}, u32[]{:S(2)}, u32[]{:S(2)}) collective-permute-start(bf16[4,256,128]{2,1,0:T(8,128)(2,1)S(1)} %get-tuple-element.32.refs_0_), channel_id=1, source_target_pairs={{0,1},{1,0},{2,3},{3,2},{4,5},{5,4},{6,7},{7,6},{8,9},{9,8},{10,11... | collective-permute-start | bytes 786440 | tf_op jit(solution)/shard_map/ppermute | solution.py:845
  11.2 6.1 %collective-permute-start.2 = (bf16[4,256,128]{2,1,0:T(8,128)(2,1)S(1)}, bf16[4,256,128]{2,1,0:T(8,128)(2,1)S(1)}, u32[]{:S(2)}, u32[]{:S(2)}) collective-permute-start(bf16[4,256,128]{2,1,0:T(8,128)(2,1)S(1)} %collective-permute-done.1.refs_2_), channel_id=1, source_target_pairs={{0,1},{1,0},{2,3},{3,2},{4,5},{5,4},{6,7},{7,6},{8,9},{9,8},{10,11... | collective-permute-start | bytes 786440 | tf_op jit(solution)/shard_map/ppermute | solution.py:845
  11.2 12.6 %all-to-all-start = ((s32[8,1,128]{2,1,0:T(1,128)}), s32[8,1,128]{2,1,0:T(1,128)S(1)}, u32[]{:S(2)}, u32[]{:S(2)}) async-start(s32[8,1,128]{2,1,0:T(1,128)} %bitcast.2), calls=%async_computation | async-start | bytes 8192 | tf_op jit(solution)/shard_map/all_to_all | solution.py:849
  25.1 11.1 %all-to-all-start.1 = ((bf16[8,96,128]{2,1,0:T(8,128)(2,1)}), bf16[8,96,128]{2,1,0:T(8,128)(2,1)S(1)}, u32[]{:S(2)}, u32[]{:S(2)}) async-start(bf16[8,96,128]{2,1,0:T(8,128)(2,1)} %bitcast.4), calls=%async_computation.1 | async-start | bytes 393216 | tf_op jit(solution)/shard_map/all_to_all | solution.py:849
  38.8 9.3 %copy-start = (f32[1024,128]{1,0:T(8,128)S(1)}, f32[1024,128]{1,0:T(8,128)}, u32[]{:S(2)}) copy-start(f32[1024,128]{1,0:T(8,128)} %get-tuple-element.38.keep) | copy-start | bytes 1572868
  38.8 5.3 %collective-permute-start.3 = (f32[1024,128]{1,0:T(8,128)}, f32[1024,128]{1,0:T(8,128)S(1)}, u32[]{:S(2)}, u32[]{:S(2)}) collective-permute-start(f32[1024,128]{1,0:T(8,128)} %get-tuple-element.37), channel_id=1, source_target_pairs={{0,1},{1,0},{2,3},{3,2},{4,5},{5,4},{6,7},{7,6},{8,9},{9,8},{10,11... | collective-permute-start | bytes 1572872 | tf_op jit(solution)/shard_map/ppermute | solution.py:845
  38.8 9.3 %collective-permute-start.5 = (f32[1024,128]{1,0:T(8,128)}, f32[1024,128]{1,0:T(8,128)S(1)}, u32[]{:S(2)}, u32[]{:S(2)}) collective-permute-start(f32[1024,128]{1,0:T(8,128)} %get-tuple-element.39), channel_id=1, source_target_pairs={{0,1},{1,0},{2,3},{3,2},{4,5},{5,4},{6,7},{7,6},{8,9},{9,8},{10,11... | collective-permute-start | bytes 1572872 | tf_op jit(solution)/shard_map/ppermute | solution.py:845
  39.4 24.9 %all-to-all-start.3 = ((bf16[16,128,128]{2,1,0:T(8,128)(2,1)}), bf16[16,128,128]{2,1,0:T(8,128)(2,1)S(1)}, u32[]{:S(2)}, u32[]{:S(2)}) async-start(bf16[16,128,128]{2,1,0:T(8,128)(2,1)} %get-tuple-element.35.own.refs_4_), calls=%async_computation.3 | async-start | bytes 1048576 | tf_op jit(solution)/shard_map/all_to_all | solution.py:849
  44.1 0.8 copy-start.1
  44.9 1.0 copy-start.2
  46.5 9.3 %collective-permute-start.4 = (s16[1040,128]{1,0:T(8,128)(2,1)S(1)}, s16[1040,128]{1,0:T(8,128)(2,1)S(1)}, u32[]{:S(2)}, u32[]{:S(2)}) collective-permute-start(s16[1040,128]{1,0:T(8,128)(2,1)S(1)} %encode.4.refs_0_), channel_id=1, source_target_pairs={{0,2},{1,3},{2,0},{3,1},{4,6},{5,7},{6,4},{7,5},{8,10},{9,11},{10,... | collective-permute-start | bytes 798728 | tf_op jit(solution)/shard_map/ppermute | solution.py:845
  48.6 11.7 %collective-permute-start.6 = (s16[1040,128]{1,0:T(8,128)(2,1)S(1)}, s16[1040,128]{1,0:T(8,128)(2,1)S(1)}, u32[]{:S(2)}, u32[]{:S(2)}) collective-permute-start(s16[1040,128]{1,0:T(8,128)(2,1)S(1)} %encode.5.refs_0_), channel_id=1, source_target_pairs={{0,2},{1,3},{2,0},{3,1},{4,6},{5,7},{6,4},{7,5},{8,10},{9,11},{10,... | collective-permute-start | bytes 798728 | tf_op jit(solution)/shard_map/ppermute | solution.py:845
  56.3 4.6 %collective-permute-start.7 = (f32[1040,128]{1,0:T(8,128)S(1)}, f32[1040,128]{1,0:T(8,128)S(1)}, u32[]{:S(2)}, u32[]{:S(2)}) collective-permute-start(f32[1040,128]{1,0:T(8,128)S(1)} %decode.4.refs_2_.refs_0_), channel_id=1, source_target_pairs={{0,1},{1,0},{2,3},{3,2},{4,5},{5,4},{6,7},{7,6},{8,9},{9,8},{10,11... | collective-permute-start | bytes 1597448 | tf_op jit(solution)/shard_map/ppermute | solution.py:845
  60.8 2.0 %collective-permute-start.8 = (f32[1040,128]{1,0:T(8,128)S(1)}, f32[1040,128]{1,0:T(8,128)S(1)}, u32[]{:S(2)}, u32[]{:S(2)}) collective-permute-start(f32[1040,128]{1,0:T(8,128)S(1)} %decode.5.refs_1_.refs_2_), channel_id=1, source_target_pairs={{0,1},{1,0},{2,3},{3,2},{4,5},{5,4},{6,7},{7,6},{8,9},{9,8},{10,11... | collective-permute-start | bytes 1597448 | tf_op jit(solution)/shard_map/ppermute | solution.py:845
  84.1 2.0 %collective-permute-start.9 = (f32[1024,128]{1,0:T(8,128)S(1)}, f32[1024,128]{1,0:T(8,128)S(1)}, u32[]{:S(2)}, u32[]{:S(2)}) collective-permute-start(f32[1024,128]{1,0:T(8,128)S(1)} %get-tuple-element.41), channel_id=1, source_target_pairs={{0,1},{1,0},{2,3},{3,2},{4,5},{5,4},{6,7},{7,6},{8,9},{9,8},{10,11... | collective-permute-start | bytes 1572872 | tf_op jit(solution)/shard_map/ppermute | solution.py:845
  84.1 4.0 %collective-permute-start.11 = (f32[1024,128]{1,0:T(8,128)S(1)}, f32[1024,128]{1,0:T(8,128)S(1)}, u32[]{:S(2)}, u32[]{:S(2)}) collective-permute-start(f32[1024,128]{1,0:T(8,128)S(1)} %get-tuple-element.43), channel_id=1, source_target_pairs={{0,1},{1,0},{2,3},{3,2},{4,5},{5,4},{6,7},{7,6},{8,9},{9,8},{10,11... | collective-permute-start | bytes 1572872 | tf_op jit(solution)/shard_map/ppermute | solution.py:845
  86.6 9.3 %collective-permute-start.10 = (s16[1040,128]{1,0:T(8,128)(2,1)S(1)}, s16[1040,128]{1,0:T(8,128)(2,1)S(1)}, u32[]{:S(2)}, u32[]{:S(2)}) collective-permute-start(s16[1040,128]{1,0:T(8,128)(2,1)S(1)} %encode.6.refs_0_), channel_id=1, source_target_pairs={{0,2},{1,3},{2,0},{3,1},{4,6},{5,7},{6,4},{7,5},{8,10},{9,11},{10,... | collective-permute-start | bytes 798728 | tf_op jit(solution)/shard_map/ppermute | solution.py:845
  88.7 12.1 %collective-permute-start.12 = (s16[1040,128]{1,0:T(8,128)(2,1)S(1)}, s16[1040,128]{1,0:T(8,128)(2,1)S(1)}, u32[]{:S(2)}, u32[]{:S(2)}) collective-permute-start(s16[1040,128]{1,0:T(8,128)(2,1)S(1)} %encode.7.refs_0_), channel_id=1, source_target_pairs={{0,2},{1,3},{2,0},{3,1},{4,6},{5,7},{6,4},{7,5},{8,10},{9,11},{10,... | collective-permute-start | bytes 798728 | tf_op jit(solution)/shard_map/ppermute | solution.py:845
  96.4 5.0 %collective-permute-start.13 = (f32[1056,128]{1,0:T(8,128)S(1)}, f32[1056,128]{1,0:T(8,128)S(1)}, u32[]{:S(2)}, u32[]{:S(2)}) collective-permute-start(f32[1056,128]{1,0:T(8,128)S(1)} %decode.6.refs_3_.refs_0_), channel_id=1, source_target_pairs={{0,1},{1,0},{2,3},{3,2},{4,5},{5,4},{6,7},{7,6},{8,9},{9,8},{10,11... | collective-permute-start | bytes 1622024 | tf_op jit(solution)/shard_map/ppermute | solution.py:845
  101.2 2.0 %collective-permute-start.14 = (f32[1056,128]{1,0:T(8,128)S(1)}, f32[1056,128]{1,0:T(8,128)S(1)}, u32[]{:S(2)}, u32[]{:S(2)}) collective-permute-start(f32[1056,128]{1,0:T(8,128)S(1)} %decode.7.refs_1_.image), channel_id=1, source_target_pairs={{0,1},{1,0},{2,3},{3,2},{4,5},{5,4},{6,7},{7,6},{8,9},{9,8},{10,11... | collective-permute-start | bytes 1622024 | tf_op jit(solution)/shard_map/ppermute | solution.py:845
  105.5 10.2 %all-to-all-start.4 = ((bf16[8,32,128]{2,1,0:T(8,128)(2,1)}), bf16[8,32,128]{2,1,0:T(8,128)(2,1)S(1)}, u32[]{:S(2)}, u32[]{:S(2)}) async-start(bf16[8,32,128]{2,1,0:T(8,128)(2,1)} %bitcast.8), calls=%async_computation.4 | async-start | bytes 131072 | tf_op jit(solution)/shard_map/all_to_all | solution.py:849
  116.4 12.4 %all-to-all-start.5 = ((f32[32,1,128]{2,1,0:T(1,128)}), f32[32,1,128]{2,1,0:T(1,128)S(1)}, u32[]{:S(2)}, u32[]{:S(2)}) async-start(f32[32,1,128]{2,1,0:T(1,128)} %bitcast.11), calls=%async_computation.5 | async-start | bytes 32768 | tf_op jit(solution)/shard_map/all_to_all | solution.py:898
